TPU v7x, 32 devices: a whole 2x2x4 slice. The times are simulated.
32 devices in a mesh: dp: 16 (over z, x, core), tensor: 2 (over y).
Axes of the slice: x: 2, y: 2, z: 4, core: 2. Of those that a mesh axis runs over, the one named last changes fastest.
Arguments:
- tokens: bfloat16 [2048, 768], P('dp'), may hold values from -6 to 6
- seg_ids: int32 [2048], P('dp'), may hold values from -1 to 6, as said below
- query_weight: bfloat16 [768, 768], P(None, 'tensor'), may hold values from -0.21875 to 0.21875
- key_weight: bfloat16 [768, 768], P(None, 'tensor'), may hold values from -0.21875 to 0.21875
- value_weight: bfloat16 [768, 768], P(None, 'tensor'), may hold values from -0.21875 to 0.21875
- query_bias: float32 [768], P('tensor'), may hold values from -3 to 3
- value_bias: float32 [768], P('tensor'), may hold values from -3 to 3
- out_weight: bfloat16 [768, 768], P(None, 'tensor'), may hold values from -1.75 to 1.75
- out_bias: float32 [768], replicated, may hold values from -3 to 3
- attention_norm_gain: float32 [768], replicated, may hold values from 0.25 to 1.75
- attention_norm_shift: float32 [768], replicated, may hold values from -3 to 3
- up_weight: bfloat16 [768, 3072], P(None, 'tensor'), may hold values from -0.21875 to 0.21875
- up_bias: float32 [3072], P('tensor'), may hold values from -3 to 3
- down_weight: bfloat16 [768, 3072], P(None, 'tensor'), may hold values from -0.109375 to 0.109375
- down_bias: float32 [768], replicated, may hold values from -3 to 3
- feedforward_norm_gain: float32 [768], replicated, may hold values from 0.25 to 1.75
- feedforward_norm_shift: float32 [768], replicated, may hold values from -3 to 3
- cotangent: bfloat16 [2048, 768], P('dp'), may hold values from -6 to 6
Outputs:
- mixed: bfloat16 [2048, 768], P('dp')
- grad_tokens: float32 [2048, 768], P('dp')
- grad_query_weight: float32 [768, 768], P('dp', 'tensor')
- grad_key_weight: float32 [768, 768], P('dp', 'tensor')
- grad_value_weight: float32 [768, 768], P('dp', 'tensor')
- grad_query_bias: float32 [768], P('tensor')
- grad_value_bias: float32 [768], P('tensor')
- grad_out_weight: float32 [768, 768], P('dp', 'tensor')
- grad_out_bias: float32 [768], replicated
- grad_gain_first: float32 [768], replicated
- grad_shift_first: float32 [768], replicated
- grad_up_weight: float32 [768, 3072], P('dp', 'tensor')
- grad_up_bias: float32 [3072], P('tensor')
- grad_down_weight: float32 [768, 3072], P('dp', 'tensor')
- grad_down_bias: float32 [768], replicated
- grad_gain_second: float32 [768], replicated
- grad_shift_second: float32 [768], replicated
Inputs may be any that keep to these rules, and one draw needn't show every extreme that they name: `seg_ids`: within each device's block of 128 tokens the ids are 0, 1, 2, ... in order, one for each packed sequence of 16 to 127 tokens, and -1 marks the padding from the last sequence's end to the block's end; the block's last token is always padding. Some block holds the most sequences that fit, and some block one sequence of 127 tokens.
All inputs are finite; a program needn't handle non-finite values.
Results may differ from a plain program's by a relative error of at most 0.013.
Values sent between devices are 32-bit elements; how exact they have to be, the bound alone decides.
A program may use at most 128 MiB of HBM per device.

v0:
```python
import math

import jax
import jax.numpy as jnp
from jax import lax
from jax.sharding import PartitionSpec as P

HEAD_DIM = 64


epsilon = 1e-12
masked_value = -1e30


def dot_rows(left, right):
    return lax.dot_general(
        left, right, (((1,), (1,)), ((), ())), preferred_element_type=jnp.float32
    )


def dot_cols(left, right):
    return lax.dot_general(
        left, right, (((0,), (0,)), ((), ())), preferred_element_type=jnp.float32
    )


def apply_layer_norm(rows):
    row_mean = jnp.mean(rows, axis=1, keepdims=True)
    centred = rows - row_mean
    inverse_deviation = lax.rsqrt(jnp.mean(centred * centred, axis=1, keepdims=True) + epsilon)
    return (centred * inverse_deviation, inverse_deviation)


def norm_backward_pass(incoming_gradient, centered_rows, inverse_deviation, norm_gain):
    scaled_rows = incoming_gradient * norm_gain
    row_gradient = inverse_deviation * (
        scaled_rows
        - jnp.mean(scaled_rows, axis=1, keepdims=True)
        - centered_rows * jnp.mean(scaled_rows * centered_rows, axis=1, keepdims=True)
    )
    return (
        row_gradient,
        jnp.sum(incoming_gradient * centered_rows, axis=0),
        jnp.sum(incoming_gradient, axis=0),
    )


def attend_forward(queries, key_rows, value_rows, seg_ids, head_count, head_width):
    key_count = key_rows.shape[0]
    block_rows = min(512, key_count)
    block_count = key_count // block_rows
    key_heads = key_rows.reshape(key_count, head_count, head_width)
    value_heads = value_rows.reshape(key_count, head_count, head_width)
    score_scale = 1.0 / math.sqrt(head_width)

    def one_block(block_item):
        query_block, block_ids = block_item
        query_heads = query_block.reshape(block_rows, head_count, head_width)
        scores = (
            jnp.einsum("qhe,khe->hqk", query_heads, key_heads, preferred_element_type=jnp.float32)
            * score_scale
        )
        allowed = (block_ids[:, None] == seg_ids[None, :])[None]
        scores = jnp.where(allowed, scores, masked_value)
        row_max = jnp.max(scores, axis=2, keepdims=True)
        weights_exp = jnp.exp(scores - row_max)
        mass = jnp.sum(weights_exp, axis=2, keepdims=True)
        probabilities = (weights_exp / mass).astype(jnp.bfloat16)
        context = jnp.einsum(
            "hqk,khe->qhe", probabilities, value_heads, preferred_element_type=jnp.float32
        )
        return (
            context.reshape(block_rows, head_count * head_width).astype(jnp.bfloat16),
            (row_max + jnp.log(mass))[:, :, 0],
        )

    contexts, log_mass = lax.map(
        one_block,
        (
            queries.reshape(block_count, block_rows, head_count * head_width),
            seg_ids.reshape(block_count, block_rows),
        ),
    )
    return (contexts.reshape(key_count, head_count * head_width), log_mass)


def attend_backward(
    queries, key_rows, value_rows, seg_ids, log_mass, grad_context, head_count, head_width
):
    key_count = key_rows.shape[0]
    block_rows = min(512, key_count)
    block_count = key_count // block_rows
    key_heads = key_rows.reshape(key_count, head_count, head_width)
    value_heads = value_rows.reshape(key_count, head_count, head_width)
    score_scale = 1.0 / math.sqrt(head_width)

    def one_block(carry, block_item):
        grad_keys, grad_values = carry
        query_block, block_ids, block_mass, grad_block = block_item
        query_heads = query_block.reshape(block_rows, head_count, head_width)
        grad_heads = grad_block.reshape(block_rows, head_count, head_width)
        scores = (
            jnp.einsum("qhe,khe->hqk", query_heads, key_heads, preferred_element_type=jnp.float32)
            * score_scale
        )
        allowed = (block_ids[:, None] == seg_ids[None, :])[None]
        probabilities = jnp.where(allowed, jnp.exp(scores - block_mass[:, :, None]), 0.0)
        rounded = probabilities.astype(jnp.bfloat16)
        grad_values = grad_values + jnp.einsum(
            "hqk,qhe->khe", rounded, grad_heads, preferred_element_type=jnp.float32
        )
        grad_probs = jnp.einsum(
            "qhe,khe->hqk", grad_heads, value_heads, preferred_element_type=jnp.float32
        )
        grad_scores = probabilities * (
            grad_probs - jnp.sum(probabilities * grad_probs, axis=2, keepdims=True)
        )
        grad_scores = grad_scores.astype(jnp.bfloat16)
        grad_query = (
            jnp.einsum("hqk,khe->qhe", grad_scores, key_heads, preferred_element_type=jnp.float32)
            * score_scale
        )
        grad_keys = (
            grad_keys
            + jnp.einsum(
                "hqk,qhe->khe", grad_scores, query_heads, preferred_element_type=jnp.float32
            )
            * score_scale
        )
        return ((grad_keys, grad_values), grad_query.reshape(block_rows, head_count * head_width))

    empty = jnp.zeros((key_count, head_count, head_width), jnp.float32)
    (grad_keys, grad_values), grad_queries = lax.scan(
        one_block,
        (empty, empty),
        (
            queries.reshape(block_count, block_rows, head_count * head_width),
            seg_ids.reshape(block_count, block_rows),
            log_mass,
            grad_context.reshape(block_count, block_rows, head_count * head_width),
        ),
    )
    width = head_count * head_width
    return (
        grad_queries.reshape(key_count, width).astype(jnp.bfloat16),
        grad_keys.reshape(key_count, width).astype(jnp.bfloat16),
        grad_values.reshape(key_count, width).astype(jnp.bfloat16),
    )


def local(
    tokens,
    seg_ids,
    query_weight,
    key_weight,
    value_weight,
    query_bias,
    value_bias,
    out_weight,
    out_bias,
    attention_norm_gain,
    attention_norm_shift,
    up_weight,
    up_bias,
    down_weight,
    down_bias,
    feedforward_norm_gain,
    feedforward_norm_shift,
    cotangent,
):
    head_width = HEAD_DIM
    head_count = query_weight.shape[1] // head_width
    valid_token_mask = (seg_ids >= 0)[:, None]
    queries = (
        jnp.dot(tokens, query_weight, preferred_element_type=jnp.float32) + query_bias
    ).astype(jnp.bfloat16)
    key_rows = jnp.dot(tokens, key_weight, preferred_element_type=jnp.float32).astype(jnp.bfloat16)
    value_rows = (
        jnp.dot(tokens, value_weight, preferred_element_type=jnp.float32) + value_bias
    ).astype(jnp.bfloat16)
    context, log_mass = attend_forward(
        queries, key_rows, value_rows, seg_ids, head_count, head_width
    )
    attn_sum = lax.psum(dot_rows(context, out_weight), "tensor")
    attention_residual = tokens.astype(jnp.float32) + attn_sum + out_bias
    centered_rows_first, inverse_deviation_first = apply_layer_norm(attention_residual)
    hidden_state = centered_rows_first * attention_norm_gain + attention_norm_shift
    hidden_low = hidden_state.astype(jnp.bfloat16)
    up_rows = jnp.dot(hidden_low, up_weight, preferred_element_type=jnp.float32) + up_bias
    act_low = jax.nn.gelu(up_rows, approximate=False).astype(jnp.bfloat16)
    down_sum = lax.psum(dot_rows(act_low, down_weight), "tensor")
    feedforward_residual = hidden_state + down_sum + down_bias
    centered_rows_second, inverse_deviation_second = apply_layer_norm(feedforward_residual)
    mixed = jnp.where(
        valid_token_mask, centered_rows_second * feedforward_norm_gain + feedforward_norm_shift, 0.0
    ).astype(jnp.bfloat16)
    incoming_gradient = jnp.where(valid_token_mask, cotangent.astype(jnp.float32), 0.0)
    grad_res_two, grad_gain_second, grad_shift_second = norm_backward_pass(
        incoming_gradient, centered_rows_second, inverse_deviation_second, feedforward_norm_gain
    )
    grad_down_low = grad_res_two.astype(jnp.bfloat16)
    grad_down_bias = jnp.sum(grad_down_low, axis=0, dtype=jnp.float32)
    grad_down_weight = dot_cols(grad_down_low, act_low)
    grad_act = jnp.dot(grad_down_low, down_weight, preferred_element_type=jnp.float32)
    normal_cdf = 0.5 * (1.0 + lax.erf(up_rows * (1.0 / math.sqrt(2.0))))
    normal_density = jnp.exp(-0.5 * up_rows * up_rows) * (1.0 / math.sqrt(2.0 * math.pi))
    grad_up_low = (grad_act * (normal_cdf + up_rows * normal_density)).astype(jnp.bfloat16)
    grad_up_bias = jnp.sum(grad_up_low, axis=0, dtype=jnp.float32)
    grad_up_weight = dot_cols(hidden_low, grad_up_low)
    back_sum = lax.psum(dot_rows(grad_up_low, up_weight), "tensor")
    hidden_gradient = grad_res_two + back_sum
    grad_res_one, grad_gain_first, grad_shift_first = norm_backward_pass(
        hidden_gradient, centered_rows_first, inverse_deviation_first, attention_norm_gain
    )
    grad_attn_low = grad_res_one.astype(jnp.bfloat16)
    grad_out_bias = jnp.sum(grad_attn_low, axis=0, dtype=jnp.float32)
    grad_out_weight = dot_cols(grad_attn_low, context)
    grad_context = jnp.dot(grad_attn_low, out_weight, preferred_element_type=jnp.float32).astype(
        jnp.bfloat16
    )
    grad_queries, grad_keys, grad_values = attend_backward(
        queries, key_rows, value_rows, seg_ids, log_mass, grad_context, head_count, head_width
    )
    grad_query_bias = jnp.sum(grad_queries, axis=0, dtype=jnp.float32)
    grad_value_bias = jnp.sum(grad_values, axis=0, dtype=jnp.float32)
    grad_query_weight = dot_cols(tokens, grad_queries)
    grad_key_weight = dot_cols(tokens, grad_keys)
    grad_value_weight = dot_cols(tokens, grad_values)
    input_part = (
        dot_rows(grad_queries, query_weight)
        + dot_rows(grad_keys, key_weight)
        + dot_rows(grad_values, value_weight)
    )
    grad_tokens = grad_res_one + lax.psum(input_part, "tensor")
    query_share, key_share, value_share, out_share, up_share, down_share = (
        lax.psum_scatter(grad_query_weight, "dp", scatter_dimension=0, tiled=True),
        lax.psum_scatter(grad_key_weight, "dp", scatter_dimension=0, tiled=True),
        lax.psum_scatter(grad_value_weight, "dp", scatter_dimension=0, tiled=True),
        lax.psum_scatter(grad_out_weight, "dp", scatter_dimension=0, tiled=True),
        lax.psum_scatter(grad_up_weight, "dp", scatter_dimension=0, tiled=True),
        lax.psum_scatter(grad_down_weight, "dp", scatter_dimension=0, tiled=True),
    )
    (
        query_bias_sum,
        value_bias_sum,
        up_bias_sum,
        out_bias_sum,
        gain_first_sum,
        shift_first_sum,
        down_bias_sum,
        gain_second_sum,
        shift_second_sum,
    ) = lax.psum(
        (
            grad_query_bias,
            grad_value_bias,
            grad_up_bias,
            grad_out_bias,
            grad_gain_first,
            grad_shift_first,
            grad_down_bias,
            grad_gain_second,
            grad_shift_second,
        ),
        "dp",
    )
    return (
        mixed,
        grad_tokens,
        query_share,
        key_share,
        value_share,
        query_bias_sum,
        value_bias_sum,
        out_share,
        out_bias_sum,
        gain_first_sum,
        shift_first_sum,
        up_share,
        up_bias_sum,
        down_share,
        down_bias_sum,
        gain_second_sum,
        shift_second_sum,
    )


def solution(mesh):
    return jax.shard_map(
        local,
        mesh=mesh,
        in_specs=(
            P("dp", None),
            P("dp"),
            P(None, "tensor"),
            P(None, "tensor"),
            P(None, "tensor"),
            P("tensor"),
            P("tensor"),
            P(None, "tensor"),
            P(),
            P(),
            P(),
            P(None, "tensor"),
            P("tensor"),
            P(None, "tensor"),
            P(),
            P(),
            P(),
            P("dp", None),
        ),
        out_specs=(
            P("dp", None),
            P("dp", None),
            P("dp", "tensor"),
            P("dp", "tensor"),
            P("dp", "tensor"),
            P("tensor"),
            P("tensor"),
            P("dp", "tensor"),
            P(),
            P(),
            P(),
            P("dp", "tensor"),
            P("tensor"),
            P("dp", "tensor"),
            P(),
            P(),
            P(),
        ),
        check_vma=False,
    )
```

profile of v0, /device:TPU:0, one launch (start us, length us, event | category | flops | bytes accessed | tf_op | source)
XLA Modules:
  0.0 563.0 jit_solution(751926285246381963)
XLA Ops:
  7.2 0.9 broadcast_compare_fusion
  8.2 1.4 fusion.2
  9.5 0.1 copy.62
  9.7 1.4 fusion.1
  11.0 0.1 copy.61
  11.2 1.5 convolution_convert_fusion.1
  12.7 0.1 copy.63
  12.8 0.3 select_reduce_fusion
  13.1 0.1 fusion.23
  13.2 0.2 convolution_convert_fusion.3
  13.4 2.2 fusion.43
  15.6 0.0 all-reduce.8.cloned.1.call-start
  15.7 28.5 %all-reduce.6.cloned.1.call-done = f32[128,768]{1,0:T(8,128)} async-done(((f32[128,768]{1,0:T(8,128)}), f32[128,768]{1,0:T(8,128)}) %all-reduce.6.cloned.1.call-update) | async-done | bytes 393232 | tf_op jit(solution)/shard_map/psum | solution.py:184
  44.2 1.1 fusion.42
  45.4 0.2 multiply_reduce_fusion.6
  45.6 3.8 fusion.7
  49.4 0.7 copy-done.13
  50.1 1.6 fusion.44
  51.9 25.8 %all-reduce.8.cloned.1.call-done = f32[128,768]{1,0:T(8,128)} async-done(((f32[128,768]{1,0:T(8,128)}), f32[128,768]{1,0:T(8,128)}) %all-reduce.8.cloned.1.call-update) | async-done | bytes 393232 | tf_op jit(solution)/shard_map/psum | solution.py:191
  77.7 1.4 fusion.41
  79.1 0.2 multiply_reduce_fusion.5
  79.3 1.8 multiply_reduce_fusion
  81.1 2.4 convert_reduce_fusion.1
  83.6 0.7 copy-done.4
  84.3 1.3 convert_reduce_fusion
  85.6 0.8 copy-done.12
  86.4 1.6 fusion.45
  88.1 0.6 log_add_fusion
  88.7 25.2 %all-reduce.10.cloned.1.call-done = f32[128,768]{1,0:T(8,128)} async-done(((f32[128,768]{1,0:T(8,128)}), f32[128,768]{1,0:T(8,128)}) %all-reduce.10.cloned.1.call-update) | async-done | bytes 393232 | tf_op jit(solution)/shard_map/psum | solution.py:210
  113.9 2.0 multiply_reduce_fusion.1
  115.9 0.8 convert_reduce_fusion.2
  116.7 0.7 copy-done.2
  117.5 0.3 convolution_convert_fusion
  117.7 0.8 copy.65
  118.5 1.9 convert_reduce_fusion.3
  120.4 1.2 multiply_reduce_fusion.2
  121.6 0.9 multiply_convert_fusion
  122.5 0.2 fusion.4
  122.8 1.2 convert_reduce_fusion.4
  124.0 0.3 fusion.46
  124.4 0.3 convolution_add_fusion.2
  124.7 1.1 convolution_add_fusion.1
  125.8 0.0 reduce-scatter.13.cloned.1.call-start
  125.9 2.2 fusion.30
  128.2 1.3 convolution_bitcast_fusion
  129.5 2.7 copy.80
  132.3 1.3 convolution_bitcast_fusion.1
  133.6 2.7 copy.78
  136.5 1.3 convolution_bitcast_fusion.2
  137.8 2.7 copy.76
  140.5 0.0 reduce-scatter.15.cloned.1.call-start
  140.6 4.0 fusion.38
  144.7 0.9 copy-done.5
  145.6 4.0 fusion.33
  149.6 0.6 copy-done.34
  150.2 0.1 reduce_sum.190
  150.3 0.1 reduce_sum.188
  150.4 61.9 %all-reduce = (f32[384]{0:T(512)}, f32[384]{0:T(512)}, f32[768]{0:T(1024)}, f32[768]{0:T(1024)}, f32[768]{0:T(1024)}, /*index=5*/f32[1536]{0:T(1024)}, f32[768]{0:T(1024)}, f32[768]{0:T(1024)}, f32[768]{0:T(1024)}) all-reduce(f32[384]{0:T(512)S(1)} %reduce_sum.188, ...), channel_id=1, replica_groups=mesh['dp'=16,'tensor'=2] {'dp'}, use_global_device_ids=true, to_apply=%region_19.20 | all-reduce | flops 6912 | bytes 55296 | tf_op jit(solution)/shard_map/psum | solution.py:253
  212.3 1.8 add.176
  214.1 61.0 %reduce-scatter.23.cloned.1.call-done = f32[48,384]{1,0:T(8,128)} async-done(((f32[768,384]{1,0:T(8,128)}), f32[48,384]{1,0:T(8,128)}) %reduce-scatter.23.cloned.1.call-update) | async-done | bytes 73744
  275.1 61.3 %reduce-scatter.21.cloned.1.call-done = f32[48,384]{1,0:T(8,128)} async-done(((f32[768,384]{1,0:T(8,128)}), f32[48,384]{1,0:T(8,128)}) %reduce-scatter.21.cloned.1.call-update) | async-done | bytes 73744
  336.4 61.3 %reduce-scatter.19.cloned.1.call-done = f32[48,384]{1,0:T(8,128)} async-done(((f32[768,384]{1,0:T(8,128)}), f32[48,384]{1,0:T(8,128)}) %reduce-scatter.19.cloned.1.call-update) | async-done | bytes 73744
  397.7 79.0 %reduce-scatter.15.cloned.1.call-done = f32[48,1536]{1,0:T(8,128)} async-done(((f32[768,1536]{1,0:T(8,128)}), f32[48,1536]{1,0:T(8,128)}) %reduce-scatter.15.cloned.1.call-update) | async-done | bytes 294928 | tf_op jit(solution)/shard_map/reduce_scatter | solution.py:240
  476.7 79.4 %reduce-scatter.17.cloned.1.call-done = f32[48,1536]{1,0:T(8,128)} async-done(((f32[768,1536]{1,0:T(8,128)}), f32[48,1536]{1,0:T(8,128)}) %reduce-scatter.17.cloned.1.call-update) | async-done | bytes 294928 | tf_op jit(solution)/shard_map/reduce_scatter | solution.py:241
  (109 shorter events, 0.7 us)
Async XLA Ops:
  7.2 38.4 %copy-start = (bf16[768,1536]{1,0:T(8,128)(2,1)S(1)}, bf16[768,1536]{1,0:T(8,128)(2,1)}, u32[]{:S(2)}) copy-start(bf16[768,1536]{1,0:T(8,128)(2,1)} %param.29) | copy-start | bytes 7077892
  7.2 37.0 %all-reduce.6.cloned.1.call-start = ((), (), s32[]{:S(2)}) async-start(), calls=%async_computation.6 | async-start | bytes 786432 | tf_op jit(solution)/shard_map/psum | solution.py:184
  11.2 4.5 copy-start.18
  12.6 31.6 %copy-start.1 = (bf16[128,768]{1,0:T(8,128)(2,1)S(1)}, bf16[128,768]{1,0:T(8,128)(2,1)}, u32[]{:S(2)}) copy-start(bf16[128,768]{1,0:T(8,128)(2,1)} %param.18) | copy-start | bytes 589828
  12.8 32.6 %copy-start.16 = (bf16[128,384]{0,1:T(8,128)(2,1)}, bf16[128,384]{0,1:T(8,128)(2,1)S(1)}, u32[]{:S(2)}) copy-start(bf16[128,384]{0,1:T(8,128)(2,1)S(1)} %copy.63) | copy-start | bytes 294916
  13.1 2.6 copy-start.21
  13.2 2.5 copy-start.32
  13.4 2.3 copy-start.17
  15.6 62.0 %all-reduce.8.cloned.1.call-start = ((), (), s32[]{:S(2)}) async-start(), calls=%async_computation.7 | async-start | bytes 786432 | tf_op jit(solution)/shard_map/psum | solution.py:191
  45.4 70.5 %copy-start.35 = (f32[128]{0:T(128)}, f32[128]{0:T(128)S(1)}, u32[]{:S(2)}) copy-start(f32[128]{0:T(128)S(1)} %broadcast_multiply_fusion.5) | copy-start | bytes 1540
  45.6 70.3 %copy-start.37 = (f32[128]{0:T(128)}, f32[128]{0:T(128)S(1)}, u32[]{:S(2)}) copy-start(f32[128]{0:T(128)S(1)} %add_rsqrt_fusion.1) | copy-start | bytes 1540
  45.6 4.5 copy-start.6
  49.4 0.7 copy-start.13
  49.4 2.4 copy-start.42
  49.4 28.3 %copy-start.19 = (f32[768]{0:T(1024)S(1)}, f32[768]{0:T(1024)}, u32[]{:S(2)}) copy-start(f32[768]{0:T(1024)} %param.27) | copy-start | bytes 9220
  49.4 28.3 %copy-start.24 = (f32[768]{0:T(1024)S(1)}, f32[768]{0:T(1024)}, u32[]{:S(2)}) copy-start(f32[768]{0:T(1024)} %param.28) | copy-start | bytes 9220
  49.4 28.3 %copy-start.40 = (f32[768]{0:T(1024)S(1)}, f32[768]{0:T(1024)}, u32[]{:S(2)}) copy-start(f32[768]{0:T(1024)} %param.32) | copy-start | bytes 9220
  50.1 29.2 %copy-start.23 = (f32[768]{0:T(1024)S(1)}, f32[768]{0:T(1024)}, u32[]{:S(2)}) copy-start(f32[768]{0:T(1024)} %param.33) | copy-start | bytes 9220
  50.1 31.0 %copy-start.41 = (f32[768]{0:T(1024)S(1)}, f32[768]{0:T(1024)}, u32[]{:S(2)}) copy-start(f32[768]{0:T(1024)} %param.34) | copy-start | bytes 9220
  51.8 62.1 %all-reduce.10.cloned.1.call-start = ((), (), s32[]{:S(2)}) async-start(), calls=%async_computation.8 | async-start | bytes 786432 | tf_op jit(solution)/shard_map/psum | solution.py:210
  77.7 6.6 %copy-start.7 = (bf16[768,1536]{1,0:T(8,128)(2,1)S(1)}, bf16[768,1536]{1,0:T(8,128)(2,1)}, u32[]{:S(2)}) copy-start(bf16[768,1536]{1,0:T(8,128)(2,1)} %param.31) | copy-start | bytes 7077892
  77.7 6.6 %copy-start.43 = (f32[128,1536]{1,0:T(8,128)S(1)}, f32[128,1536]{1,0:T(8,128)}, u32[]{:S(2)}) copy-start(f32[128,1536]{1,0:T(8,128)} %get-tuple-element.155) | copy-start | bytes 2359300
  83.6 0.7 copy-start.4
  85.6 0.8 copy-start.12
  85.6 2.5 copy-start.22
  85.6 2.5 copy-start.33
  88.0 124.3 %all-reduce.12.cloned.1.call-start = ((), (), s32[]{:S(2)}) async-start(), calls=%async_computation.9 | async-start | bytes 786432 | tf_op jit(solution)/shard_map/psum | solution.py:234
  113.9 3.5 copy-start.8
  116.7 0.7 copy-start.2
  118.5 5.5 copy-start.9
  118.5 5.9 %copy-start.10 = (bf16[768,384]{1,0:T(8,128)(2,1)S(1)}, bf16[768,384]{1,0:T(8,128)(2,1)}, u32[]{:S(2)}) copy-start(bf16[768,384]{1,0:T(8,128)(2,1)} %param.21) | copy-start | bytes 1769476
  121.6 3.1 copy-start.11
  122.8 2.0 copy-start.14
  122.8 3.1 copy-start.3
  125.8 88.3 %reduce-scatter.13.cloned.1.call-start = ((), (), s32[]{:S(2)}) async-start(), calls=%async_computation.10 | async-start | bytes 1253376 | tf_op jit(solution)/shard_map/reduce_scatter | solution.py:239
  128.2 146.9 %reduce-scatter.23.cloned.1.call-start = ((), (), s32[]{:S(2)}) async-start(), calls=%async_computation.15 | async-start | bytes 1253376
  129.5 2.8 copy-start.15
  132.3 204.1 %reduce-scatter.21.cloned.1.call-start = ((), (), s32[]{:S(2)}) async-start(), calls=%async_computation.14 | async-start | bytes 1253376
  136.4 4.2 copy-start.20
  136.4 4.2 copy-start.25
  136.4 4.2 copy-start.36
  136.4 4.2 copy-start.38
  136.4 261.3 %reduce-scatter.19.cloned.1.call-start = ((), (), s32[]{:S(2)}) async-start(), calls=%async_computation.13 | async-start | bytes 1253376
  140.5 336.2 %reduce-scatter.15.cloned.1.call-start = ((), (), s32[]{:S(2)}) async-start(), calls=%async_computation.11 | async-start | bytes 5013504 | tf_op jit(solution)/shard_map/reduce_scatter | solution.py:240
  144.6 1.0 copy-start.5
  144.6 411.5 %reduce-scatter.17.cloned.1.call-start = ((), (), s32[]{:S(2)}) async-start(), calls=%async_computation.12 | async-start | bytes 5013504 | tf_op jit(solution)/shard_map/reduce_scatter | solution.py:241
  149.6 0.7 copy-start.34
  149.6 0.8 copy-start.26
  149.6 0.8 copy-start.27
  149.6 0.8 copy-start.28
  149.6 0.8 copy-start.29
  149.6 0.8 copy-start.30
  149.6 0.8 copy-start.31
  149.6 0.8 copy-start.39
Sparse Core Ops, SparseCore 0:
  15.8 28.4 all-reduce.5
  51.9 25.7 all-reduce.7
  88.1 25.7 all-reduce.9
  126.0 25.7 all-reduce.11
  155.8 58.1 reduce-scatter.12
  218.0 57.0 reduce-scatter.22
  279.3 57.0 reduce-scatter.20
  340.6 57.0 reduce-scatter.18
  402.2 74.5 reduce-scatter.14
  481.5 74.5 reduce-scatter.16
where the time goes:
time: 564 us; the launch traced here: 563 us
  waiting for transfers between devices  422 us (75%)
  blocking collectives  61.9 us (11%)
  matrix products  35.9 us (6%)
  between operations  14.7 us (3%)
  other arithmetic  14.2 us (3%)
  local copies, waits for them, and re-layouts  14.1 us (2%)
    unnamed x13, waiting for transfers between devices  184 us
    reduce_scatter x1, waiting for transfers between devices, local(): lax.psum_scatter(grad_down_weight, 'dp', scatter_dimension=0, tiled=True)  79.4 us
    reduce_scatter x1, waiting for transfers between devices, local(): lax.psum_scatter(grad_up_weight, 'dp', scatter_dimension=0, tiled=True)  79 us
    psum x1, blocking collectives, local(): lax.psum((grad_query_bias, grad_value_bias, grad_up_bias, grad_out_bias,...  61.9 us
    psum x1, waiting for transfers between devices, local(): attn_sum = lax.psum(dot_rows(context, out_weight), 'tensor')  28.5 us
    psum x1, waiting for transfers between devices, local(): down_sum = lax.psum(dot_rows(act_low, down_weight), 'tensor')  25.8 us
    psum x1, waiting for transfers between devices, local(): back_sum = lax.psum(dot_rows(grad_up_low, up_weight), 'tensor')  25.2 us
    dot_general x6, matrix products, dot_cols(): lax.dot_general(left, right, (((0,), (0,)), ((), ())), preferred_element_...  14.1 us
  transfers between devices with their start and end apart: 10, of which 8 were waited for; matrix products, arithmetic and copies ran while one was open for 4% of the time, Pallas kernels for 0%

commit v1 on v0

--- a/solution.py
+++ b/solution.py
@@ -22,6 +22,36 @@
     return lax.dot_general(
         left, right, (((0,), (0,)), ((), ())), preferred_element_type=jnp.float32
     )
+
+
+def tensor_sum(part):
+    size = lax.axis_size("tensor")
+    if size != 2:
+        return lax.psum(part, "tensor")
+    return part + lax.ppermute(part, "tensor", [(0, 1), (1, 0)])
+
+
+def dp_sum(part):
+    size = lax.axis_size("dp")
+    if size & (size - 1):
+        return lax.psum(part, "dp")
+    step = 1
+    while step < size:
+        part = part + lax.ppermute(part, "dp", [(i, i ^ step) for i in range(size)])
+        step *= 2
+    return part
+
+
+def dp_share(parts):
+    widths = [part.shape[1] for part in parts]
+    share = lax.psum_scatter(
+        jnp.concatenate(parts, axis=1), "dp", scatter_dimension=0, tiled=True
+    )
+    shares, start = [], 0
+    for width in widths:
+        shares.append(share[:, start : start + width])
+        start += width
+    return shares
 
 
 def apply_layer_norm(rows):
@@ -181,14 +211,14 @@
     context, log_mass = attend_forward(
         queries, key_rows, value_rows, seg_ids, head_count, head_width
     )
-    attn_sum = lax.psum(dot_rows(context, out_weight), "tensor")
+    attn_sum = tensor_sum(dot_rows(context, out_weight))
     attention_residual = tokens.astype(jnp.float32) + attn_sum + out_bias
     centered_rows_first, inverse_deviation_first = apply_layer_norm(attention_residual)
     hidden_state = centered_rows_first * attention_norm_gain + attention_norm_shift
     hidden_low = hidden_state.astype(jnp.bfloat16)
     up_rows = jnp.dot(hidden_low, up_weight, preferred_element_type=jnp.float32) + up_bias
     act_low = jax.nn.gelu(up_rows, approximate=False).astype(jnp.bfloat16)
-    down_sum = lax.psum(dot_rows(act_low, down_weight), "tensor")
+    down_sum = tensor_sum(dot_rows(act_low, down_weight))
     feedforward_residual = hidden_state + down_sum + down_bias
     centered_rows_second, inverse_deviation_second = apply_layer_norm(feedforward_residual)
     mixed = jnp.where(
@@ -207,7 +237,7 @@
     grad_up_low = (grad_act * (normal_cdf + up_rows * normal_density)).astype(jnp.bfloat16)
     grad_up_bias = jnp.sum(grad_up_low, axis=0, dtype=jnp.float32)
     grad_up_weight = dot_cols(hidden_low, grad_up_low)
-    back_sum = lax.psum(dot_rows(grad_up_low, up_weight), "tensor")
+    back_sum = tensor_sum(dot_rows(grad_up_low, up_weight))
     hidden_gradient = grad_res_two + back_sum
     grad_res_one, grad_gain_first, grad_shift_first = norm_backward_pass(
         hidden_gradient, centered_rows_first, inverse_deviation_first, attention_norm_gain
@@ -231,15 +261,27 @@
         + dot_rows(grad_keys, key_weight)
         + dot_rows(grad_values, value_weight)
     )
-    grad_tokens = grad_res_one + lax.psum(input_part, "tensor")
-    query_share, key_share, value_share, out_share, up_share, down_share = (
-        lax.psum_scatter(grad_query_weight, "dp", scatter_dimension=0, tiled=True),
-        lax.psum_scatter(grad_key_weight, "dp", scatter_dimension=0, tiled=True),
-        lax.psum_scatter(grad_value_weight, "dp", scatter_dimension=0, tiled=True),
-        lax.psum_scatter(grad_out_weight, "dp", scatter_dimension=0, tiled=True),
-        lax.psum_scatter(grad_up_weight, "dp", scatter_dimension=0, tiled=True),
-        lax.psum_scatter(grad_down_weight, "dp", scatter_dimension=0, tiled=True),
-    )
+    grad_tokens = grad_res_one + tensor_sum(input_part)
+    down_share, up_share = dp_share([grad_down_weight, grad_up_weight])
+    query_share, key_share, value_share, out_share = dp_share(
+        [grad_query_weight, grad_key_weight, grad_value_weight, grad_out_weight]
+    )
+    rows = [
+        grad_query_bias,
+        grad_value_bias,
+        grad_up_bias,
+        grad_out_bias,
+        grad_gain_first,
+        grad_shift_first,
+        grad_down_bias,
+        grad_gain_second,
+        grad_shift_second,
+    ]
+    sums, start = [], 0
+    total = dp_sum(jnp.concatenate(rows))
+    for row in rows:
+        sums.append(total[start : start + row.shape[0]])
+        start += row.shape[0]
     (
         query_bias_sum,
         value_bias_sum,
@@ -250,20 +292,7 @@
         down_bias_sum,
         gain_second_sum,
         shift_second_sum,
-    ) = lax.psum(
-        (
-            grad_query_bias,
-            grad_value_bias,
-            grad_up_bias,
-            grad_out_bias,
-            grad_gain_first,
-            grad_shift_first,
-            grad_down_bias,
-            grad_gain_second,
-            grad_shift_second,
-        ),
-        "dp",
-    )
+    ) = sums
     return (
         mixed,
         grad_tokens,

time: 564 us -> 278 us (0.49)
  waiting for transfers between devices: 422 us -> 177 us
  blocking collectives: 61.9 us -> 0 us
  local copies, waits for them, and re-layouts: 14.1 us -> 29 us
  starting transfers between devices: 0.42 us -> 11.5 us
  matrix products: 35.9 us -> 25.4 us
    unnamed x13 -> x3, waiting for transfers between devices: 184 us -> 26.8 us
    psum x4 -> x0, waiting for transfers between devices: 79.5 us -> none  [the longest x1 28.5 us: local(): attn_sum = lax.psum(dot_rows(context, out_weight), 'tensor')]
    psum x1 -> x0, blocking collectives: 61.9 us -> none  [local(): lax.psum((grad_query_bias, grad_value_bias, grad_up_bias, grad_out_bias,...]
    reduce_scatter x3 -> x1, waiting for transfers between devices: 158 us -> 113 us  [dp_share(): lax.psum_scatter(jnp.concatenate(parts, axis=1), 'dp', scatter_dimension=...]
    ppermute x0 -> x8, waiting for transfers between devices: none -> 37.1 us  [the longest x4 27.6 us: tensor_sum(): return part + lax.ppermute(part, 'tensor', [(0, 1), (1, 0)])]
    ppermute x0 -> x8, starting transfers between devices: none -> 11.2 us  [the longest x4 7.97 us: tensor_sum(): return part + lax.ppermute(part, 'tensor', [(0, 1), (1, 0)])]
    concatenate x0 -> x2, other arithmetic: none -> 9.66 us  [dp_share(): jnp.concatenate(parts, axis=1)]
    dot_general x6, matrix products: 14.1 us -> 6 us  [dot_cols(): lax.dot_general(left, right, (((0,), (0,)), ((), ())), preferred_element_...]
  transfers between devices with their start and end apart: 10 -> 10, of which waited for: 8 -> 10; matrix products, arithmetic and copies ran while one was open for 4% -> 13% of each run, Pallas kernels for 0% -> 0%
where the time goes in v1:
time: 278 us; the launch traced here: 277 us
  waiting for transfers between devices  177 us (64%)
  local copies, waits for them, and re-layouts  29 us (10%)
  matrix products  25.4 us (9%)
  other arithmetic  19 us (7%)
  between operations  14.6 us (5%)
  starting transfers between devices  11.5 us (4%)
    reduce_scatter x1, waiting for transfers between devices, dp_share(): lax.psum_scatter(jnp.concatenate(parts, axis=1), 'dp', scatter_dimension=...  113 us
    ppermute x4, waiting for transfers between devices, tensor_sum(): return part + lax.ppermute(part, 'tensor', [(0, 1), (1, 0)])  27.6 us
    unnamed x3, waiting for transfers between devices  26.8 us
    unnamed x89, local copies, waits for them, and re-layouts  18.2 us
    concatenate x2, other arithmetic, dp_share(): jnp.concatenate(parts, axis=1)  9.66 us
    ppermute x4, waiting for transfers between devices, dp_sum(): part = part + lax.ppermute(part, 'dp', [(i, i ^ step) for i in range(size)])  9.53 us
    ppermute x4, starting transfers between devices, tensor_sum(): return part + lax.ppermute(part, 'tensor', [(0, 1), (1, 0)])  7.97 us
    dot_general x6, matrix products, dot_rows(): lax.dot_general(left, right, (((1,), (1,)), ((), ())), preferred_element_...  6.18 us
  transfers between devices with their start and end apart: 10, of which 10 were waited for; matrix products, arithmetic and copies ran while one was open for 13% of the time, Pallas kernels for 0%

profile of v1, /device:TPU:0, one launch (start us, length us, event | category | flops | bytes accessed | tf_op | source)
XLA Modules:
  0.0 276.8 jit_solution(8371184308490384005)
XLA Ops:
  7.2 0.9 broadcast_compare_fusion
  8.2 1.4 fusion.2
  9.7 1.4 fusion.1
  11.2 1.5 convolution_convert_fusion.1
  13.4 1.4 fusion.47
  14.9 3.0 %collective-permute-start = (f32[128,768]{1,0:T(8,128)S(1)}, f32[128,768]{1,0:T(8,128)S(1)}, u32[]{:S(2)}, u32[]{:S(2)}) collective-permute-start(f32[128,768]{1,0:T(8,128)S(1)} %fusion.47), channel_id=1, source_target_pairs={{0,1},{1,0},{2,3},{3,2},{4,5},{5,4},{6,7},{7,6},{8,9},{9,8},{10,11... | collective-permute-start | bytes 1179656 | tf_op jit(solution)/shard_map/ppermute | solution.py:31
  17.9 9.1 %collective-permute-done = f32[128,768]{1,0:T(8,128)S(1)} collective-permute-done((f32[128,768]{1,0:T(8,128)S(1)}, f32[128,768]{1,0:T(8,128)S(1)}, u32[]{:S(2)}, u32[]{:S(2)}) %collective-permute-start) | collective-permute-done | bytes 393248 | tf_op jit(solution)/shard_map/ppermute | solution.py:31
  27.1 0.8 fusion.42
  28.2 2.1 fusion.7
  30.3 0.9 fusion.48
  31.2 1.8 collective-permute-start.1
  33.0 8.6 %collective-permute-done.1 = f32[128,768]{1,0:T(8,128)S(1)} collective-permute-done((f32[128,768]{1,0:T(8,128)S(1)}, f32[128,768]{1,0:T(8,128)S(1)}, u32[]{:S(2)}, u32[]{:S(2)}) %collective-permute-start.1) | collective-permute-done | bytes 393248 | tf_op jit(solution)/shard_map/ppermute | solution.py:31
  42.1 0.8 multiply_reduce_fusion
  42.9 1.5 convert_reduce_fusion.1
  44.4 1.3 convert_reduce_fusion
  45.7 0.9 fusion.49
  46.6 1.5 collective-permute-start.2
  48.1 0.6 log_add_fusion
  48.7 7.3 %collective-permute-done.2 = f32[128,768]{1,0:T(8,128)S(1)} collective-permute-done((f32[128,768]{1,0:T(8,128)S(1)}, f32[128,768]{1,0:T(8,128)S(1)}, u32[]{:S(2)}, u32[]{:S(2)}) %collective-permute-start.2) | collective-permute-done | bytes 393248 | tf_op jit(solution)/shard_map/ppermute | solution.py:31
  56.1 0.8 multiply_reduce_fusion.1
  56.9 0.8 convert_reduce_fusion.2
  57.6 0.7 copy-done.2
  58.4 0.9 convolution_convert_fusion
  59.3 1.6 copy.67
  60.9 1.9 convert_reduce_fusion.3
  62.8 1.3 multiply_reduce_fusion.2
  64.1 0.8 multiply_convert_fusion
  65.1 0.9 convert_reduce_fusion.4
  67.2 2.4 pad_maximum_fusion.1
  69.7 6.1 %copy.79 = f32[768,1536]{1,0:T(8,128)} copy(f32[768,1536]{0,1:T(8,128)} %pad_maximum_fusion.1) | data formatting | bytes 9437184
  76.1 0.7 copy-done.6
  76.8 1.8 fusion.33
  78.6 3.0 %fusion.38 = f32[768,1536]{1,0:T(8,128)} fusion(bf16[128,1536]{1,0:T(8,128)(2,1)S(1)} %copy-done.12, f32[128,768]{1,0:T(8,128)S(1)} %get-tuple-element.141, f32[768]{0:T(1024)S(1)} %copy-done.27, f32[768]{0:T(1024)S(1)} %copy-done.24, f32[128]{0:T(128)S(1)} %copy-done.35, f32[128]{0:T(128)S(1)} %copy-done.33), kind=kOutput, calls=%fused_computation.114 | convolution fusion | flops 302481408 | bytes 5512192 | tf_op jit(solution)/shard_map/dot_general | solution.py:22
  81.6 7.2 %pad_maximum_fusion = f32[768,3072]{1,0:T(8,128)} fusion(f32[768,1536]{1,0:T(8,128)} %fusion.38, f32[768,1536]{1,0:T(8,128)S(1)} %fusion.33), kind=kLoop, calls=%fused_computation | loop fusion | flops 2359296 | bytes 18874368 | tf_op jit(solution)/shard_map/concatenate | solution.py:48
  88.9 1.5 reduce_sum.190
  90.4 1.3 reduce_sum.188
  91.7 1.4 constant_dynamic-update-slice_fusion.8
  93.1 1.3 constant_dynamic-update-slice_fusion.7
  94.4 1.3 constant_dynamic-update-slice_fusion.6
  95.7 1.3 constant_dynamic-update-slice_fusion.5
  97.0 1.3 constant_dynamic-update-slice_fusion.4
  98.3 1.3 constant_dynamic-update-slice_fusion.3
  99.6 1.3 constant_dynamic-update-slice_fusion.2
  100.9 1.3 constant_dynamic-update-slice_fusion.1
  102.2 0.6 constant_dynamic-update-slice_fusion
  102.8 1.4 collective-permute-done.4
  104.3 0.8 add.171
  105.0 1.1 collective-permute-start.5
  106.2 1.3 fusion.50
  107.4 1.9 collective-permute-done.5
  109.3 1.0 collective-permute-start.6
  110.3 1.4 convolution_add_fusion.2
  111.7 3.2 %collective-permute-done.6 = f32[6912]{0:T(1024)S(1)} collective-permute-done((f32[6912]{0:T(1024)S(1)}, f32[6912]{0:T(1024)S(1)}, u32[]{:S(2)}, u32[]{:S(2)}) %collective-permute-start.6) | collective-permute-done | bytes 27680 | tf_op jit(solution)/shard_map/ppermute | solution.py:40
  115.0 1.1 collective-permute-start.7
  116.5 1.6 collective-permute-start.3
  118.1 3.0 %collective-permute-done.7 = f32[6912]{0:T(1024)S(1)} collective-permute-done((f32[6912]{0:T(1024)S(1)}, f32[6912]{0:T(1024)S(1)}, u32[]{:S(2)}, u32[]{:S(2)}) %collective-permute-start.7) | collective-permute-done | bytes 27680 | tf_op jit(solution)/shard_map/ppermute | solution.py:40
  121.1 0.6 slice.70
  122.3 0.6 fusion.45
  122.9 2.5 collective-permute-done.3
  125.4 0.8 add_add_fusion
  126.2 26.8 %reduce-scatter.7.cloned.1.call-done = f32[48,1536]{1,0:T(8,128)} async-done(((f32[768,1536]{1,0:T(8,128)}), f32[48,1536]{1,0:T(8,128)}) %reduce-scatter.7.cloned.1.call-update) | async-done | bytes 294928
  153.0 1.7 fusion.44
  154.7 113.4 %reduce-scatter.5.cloned.1.call-done = f32[48,3072]{1,0:T(8,128)} async-done(((f32[768,3072]{1,0:T(8,128)}), f32[48,3072]{1,0:T(8,128)}) %reduce-scatter.5.cloned.1.call-update) | async-done | bytes 589840 | tf_op jit(solution)/shard_map/reduce_scatter | solution.py:47
  268.1 1.9 fusion.43
  (111 shorter events, 4.5 us)
Async XLA Ops:
  7.2 20.9 %copy-start = (bf16[768,1536]{1,0:T(8,128)(2,1)S(1)}, bf16[768,1536]{1,0:T(8,128)(2,1)}, u32[]{:S(2)}) copy-start(bf16[768,1536]{1,0:T(8,128)(2,1)} %param.29) | copy-start | bytes 7077892
  7.2 145.8 %reduce-scatter.7.cloned.1.call-start = ((), (), s32[]{:S(2)}) async-start(), calls=%async_computation.3 | async-start | bytes 5013504
  11.2 3.7 %copy-start.22 = (bf16[128,384]{0,1:T(8,128)(2,1)}, bf16[128,384]{0,1:T(8,128)(2,1)S(1)}, u32[]{:S(2)}) copy-start(bf16[128,384]{0,1:T(8,128)(2,1)S(1)} %copy.63) | copy-start | bytes 294916
  11.2 15.9 %copy-start.1 = (bf16[128,768]{1,0:T(8,128)(2,1)S(1)}, bf16[128,768]{1,0:T(8,128)(2,1)}, u32[]{:S(2)}) copy-start(bf16[128,768]{1,0:T(8,128)(2,1)} %param.18) | copy-start | bytes 589828
  13.2 15.0 %copy-start.23 = (f32[768]{0:T(1024)S(1)}, f32[768]{0:T(1024)}, u32[]{:S(2)}) copy-start(f32[768]{0:T(1024)} %param.27) | copy-start | bytes 9220
  13.2 15.0 %copy-start.26 = (f32[768]{0:T(1024)S(1)}, f32[768]{0:T(1024)}, u32[]{:S(2)}) copy-start(f32[768]{0:T(1024)} %param.28) | copy-start | bytes 9220
  13.2 15.0 %copy-start.39 = (f32[1536]{0:T(1024)S(1)}, f32[1536]{0:T(1024)}, u32[]{:S(2)}) copy-start(f32[1536]{0:T(1024)} %param.30) | copy-start | bytes 18436
  13.4 14.7 %copy-start.20 = (bf16[6,64,128]{2,1,0:T(8,128)(2,1)}, bf16[6,64,128]{2,1,0:T(8,128)(2,1)S(1)}, u32[]{:S(2)}) copy-start(bf16[6,64,128]{2,1,0:T(8,128)(2,1)S(1)} %convolution_convert_fusion.3) | copy-start | bytes 294916
  14.9 12.2 %collective-permute-start = (f32[128,768]{1,0:T(8,128)S(1)}, f32[128,768]{1,0:T(8,128)S(1)}, u32[]{:S(2)}, u32[]{:S(2)}) collective-permute-start(f32[128,768]{1,0:T(8,128)S(1)} %fusion.47), channel_id=1, source_target_pairs={{0,1},{1,0},{2,3},{3,2},{4,5},{5,4},{6,7},{7,6},{8,9},{9,8},{10,11... | collective-permute-start | bytes 1179656 | tf_op jit(solution)/shard_map/ppermute | solution.py:31
  27.9 28.9 %copy-start.32 = (f32[128]{0:T(128)}, f32[128]{0:T(128)S(1)}, u32[]{:S(2)}) copy-start(f32[128]{0:T(128)S(1)} %broadcast_multiply_fusion.5) | copy-start | bytes 1540
  28.2 28.7 %copy-start.34 = (f32[128]{0:T(128)}, f32[128]{0:T(128)S(1)}, u32[]{:S(2)}) copy-start(f32[128]{0:T(128)S(1)} %add_rsqrt_fusion.1) | copy-start | bytes 1540
  28.2 2.1 copy-start.7
  30.3 11.6 %copy-start.13 = (bf16[128,1536]{1,0:T(8,128)(2,1)}, bf16[128,1536]{1,0:T(8,128)(2,1)S(1)}, u32[]{:S(2)}) copy-start(bf16[128,1536]{1,0:T(8,128)(2,1)S(1)} %get-tuple-element.159) | copy-start | bytes 1179652
  30.3 2.7 copy-start.38
  30.3 11.3 %copy-start.36 = (f32[768]{0:T(1024)S(1)}, f32[768]{0:T(1024)}, u32[]{:S(2)}) copy-start(f32[768]{0:T(1024)} %param.32) | copy-start | bytes 9220
  30.3 11.8 %copy-start.19 = (bf16[128,768]{1,0:T(8,128)(2,1)S(1)}, bf16[128,768]{1,0:T(8,128)(2,1)}, u32[]{:S(2)}) copy-start(bf16[128,768]{1,0:T(8,128)(2,1)} %param.35) | copy-start | bytes 589828
  30.3 11.8 %copy-start.25 = (f32[768]{0:T(1024)S(1)}, f32[768]{0:T(1024)}, u32[]{:S(2)}) copy-start(f32[768]{0:T(1024)} %param.33) | copy-start | bytes 9220
  30.3 12.6 %copy-start.37 = (f32[768]{0:T(1024)S(1)}, f32[768]{0:T(1024)}, u32[]{:S(2)}) copy-start(f32[768]{0:T(1024)} %param.34) | copy-start | bytes 9220
  31.2 10.4 %collective-permute-start.1 = (f32[128,768]{1,0:T(8,128)S(1)}, f32[128,768]{1,0:T(8,128)S(1)}, u32[]{:S(2)}, u32[]{:S(2)}) collective-permute-start(f32[128,768]{1,0:T(8,128)S(1)} %fusion.48), channel_id=1, source_target_pairs={{0,1},{1,0},{2,3},{3,2},{4,5},{5,4},{6,7},{7,6},{8,9},{9,8},{10,11... | collective-permute-start | bytes 1179656 | tf_op jit(solution)/shard_map/ppermute | solution.py:31
  44.4 11.6 %copy-start.5 = (f32[128,768]{1,0:T(8,128)}, f32[128,768]{1,0:T(8,128)S(1)}, u32[]{:S(2)}) copy-start(f32[128,768]{1,0:T(8,128)S(1)} %get-tuple-element.134) | copy-start | bytes 1179652
  45.7 11.1 %copy-start.11 = (bf16[128,1536]{1,0:T(8,128)(2,1)}, bf16[128,1536]{1,0:T(8,128)(2,1)S(1)}, u32[]{:S(2)}) copy-start(bf16[128,1536]{1,0:T(8,128)(2,1)S(1)} %get-tuple-element.168) | copy-start | bytes 1179652
  46.6 11.8 %copy-start.8 = (bf16[768,384]{1,0:T(8,128)(2,1)S(1)}, bf16[768,384]{1,0:T(8,128)(2,1)}, u32[]{:S(2)}) copy-start(bf16[768,384]{1,0:T(8,128)(2,1)} %param.25) | copy-start | bytes 1769476
  46.6 9.4 %collective-permute-start.2 = (f32[128,768]{1,0:T(8,128)S(1)}, f32[128,768]{1,0:T(8,128)S(1)}, u32[]{:S(2)}, u32[]{:S(2)}) collective-permute-start(f32[128,768]{1,0:T(8,128)S(1)} %fusion.49), channel_id=1, source_target_pairs={{0,1},{1,0},{2,3},{3,2},{4,5},{5,4},{6,7},{7,6},{8,9},{9,8},{10,11... | collective-permute-start | bytes 1179656 | tf_op jit(solution)/shard_map/ppermute | solution.py:31
  57.6 0.7 copy-start.2
  60.9 5.1 %copy-start.3 = (f32[128,768]{1,0:T(8,128)S(1)}, f32[128,768]{1,0:T(8,128)}, u32[]{:S(2)}) copy-start(f32[128,768]{1,0:T(8,128)} %copy-done.2) | copy-start | bytes 1179652
  60.9 5.1 %copy-start.21 = (bf16[6,64,128]{2,1,0:T(8,128)(2,1)S(1)}, bf16[6,64,128]{2,1,0:T(8,128)(2,1)}, u32[]{:S(2)}) copy-start(bf16[6,64,128]{2,1,0:T(8,128)(2,1)} %copy-done.20) | copy-start | bytes 294916
  62.8 3.8 %copy-start.14 = (bf16[6,64,128]{2,1,0:T(8,128)(2,1)}, bf16[6,64,128]{2,1,0:T(8,128)(2,1)S(1)}, u32[]{:S(2)}) copy-start(bf16[6,64,128]{2,1,0:T(8,128)(2,1)S(1)} %get-tuple-element.166) | copy-start | bytes 294916
  65.1 1.8 copy-start.16
  66.0 1.2 copy-start.18
  75.8 1.0 copy-start.6
  75.8 2.8 copy-start.12
  75.8 2.8 copy-start.24
  75.8 2.8 copy-start.27
  75.8 2.8 copy-start.33
  75.8 2.8 copy-start.35
  75.8 192.3 %reduce-scatter.5.cloned.1.call-start = ((), (), s32[]{:S(2)}) async-start(), calls=%async_computation.2 | async-start | bytes 10027008 | tf_op jit(solution)/shard_map/reduce_scatter | solution.py:47
  88.8 9.5 %copy-start.31 = (f32[768]{0:T(1024)S(1)}, f32[768]{0:T(1024)}, u32[]{:S(2)}) copy-start(f32[768]{0:T(1024)} %get-tuple-element.130) | copy-start | bytes 9220
  88.8 10.8 %copy-start.30 = (f32[768]{0:T(1024)S(1)}, f32[768]{0:T(1024)}, u32[]{:S(2)}) copy-start(f32[768]{0:T(1024)} %get-tuple-element.133) | copy-start | bytes 9220
  88.8 12.1 %copy-start.29 = (f32[768]{0:T(1024)S(1)}, f32[768]{0:T(1024)}, u32[]{:S(2)}) copy-start(f32[768]{0:T(1024)} %get-tuple-element.127) | copy-start | bytes 9220
  88.8 13.4 %copy-start.28 = (f32[768]{0:T(1024)S(1)}, f32[768]{0:T(1024)}, u32[]{:S(2)}) copy-start(f32[768]{0:T(1024)} %get-tuple-element.132) | copy-start | bytes 9220
  88.9 17.3 %copy-start.9 = (bf16[768,384]{1,0:T(8,128)(2,1)S(1)}, bf16[768,384]{1,0:T(8,128)(2,1)}, u32[]{:S(2)}) copy-start(bf16[768,384]{1,0:T(8,128)(2,1)} %param.20) | copy-start | bytes 1769476
  88.9 21.5 %copy-start.17 = (bf16[6,64,128]{2,1,0:T(8,128)(2,1)S(1)}, bf16[6,64,128]{2,1,0:T(8,128)(2,1)}, u32[]{:S(2)}) copy-start(bf16[6,64,128]{2,1,0:T(8,128)(2,1)} %copy-done.16) | copy-start | bytes 294916
  88.9 27.2 %copy-start.15 = (bf16[6,64,128]{2,1,0:T(8,128)(2,1)S(1)}, bf16[6,64,128]{2,1,0:T(8,128)(2,1)}, u32[]{:S(2)}) copy-start(bf16[6,64,128]{2,1,0:T(8,128)(2,1)} %copy-done.14) | copy-start | bytes 294916
  88.9 36.5 %copy-start.4 = (f32[128,768]{1,0:T(8,128)S(1)}, f32[128,768]{1,0:T(8,128)}, u32[]{:S(2)}) copy-start(f32[128,768]{1,0:T(8,128)} %copy-done.2) | copy-start | bytes 1179652
  91.7 24.4 %copy-start.10 = (bf16[768,384]{1,0:T(8,128)(2,1)S(1)}, bf16[768,384]{1,0:T(8,128)(2,1)}, u32[]{:S(2)}) copy-start(bf16[768,384]{1,0:T(8,128)(2,1)} %param.22) | copy-start | bytes 1769476
  102.8 1.4 collective-permute-start.4
  105.0 4.3 %collective-permute-start.5 = (f32[6912]{0:T(1024)S(1)}, f32[6912]{0:T(1024)S(1)}, u32[]{:S(2)}, u32[]{:S(2)}) collective-permute-start(f32[6912]{0:T(1024)S(1)} %add.171), channel_id=1, source_target_pairs={{0,4},{2,6},{4,0},{6,2},{8,12},{10,14},{12,8},{14,10},{16,20},{18,... | collective-permute-start | bytes 82952 | tf_op jit(solution)/shard_map/ppermute | solution.py:40
  109.3 5.6 %collective-permute-start.6 = (f32[6912]{0:T(1024)S(1)}, f32[6912]{0:T(1024)S(1)}, u32[]{:S(2)}, u32[]{:S(2)}) collective-permute-start(f32[6912]{0:T(1024)S(1)} %add.172), channel_id=1, source_target_pairs={{0,8},{2,10},{4,12},{6,14},{8,0},{10,2},{12,4},{14,6},{16,24},{18,... | collective-permute-start | bytes 82952 | tf_op jit(solution)/shard_map/ppermute | solution.py:40
  115.0 6.1 %collective-permute-start.7 = (f32[6912]{0:T(1024)S(1)}, f32[6912]{0:T(1024)S(1)}, u32[]{:S(2)}, u32[]{:S(2)}) collective-permute-start(f32[6912]{0:T(1024)S(1)} %add.173), channel_id=1, source_target_pairs={{0,16},{2,18},{4,20},{6,22},{8,24},{10,26},{12,28},{14,30},{16,0},... | collective-permute-start | bytes 82952 | tf_op jit(solution)/shard_map/ppermute | solution.py:40
  116.5 8.9 %collective-permute-start.3 = (f32[128,768]{1,0:T(8,128)S(1)}, f32[128,768]{1,0:T(8,128)S(1)}, u32[]{:S(2)}, u32[]{:S(2)}) collective-permute-start(f32[128,768]{1,0:T(8,128)S(1)} %convolution_add_fusion.1), channel_id=1, source_target_pairs={{0,1},{1,0},{2,3},{3,2},{4,5},{5,4},{6,7},{7,6},{8,9},{9,8},{10,11... | collective-permute-start | bytes 1179656 | tf_op jit(solution)/shard_map/ppermute | solution.py:31
Sparse Core Ops, SparseCore 0:
  75.9 77.0 reduce-scatter.6
  157.6 110.4 reduce-scatter.4

commit v2 on v1

--- a/solution.py
+++ b/solution.py
@@ -42,16 +42,52 @@
     return part
 
 
-def dp_share(parts):
-    widths = [part.shape[1] for part in parts]
-    share = lax.psum_scatter(
-        jnp.concatenate(parts, axis=1), "dp", scatter_dimension=0, tiled=True
-    )
-    shares, start = [], 0
-    for width in widths:
-        shares.append(share[:, start : start + width])
-        start += width
-    return shares
+def dp_share(left, right, order):
+    size = lax.axis_size("dp")
+    count = size.bit_length() - 1
+    if size != 1 << count:
+        return lax.psum_scatter(dot_cols(left, right), "dp", scatter_dimension=0, tiled=True)
+    place = lax.axis_index("dp")
+    tokens, width = right.shape
+    rows = left.shape[1] // size
+    axes = list(range(count - 1, -1, -1))
+    part = left.T.reshape((2,) * count + (rows, tokens))
+    for step, bit in enumerate(order(count)):
+        axis = axes.index(bit)
+        mine = (place >> bit) & 1
+        send = lax.dynamic_index_in_dim(part, 1 - mine, axis, keepdims=False)
+        keep = lax.dynamic_index_in_dim(part, mine, axis, keepdims=False)
+        axes.remove(bit)
+        if step == 0:
+            shape = (2,) * len(axes) + (rows, width)
+            send, keep = (
+                jnp.dot(
+                    half.reshape(-1, tokens), right, preferred_element_type=jnp.float32
+                ).reshape(shape)
+                for half in (send, keep)
+            )
+        got = lax.ppermute(send, "dp", [(i, i ^ (1 << bit)) for i in range(size)])
+        part = keep + got
+    return part
+
+
+def upward(count):
+    return list(range(count))
+
+
+def rotated(count):
+    return [0] + list(range(2, count)) + list(range(1, min(2, count)))
+
+
+def dp_share_halves(left, right):
+    middle = right.shape[1] // 2
+    return jnp.concatenate(
+        [
+            dp_share(left, right[:, :middle], upward),
+            dp_share(left, right[:, middle:], rotated),
+        ],
+        axis=1,
+    )
 
 
 def apply_layer_norm(rows):
@@ -230,13 +266,13 @@
     )
     grad_down_low = grad_res_two.astype(jnp.bfloat16)
     grad_down_bias = jnp.sum(grad_down_low, axis=0, dtype=jnp.float32)
-    grad_down_weight = dot_cols(grad_down_low, act_low)
+    down_share = dp_share_halves(grad_down_low, act_low)
     grad_act = jnp.dot(grad_down_low, down_weight, preferred_element_type=jnp.float32)
     normal_cdf = 0.5 * (1.0 + lax.erf(up_rows * (1.0 / math.sqrt(2.0))))
     normal_density = jnp.exp(-0.5 * up_rows * up_rows) * (1.0 / math.sqrt(2.0 * math.pi))
     grad_up_low = (grad_act * (normal_cdf + up_rows * normal_density)).astype(jnp.bfloat16)
     grad_up_bias = jnp.sum(grad_up_low, axis=0, dtype=jnp.float32)
-    grad_up_weight = dot_cols(hidden_low, grad_up_low)
+    up_share = dp_share_halves(hidden_low, grad_up_low)
     back_sum = tensor_sum(dot_rows(grad_up_low, up_weight))
     hidden_gradient = grad_res_two + back_sum
     grad_res_one, grad_gain_first, grad_shift_first = norm_backward_pass(
@@ -244,7 +280,7 @@
     )
     grad_attn_low = grad_res_one.astype(jnp.bfloat16)
     grad_out_bias = jnp.sum(grad_attn_low, axis=0, dtype=jnp.float32)
-    grad_out_weight = dot_cols(grad_attn_low, context)
+    out_share = dp_share(grad_attn_low, context, upward)
     grad_context = jnp.dot(grad_attn_low, out_weight, preferred_element_type=jnp.float32).astype(
         jnp.bfloat16
     )
@@ -253,19 +289,15 @@
     )
     grad_query_bias = jnp.sum(grad_queries, axis=0, dtype=jnp.float32)
     grad_value_bias = jnp.sum(grad_values, axis=0, dtype=jnp.float32)
-    grad_query_weight = dot_cols(tokens, grad_queries)
-    grad_key_weight = dot_cols(tokens, grad_keys)
-    grad_value_weight = dot_cols(tokens, grad_values)
+    query_share = dp_share(tokens, grad_queries, upward)
+    key_share = dp_share(tokens, grad_keys, rotated)
+    value_share = dp_share(tokens, grad_values, rotated)
     input_part = (
         dot_rows(grad_queries, query_weight)
         + dot_rows(grad_keys, key_weight)
         + dot_rows(grad_values, value_weight)
     )
     grad_tokens = grad_res_one + tensor_sum(input_part)
-    down_share, up_share = dp_share([grad_down_weight, grad_up_weight])
-    query_share, key_share, value_share, out_share = dp_share(
-        [grad_query_weight, grad_key_weight, grad_value_weight, grad_out_weight]
-    )
     rows = [
         grad_query_bias,
         grad_value_bias,
@@ -277,11 +309,14 @@
         grad_gain_second,
         grad_shift_second,
     ]
-    sums, start = [], 0
-    total = dp_sum(jnp.concatenate(rows))
-    for row in rows:
-        sums.append(total[start : start + row.shape[0]])
-        start += row.shape[0]
+    width = max(row.shape[0] for row in rows)
+    line = lax.broadcasted_iota(jnp.int32, (len(rows), width), 0)
+    stacked = jnp.zeros((len(rows), width), jnp.float32)
+    for index, row in enumerate(rows):
+        padded = jnp.pad(row, (0, width - row.shape[0]))
+        stacked = jnp.where(line == index, padded[None, :], stacked)
+    total = dp_sum(stacked)
+    sums = [total[index, : row.shape[0]] for index, row in enumerate(rows)]
     (
         query_bias_sum,
         value_bias_sum,

time: 278 us -> 232 us (0.83)
  waiting for transfers between devices: 177 us -> 123 us
  starting transfers between devices: 11.5 us -> 33.5 us
  between operations: 14.6 us -> 2.04 us
  local copies, waits for them, and re-layouts: 29 us -> 18.5 us
  matrix products: 25.4 us -> 34.1 us
    reduce_scatter x1 -> x0, waiting for transfers between devices: 113 us -> none  [dp_share(): lax.psum_scatter(jnp.concatenate(parts, axis=1), 'dp', scatter_dimension=...]
    ppermute x0 -> x32, waiting for transfers between devices: none -> 98.8 us  [dp_share(): got = lax.ppermute(send, 'dp', [(i, i ^ 1 << bit) for i in range(size)])]
    unnamed x3 -> x0, waiting for transfers between devices: 26.8 us -> none
    ppermute x0 -> x32, starting transfers between devices: none -> 20.7 us  [dp_share(): got = lax.ppermute(send, 'dp', [(i, i ^ 1 << bit) for i in range(size)])]
    unnamed x89 -> x151, local copies, waits for them, and re-layouts: 18.2 us -> 2.98 us
    ppermute x4, waiting for transfers between devices: 27.6 us -> 15.2 us  [tensor_sum(): return part + lax.ppermute(part, 'tensor', [(0, 1), (1, 0)])]
    dot_general x6 -> x16, matrix products: 6 us -> 17.6 us  [dp_share(): jnp.dot(half.reshape(-1, tokens), right, preferred_element_type=jnp.float32)]
    concatenate x2, other arithmetic: 9.66 us -> 1.47 us  [dp_share_halves(): jnp.concatenate([dp_share(left, right[:, :middle], upward), dp_share(left...]
  transfers between devices with their start and end apart: 10 -> 40, of which waited for: 10 -> 21; matrix products, arithmetic and copies ran while one was open for 13% -> 23% of each run, Pallas kernels for 0% -> 0%
where the time goes in v2:
time: 232 us; the launch traced here: 231 us
  waiting for transfers between devices  123 us (53%)
  matrix products  34.1 us (15%)
  starting transfers between devices  33.5 us (14%)
  other arithmetic  20.4 us (9%)
  local copies, waits for them, and re-layouts  18.5 us (8%)
    ppermute x32, waiting for transfers between devices, dp_share(): got = lax.ppermute(send, 'dp', [(i, i ^ 1 << bit) for i in range(size)])  98.8 us
    ppermute x32, starting transfers between devices, dp_share(): got = lax.ppermute(send, 'dp', [(i, i ^ 1 << bit) for i in range(size)])  20.7 us
    dot_general x16, matrix products, dp_share(): jnp.dot(half.reshape(-1, tokens), right, preferred_element_type=jnp.float32)  17.6 us
    ppermute x4, waiting for transfers between devices, tensor_sum(): return part + lax.ppermute(part, 'tensor', [(0, 1), (1, 0)])  15.2 us
    ppermute x4, waiting for transfers between devices, dp_sum(): part = part + lax.ppermute(part, 'dp', [(i, i ^ step) for i in range(size)])  8.92 us
    ppermute x4, starting transfers between devices, tensor_sum(): return part + lax.ppermute(part, 'tensor', [(0, 1), (1, 0)])  6.86 us
    ppermute x4, starting transfers between devices, dp_sum(): part = part + lax.ppermute(part, 'dp', [(i, i ^ step) for i in range(size)])  5.87 us
    pad x8, local copies, waits for them, and re-layouts, local(): padded = jnp.pad(row, (0, width - row.shape[0]))  5.29 us
  transfers between devices with their start and end apart: 40, of which 21 were waited for; matrix products, arithmetic and copies ran while one was open for 23% of the time, Pallas kernels for 0%

profile of v2, /device:TPU:0, one launch (start us, length us, event | category | flops | bytes accessed | tf_op | source)
XLA Modules:
  0.0 231.4 jit_solution(6107727806066722010)
XLA Ops:
  0.7 1.5 fusion.1
  3.2 0.9 fusion.2
  4.3 1.4 convolution_convert_fusion.1
  7.5 3.0 %collective-permute-start = (f32[128,768]{1,0:T(8,128)S(1)}, f32[128,768]{1,0:T(8,128)}, u32[]{:S(2)}, u32[]{:S(2)}) collective-permute-start(f32[128,768]{1,0:T(8,128)S(1)} %fusion.95), channel_id=1, source_target_pairs={{0,1},{1,0},{2,3},{3,2},{4,5},{5,4},{6,7},{7,6},{8,9},{9,8},{10,11... | collective-permute-start | bytes 1179656 | tf_op jit(solution)/shard_map/ppermute | solution.py:31
  14.2 5.6 %collective-permute-done = f32[128,768]{1,0:T(8,128)} collective-permute-done((f32[128,768]{1,0:T(8,128)S(1)}, f32[128,768]{1,0:T(8,128)}, u32[]{:S(2)}, u32[]{:S(2)}) %collective-permute-start) | collective-permute-done | bytes 393248 | tf_op jit(solution)/shard_map/ppermute | solution.py:31
  19.8 1.3 fusion.94
  21.3 2.9 %fusion.7 = (bf16[128,1536]{1,0:T(8,128)(2,1)S(1)}, f32[128,1536]{1,0:T(8,128)S(1)}) fusion(f32[1536]{0:T(1024)} %param.30, bf16[768,1536]{1,0:T(8,128)(2,1)S(1)} %copy-done, f32[128,768]{1,0:T(8,128)S(1)} %get-tuple-element.98, f32[768]{0:T(1024)} %param.28, f32[768]{0:T(1024)} %param.27, f32[128]{0:T(128)S(1)} %add_rsqrt_fusion.1, ...), kind=kOutput, calls=%fused_computation.30 | convolution fusion | flops 315457536 | bytes 3945472 | tf_op jit(solution)/shard_map/dot_general | solution.py:255
  25.2 1.8 collective-permute-start.1
  27.6 7.9 %collective-permute-done.1 = f32[128,768]{1,0:T(8,128)S(1)} collective-permute-done((f32[128,768]{1,0:T(8,128)S(1)}, f32[128,768]{1,0:T(8,128)S(1)}, u32[]{:S(2)}, u32[]{:S(2)}) %collective-permute-start.1) | collective-permute-done | bytes 393248 | tf_op jit(solution)/shard_map/ppermute | solution.py:31
  37.0 1.0 convert_bitcast_fusion.1
  38.0 1.3 convert_reduce_fusion
  39.3 1.7 fusion.97
  41.0 1.4 collective-permute-start.2
  43.6 1.7 copy.81
  45.3 2.3 fusion.31
  47.6 1.7 copy.82
  49.4 2.4 %fusion.30 = f32[2,2,2,48,768]{4,3,2,1,0:T(8,128)} fusion(bf16[128,1536]{1,0:T(8,128)(2,1)} %copy-done.2, bf16[2,2,2,2,48,128]{5,4,3,2,1,0:T(8,128)(2,1)} %bitcast.252, s32[]{:T(128)S(6)} %select_n.140), kind=kOutput, calls=%fused_computation.119 | convolution fusion | flops 75497472 | bytes 1474564 | tf_op jit(solution)/shard_map/dot_general | solution.py:64
  51.8 1.3 fusion.33
  53.1 2.0 multiply_reduce_fusion
  57.1 1.0 multiply_reduce_fusion.2
  60.2 0.9 convert_reduce_fusion.4
  62.2 1.1 convolution_add_fusion.9
  63.9 1.3 fusion.32
  65.3 1.1 fusion.49
  66.6 1.3 reduce_sum.197
  68.0 1.3 pad.33
  69.3 1.3 reduce_sum.195
  73.5 1.7 collective-permute-done.3
  75.2 1.9 convert_reduce_fusion.1
  77.4 1.1 fusion.47
  79.8 1.5 collective-permute-start.17
  81.3 1.1 fusion.45
  82.4 1.1 copy.78
  83.5 1.4 collective-permute-done.17
  84.9 1.1 fusion.138
  86.0 1.7 collective-permute-start.18
  87.9 2.8 %collective-permute-done.18 = f32[9,1536]{1,0:T(8,128)S(1)} collective-permute-done((f32[9,1536]{1,0:T(8,128)S(1)}, f32[9,1536]{1,0:T(8,128)S(1)}, u32[]{:S(2)}, u32[]{:S(2)}) %collective-permute-start.18) | collective-permute-done | bytes 55328 | tf_op jit(solution)/shard_map/ppermute | solution.py:40
  91.3 1.3 convolution_add_fusion.8
  93.0 1.3 convolution_add_fusion.7
  94.8 1.3 convolution_add_fusion.6
  96.2 2.7 %collective-permute-start.19 = (f32[9,1536]{1,0:T(8,128)S(1)}, f32[9,1536]{1,0:T(8,128)S(1)}, u32[]{:S(2)}, u32[]{:S(2)}) collective-permute-start(f32[9,1536]{1,0:T(8,128)S(1)} %add.396), channel_id=1, source_target_pairs={{0,16},{2,18},{4,20},{6,22},{8,24},{10,26},{12,28},{14,30},{16,0},... | collective-permute-start | bytes 165896 | tf_op jit(solution)/shard_map/ppermute | solution.py:40
  99.3 4.8 %collective-permute-done.19 = f32[9,1536]{1,0:T(8,128)S(1)} collective-permute-done((f32[9,1536]{1,0:T(8,128)S(1)}, f32[9,1536]{1,0:T(8,128)S(1)}, u32[]{:S(2)}, u32[]{:S(2)}) %collective-permute-start.19) | collective-permute-done | bytes 55328 | tf_op jit(solution)/shard_map/ppermute | solution.py:40
  104.1 1.5 collective-permute-start.5
  108.1 1.6 convolution_add_fusion.3
  109.7 1.4 collective-permute-start.13
  113.6 1.6 collective-permute-start.25
  115.2 2.1 collective-permute-done.9
  118.1 5.6 %collective-permute-done.13 = f32[2,2,48,384]{3,2,1,0:T(8,128)S(1)} collective-permute-done((f32[2,2,48,384]{3,2,1,0:T(8,128)S(1)}, f32[2,2,48,384]{3,2,1,0:T(8,128)S(1)}, u32[]{:S(2)}, u32[]{:S(2)}) %collective-permute-start.13) | collective-permute-done | bytes 294944 | tf_op jit(solution)/shard_map/ppermute | solution.py:69
  125.1 25.0 %collective-permute-done.6 = f32[2,48,384]{2,1,0:T(8,128)S(1)} collective-permute-done((f32[2,48,384]{2,1,0:T(8,128)S(1)}, f32[2,48,384]{2,1,0:T(8,128)S(1)}, u32[]{:S(2)}, u32[]{:S(2)}) %collective-permute-start.6) | collective-permute-done | bytes 147488 | tf_op jit(solution)/shard_map/ppermute | solution.py:69
  150.1 3.1 %collective-permute-start.10 = (f32[2,48,384]{2,1,0:T(8,128)S(1)}, f32[2,48,384]{2,1,0:T(8,128)S(1)}, u32[]{:S(2)}, u32[]{:S(2)}) collective-permute-start(f32[2,48,384]{2,1,0:T(8,128)S(1)} %dynamic-slice_bitcast_fusion.18), channel_id=1, source_target_pairs={{0,16},{2,18},{4,20},{6,22},{8,24},{10,26},{12,28},{14,30},{16,0},... | collective-permute-start | bytes 442376 | tf_op jit(solution)/shard_map/ppermute | solution.py:69
  153.2 6.3 %collective-permute-done.10 = f32[2,48,384]{2,1,0:T(8,128)S(1)} collective-permute-done((f32[2,48,384]{2,1,0:T(8,128)S(1)}, f32[2,48,384]{2,1,0:T(8,128)S(1)}, u32[]{:S(2)}, u32[]{:S(2)}) %collective-permute-start.10) | collective-permute-done | bytes 147488 | tf_op jit(solution)/shard_map/ppermute | solution.py:69
  159.6 9.0 %collective-permute-done.14 = f32[2,48,384]{2,1,0:T(8,128)S(1)} collective-permute-done((f32[2,48,384]{2,1,0:T(8,128)S(1)}, f32[2,48,384]{2,1,0:T(8,128)S(1)}, u32[]{:S(2)}, u32[]{:S(2)}) %collective-permute-start.14) | collective-permute-done | bytes 147488 | tf_op jit(solution)/shard_map/ppermute | solution.py:69
  168.6 5.6 %collective-permute-done.22 = f32[2,48,384]{2,1,0:T(8,128)S(1)} collective-permute-done((f32[2,48,384]{2,1,0:T(8,128)S(1)}, f32[2,48,384]{2,1,0:T(8,128)S(1)}, u32[]{:S(2)}, u32[]{:S(2)}) %collective-permute-start.22) | collective-permute-done | bytes 147488 | tf_op jit(solution)/shard_map/ppermute | solution.py:69
  174.2 5.2 %collective-permute-done.7 = f32[48,384]{1,0:T(8,128)S(1)} collective-permute-done((f32[48,384]{1,0:T(8,128)S(1)}, f32[48,384]{1,0:T(8,128)S(1)}, u32[]{:S(2)}, u32[]{:S(2)}) %collective-permute-start.7) | collective-permute-done | bytes 73760 | tf_op jit(solution)/shard_map/ppermute | solution.py:69
  180.6 3.2 %collective-permute-done.11 = f32[48,384]{1,0:T(8,128)S(1)} collective-permute-done((f32[48,384]{1,0:T(8,128)S(1)}, f32[48,384]{1,0:T(8,128)S(1)}, u32[]{:S(2)}, u32[]{:S(2)}) %collective-permute-start.11) | collective-permute-done | bytes 73760 | tf_op jit(solution)/shard_map/ppermute | solution.py:69
  185.0 3.2 %collective-permute-done.15 = f32[48,384]{1,0:T(8,128)S(1)} collective-permute-done((f32[48,384]{1,0:T(8,128)S(1)}, f32[48,384]{1,0:T(8,128)S(1)}, u32[]{:S(2)}, u32[]{:S(2)}) %collective-permute-start.15) | collective-permute-done | bytes 73760 | tf_op jit(solution)/shard_map/ppermute | solution.py:69
  188.9 6.7 %collective-permute-done.23 = f32[48,384]{1,0:T(8,128)S(1)} collective-permute-done((f32[48,384]{1,0:T(8,128)S(1)}, f32[48,384]{1,0:T(8,128)S(1)}, u32[]{:S(2)}, u32[]{:S(2)}) %collective-permute-start.23) | collective-permute-done | bytes 73760 | tf_op jit(solution)/shard_map/ppermute | solution.py:69
  196.6 2.4 %collective-permute-start.26 = (f32[2,48,768]{2,1,0:T(8,128)S(1)}, f32[2,48,768]{2,1,0:T(8,128)S(1)}, u32[]{:S(2)}, u32[]{:S(2)}) collective-permute-start(f32[2,48,768]{2,1,0:T(8,128)S(1)} %dynamic-slice_bitcast_fusion.7), channel_id=1, source_target_pairs={{0,8},{2,10},{4,12},{6,14},{8,0},{10,2},{12,4},{14,6},{16,24},{18,... | collective-permute-start | bytes 884744 | tf_op jit(solution)/shard_map/ppermute | solution.py:69
  199.8 2.1 collective-permute-start.34
  201.9 12.7 %collective-permute-done.30 = f32[2,48,768]{2,1,0:T(8,128)S(1)} collective-permute-done((f32[2,48,768]{2,1,0:T(8,128)S(1)}, f32[2,48,768]{2,1,0:T(8,128)S(1)}, u32[]{:S(2)}, u32[]{:S(2)}) %collective-permute-start.30) | collective-permute-done | bytes 294944 | tf_op jit(solution)/shard_map/ppermute | solution.py:69
  215.5 8.5 %collective-permute-done.38 = f32[2,48,768]{2,1,0:T(8,128)S(1)} collective-permute-done((f32[2,48,768]{2,1,0:T(8,128)S(1)}, f32[2,48,768]{2,1,0:T(8,128)S(1)}, u32[]{:S(2)}, u32[]{:S(2)}) %collective-permute-start.38) | collective-permute-done | bytes 294944 | tf_op jit(solution)/shard_map/ppermute | solution.py:69
  224.3 2.0 collective-permute-done.27
  227.0 2.2 collective-permute-done.39
  229.2 1.4 collective-permute-done.35
  (302 shorter events, 37.8 us)
Async XLA Ops:
  0.7 20.6 %copy-start = (bf16[768,1536]{1,0:T(8,128)(2,1)S(1)}, bf16[768,1536]{1,0:T(8,128)(2,1)}, u32[]{:S(2)}) copy-start(bf16[768,1536]{1,0:T(8,128)(2,1)} %param.29) | copy-start | bytes 7077892
  6.8 14.2 %copy-start.30 = (bf16[6,64,128]{2,1,0:T(8,128)(2,1)}, bf16[6,64,128]{2,1,0:T(8,128)(2,1)S(1)}, u32[]{:S(2)}) copy-start(bf16[6,64,128]{2,1,0:T(8,128)(2,1)S(1)} %convolution_convert_fusion.3) | copy-start | bytes 294916
  7.1 12.6 %copy-start.70 = (f32[768]{0:T(1024)S(1)}, f32[768]{0:T(1024)}, u32[]{:S(2)}) copy-start(f32[768]{0:T(1024)} %param.26) | copy-start | bytes 9220
  7.5 6.7 %copy-start.20 = (f32[128,768]{1,0:T(8,128)}, f32[128,768]{1,0:T(8,128)S(1)}, u32[]{:S(2)}) copy-start(f32[128,768]{1,0:T(8,128)S(1)} %fusion.95) | copy-start | bytes 1179652
  7.5 12.3 %collective-permute-start = (f32[128,768]{1,0:T(8,128)S(1)}, f32[128,768]{1,0:T(8,128)}, u32[]{:S(2)}, u32[]{:S(2)}) collective-permute-start(f32[128,768]{1,0:T(8,128)S(1)} %fusion.95), channel_id=1, source_target_pairs={{0,1},{1,0},{2,3},{3,2},{4,5},{5,4},{6,7},{7,6},{8,9},{9,8},{10,11... | collective-permute-start | bytes 1179656 | tf_op jit(solution)/shard_map/ppermute | solution.py:31
  21.0 14.5 %copy-start.57 = (f32[128]{0:T(128)}, f32[128]{0:T(128)S(1)}, u32[]{:S(2)}) copy-start(f32[128]{0:T(128)S(1)} %broadcast_multiply_fusion.5) | copy-start | bytes 1540
  21.3 14.3 %copy-start.68 = (f32[128]{0:T(128)}, f32[128]{0:T(128)S(1)}, u32[]{:S(2)}) copy-start(f32[128]{0:T(128)S(1)} %add_rsqrt_fusion.1) | copy-start | bytes 1540
  24.3 11.3 %copy-start.50 = (f32[768]{0:T(1024)S(1)}, f32[768]{0:T(1024)}, u32[]{:S(2)}) copy-start(f32[768]{0:T(1024)} %param.27) | copy-start | bytes 9220
  24.3 11.3 %copy-start.71 = (f32[768]{0:T(1024)S(1)}, f32[768]{0:T(1024)}, u32[]{:S(2)}) copy-start(f32[768]{0:T(1024)} %param.32) | copy-start | bytes 9220
  24.3 11.3 %copy-start.72 = (f32[768]{0:T(1024)S(1)}, f32[768]{0:T(1024)}, u32[]{:S(2)}) copy-start(f32[768]{0:T(1024)} %param.28) | copy-start | bytes 9220
  25.2 11.5 %copy-start.36 = (bf16[128,768]{1,0:T(8,128)(2,1)S(1)}, bf16[128,768]{1,0:T(8,128)(2,1)}, u32[]{:S(2)}) copy-start(bf16[128,768]{1,0:T(8,128)(2,1)} %param.35) | copy-start | bytes 589828
  25.2 11.5 %copy-start.54 = (f32[768]{0:T(1024)S(1)}, f32[768]{0:T(1024)}, u32[]{:S(2)}) copy-start(f32[768]{0:T(1024)} %param.33) | copy-start | bytes 9220
  25.2 10.4 %collective-permute-start.1 = (f32[128,768]{1,0:T(8,128)S(1)}, f32[128,768]{1,0:T(8,128)S(1)}, u32[]{:S(2)}, u32[]{:S(2)}) collective-permute-start(f32[128,768]{1,0:T(8,128)S(1)} %fusion.96), channel_id=1, source_target_pairs={{0,1},{1,0},{2,3},{3,2},{4,5},{5,4},{6,7},{7,6},{8,9},{9,8},{10,11... | collective-permute-start | bytes 1179656 | tf_op jit(solution)/shard_map/ppermute | solution.py:31
  27.6 9.4 %copy-start.73 = (f32[768]{0:T(1024)S(1)}, f32[768]{0:T(1024)}, u32[]{:S(2)}) copy-start(f32[768]{0:T(1024)} %param.34) | copy-start | bytes 9220
  41.0 12.1 %collective-permute-start.2 = (f32[128,768]{1,0:T(8,128)}, f32[128,768]{1,0:T(8,128)}, u32[]{:S(2)}, u32[]{:S(2)}) collective-permute-start(f32[128,768]{1,0:T(8,128)} %fusion.97), channel_id=1, source_target_pairs={{0,1},{1,0},{2,3},{3,2},{4,5},{5,4},{6,7},{7,6},{8,9},{9,8},{10,11... | collective-permute-start | bytes 1179656 | tf_op jit(solution)/shard_map/ppermute | solution.py:31
  47.6 59.8 %collective-permute-start.28 = (f32[2,2,2,48,768]{4,3,2,1,0:T(8,128)}, f32[2,2,2,48,768]{4,3,2,1,0:T(8,128)}, u32[]{:S(2)}, u32[]{:S(2)}) collective-permute-start(f32[2,2,2,48,768]{4,3,2,1,0:T(8,128)} %fusion.31), channel_id=1, source_target_pairs={{0,2},{2,0},{4,6},{6,4},{8,10},{10,8},{12,14},{14,12},{16,18},{18,... | collective-permute-start | bytes 3538952 | tf_op jit(solution)/shard_map/ppermute | solution.py:69
  63.3 11.9 %copy-start.5 = (f32[128,768]{1,0:T(8,128)S(1)}, f32[128,768]{1,0:T(8,128)}, u32[]{:S(2)}) copy-start(f32[128,768]{1,0:T(8,128)} %copy-done.4) | copy-start | bytes 1179652
  63.3 11.8 %collective-permute-start.3 = (f32[128,768]{1,0:T(8,128)}, f32[128,768]{1,0:T(8,128)}, u32[]{:S(2)}, u32[]{:S(2)}) collective-permute-start(f32[128,768]{1,0:T(8,128)} %convolution_add_fusion.9), channel_id=1, source_target_pairs={{0,1},{1,0},{2,3},{3,2},{4,5},{5,4},{6,7},{7,6},{8,9},{9,8},{10,11... | collective-permute-start | bytes 1179656 | tf_op jit(solution)/shard_map/ppermute | solution.py:31
  65.3 11.8 %copy-start.40 = (f32[1536]{0:T(1024)S(1)}, f32[1536]{0:T(1024)}, u32[]{:S(2)}) copy-start(f32[1536]{0:T(1024)} %pad.27) | copy-start | bytes 18436
  65.3 11.8 %copy-start.41 = (f32[1536]{0:T(1024)S(1)}, f32[1536]{0:T(1024)}, u32[]{:S(2)}) copy-start(f32[1536]{0:T(1024)} %pad.26) | copy-start | bytes 18436
  66.4 24.3 %collective-permute-start.4 = (f32[2,2,2,48,384]{4,3,2,1,0:T(8,128)}, f32[2,2,2,48,384]{4,3,2,1,0:T(8,128)}, u32[]{:S(2)}, u32[]{:S(2)}) collective-permute-start(f32[2,2,2,48,384]{4,3,2,1,0:T(8,128)} %fusion.49), channel_id=1, source_target_pairs={{0,2},{2,0},{4,6},{6,4},{8,10},{10,8},{12,14},{14,12},{16,18},{18,... | collective-permute-start | bytes 1769480 | tf_op jit(solution)/shard_map/ppermute | solution.py:69
  70.6 6.6 %copy-start.61 = (pred[9]{0:T(512)(128)(4,1)S(1)}, pred[9]{0:T(512)(128)(4,1)}, u32[]{:S(2)}) copy-start(pred[9]{0:T(512)(128)(4,1)} %iota_compare_fusion.8) | copy-start | bytes 31
  70.7 6.8 %copy-start.22 = (bf16[6,64,128]{2,1,0:T(8,128)(2,1)S(1)}, bf16[6,64,128]{2,1,0:T(8,128)(2,1)}, u32[]{:S(2)}) copy-start(bf16[6,64,128]{2,1,0:T(8,128)(2,1)} %copy-done.21) | copy-start | bytes 294916
  71.4 7.7 %copy-start.43 = (f32[1536]{0:T(1024)}, f32[1536]{0:T(1024)S(1)}, u32[]{:S(2)}) copy-start(f32[1536]{0:T(1024)S(1)} %pad.32) | copy-start | bytes 18436
  72.1 7.0 %copy-start.44 = (f32[1536]{0:T(1024)}, f32[1536]{0:T(1024)S(1)}, u32[]{:S(2)}) copy-start(f32[1536]{0:T(1024)S(1)} %pad.30) | copy-start | bytes 18436
  73.5 7.8 %copy-start.18 = (bf16[6,64,128]{2,1,0:T(8,128)(2,1)S(1)}, bf16[6,64,128]{2,1,0:T(8,128)(2,1)}, u32[]{:S(2)}) copy-start(bf16[6,64,128]{2,1,0:T(8,128)(2,1)} %copy-done.17) | copy-start | bytes 294916
  77.3 1.7 collective-permute-start.16
  77.4 10.2 %copy-start.31 = (bf16[6,64,128]{2,1,0:T(8,128)(2,1)S(1)}, bf16[6,64,128]{2,1,0:T(8,128)(2,1)}, u32[]{:S(2)}) copy-start(bf16[6,64,128]{2,1,0:T(8,128)(2,1)} %copy-done.30) | copy-start | bytes 294916
  78.6 14.1 %collective-permute-start.8 = (f32[2,2,2,48,384]{4,3,2,1,0:T(8,128)}, f32[2,2,2,48,384]{4,3,2,1,0:T(8,128)}, u32[]{:S(2)}, u32[]{:S(2)}) collective-permute-start(f32[2,2,2,48,384]{4,3,2,1,0:T(8,128)} %fusion.47), channel_id=1, source_target_pairs={{0,2},{2,0},{4,6},{6,4},{8,10},{10,8},{12,14},{14,12},{16,18},{18,... | collective-permute-start | bytes 1769480 | tf_op jit(solution)/shard_map/ppermute | solution.py:69
  79.8 5.0 %collective-permute-start.17 = (f32[9,1536]{1,0:T(8,128)}, f32[9,1536]{1,0:T(8,128)}, u32[]{:S(2)}, u32[]{:S(2)}) collective-permute-start(f32[9,1536]{1,0:T(8,128)} %fusion.90), channel_id=1, source_target_pairs={{0,4},{2,6},{4,0},{6,2},{8,12},{10,14},{12,8},{14,10},{16,20},{18,... | collective-permute-start | bytes 165896 | tf_op jit(solution)/shard_map/ppermute | solution.py:40
  81.3 10.0 %copy-start.25 = (bf16[6,64,128]{2,1,0:T(8,128)(2,1)S(1)}, bf16[6,64,128]{2,1,0:T(8,128)(2,1)}, u32[]{:S(2)}) copy-start(bf16[6,64,128]{2,1,0:T(8,128)(2,1)} %copy-done.24) | copy-start | bytes 294916
  82.4 11.9 %collective-permute-start.12 = (f32[2,2,2,48,384]{4,3,2,1,0:T(8,128)}, f32[2,2,2,48,384]{4,3,2,1,0:T(8,128)}, u32[]{:S(2)}, u32[]{:S(2)}) collective-permute-start(f32[2,2,2,48,384]{4,3,2,1,0:T(8,128)} %fusion.45), channel_id=1, source_target_pairs={{0,2},{2,0},{4,6},{6,4},{8,10},{10,8},{12,14},{14,12},{16,18},{18,... | collective-permute-start | bytes 1769480 | tf_op jit(solution)/shard_map/ppermute | solution.py:69
  86.0 4.7 %collective-permute-start.18 = (f32[9,1536]{1,0:T(8,128)S(1)}, f32[9,1536]{1,0:T(8,128)S(1)}, u32[]{:S(2)}, u32[]{:S(2)}) collective-permute-start(f32[9,1536]{1,0:T(8,128)S(1)} %fusion.138), channel_id=1, source_target_pairs={{0,8},{2,10},{4,12},{6,14},{8,0},{10,2},{12,4},{14,6},{16,24},{18,... | collective-permute-start | bytes 165896 | tf_op jit(solution)/shard_map/ppermute | solution.py:40
  90.7 19.1 %collective-permute-start.24 = (f32[2,2,2,48,768]{4,3,2,1,0:T(8,128)}, f32[2,2,2,48,768]{4,3,2,1,0:T(8,128)S(1)}, u32[]{:S(2)}, u32[]{:S(2)}) collective-permute-start(f32[2,2,2,48,768]{4,3,2,1,0:T(8,128)} %fusion.30), channel_id=1, source_target_pairs={{0,2},{2,0},{4,6},{6,4},{8,10},{10,8},{12,14},{14,12},{16,18},{18,... | collective-permute-start | bytes 3538952 | tf_op jit(solution)/shard_map/ppermute | solution.py:69
  90.7 5.4 %collective-permute-start.20 = (f32[2,2,2,48,384]{4,3,2,1,0:T(8,128)S(1)}, f32[2,2,2,48,384]{4,3,2,1,0:T(8,128)S(1)}, u32[]{:S(2)}, u32[]{:S(2)}) collective-permute-start(f32[2,2,2,48,384]{4,3,2,1,0:T(8,128)S(1)} %fusion.42), channel_id=1, source_target_pairs={{0,2},{2,0},{4,6},{6,4},{8,10},{10,8},{12,14},{14,12},{16,18},{18,... | collective-permute-start | bytes 1769480 | tf_op jit(solution)/shard_map/ppermute | solution.py:69
  92.7 18.8 %collective-permute-start.36 = (f32[2,2,2,48,768]{4,3,2,1,0:T(8,128)S(1)}, f32[2,2,2,48,768]{4,3,2,1,0:T(8,128)S(1)}, u32[]{:S(2)}, u32[]{:S(2)}) collective-permute-start(f32[2,2,2,48,768]{4,3,2,1,0:T(8,128)S(1)} %copy-done.28), channel_id=1, source_target_pairs={{0,2},{2,0},{4,6},{6,4},{8,10},{10,8},{12,14},{14,12},{16,18},{18,... | collective-permute-start | bytes 3538952 | tf_op jit(solution)/shard_map/ppermute | solution.py:69
  94.4 18.0 %collective-permute-start.32 = (f32[2,2,2,48,768]{4,3,2,1,0:T(8,128)S(1)}, f32[2,2,2,48,768]{4,3,2,1,0:T(8,128)S(1)}, u32[]{:S(2)}, u32[]{:S(2)}) collective-permute-start(f32[2,2,2,48,768]{4,3,2,1,0:T(8,128)S(1)} %copy-done.29), channel_id=1, source_target_pairs={{0,2},{2,0},{4,6},{6,4},{8,10},{10,8},{12,14},{14,12},{16,18},{18,... | collective-permute-start | bytes 3538952 | tf_op jit(solution)/shard_map/ppermute | solution.py:69
  96.2 7.9 %collective-permute-start.19 = (f32[9,1536]{1,0:T(8,128)S(1)}, f32[9,1536]{1,0:T(8,128)S(1)}, u32[]{:S(2)}, u32[]{:S(2)}) collective-permute-start(f32[9,1536]{1,0:T(8,128)S(1)} %add.396), channel_id=1, source_target_pairs={{0,16},{2,18},{4,20},{6,22},{8,24},{10,26},{12,28},{14,30},{16,0},... | collective-permute-start | bytes 165896 | tf_op jit(solution)/shard_map/ppermute | solution.py:40
  99.1 9.0 %copy-start.3 = (bf16[128,1536]{1,0:T(8,128)(2,1)S(1)}, bf16[128,1536]{1,0:T(8,128)(2,1)}, u32[]{:S(2)}) copy-start(bf16[128,1536]{1,0:T(8,128)(2,1)} %copy-done.2) | copy-start | bytes 1179652
  99.1 9.0 %copy-start.16 = (bf16[768,128]{1,0:T(8,128)(2,1)S(1)}, bf16[768,128]{1,0:T(8,128)(2,1)}, u32[]{:S(2)}) copy-start(bf16[768,128]{1,0:T(8,128)(2,1)} %copy.81) | copy-start | bytes 589828
  104.1 9.5 %collective-permute-start.5 = (f32[2,2,48,384]{3,2,1,0:T(8,128)S(1)}, f32[2,2,48,384]{3,2,1,0:T(8,128)S(1)}, u32[]{:S(2)}, u32[]{:S(2)}) collective-permute-start(f32[2,2,48,384]{3,2,1,0:T(8,128)S(1)} %dynamic-slice_bitcast_fusion.11), channel_id=1, source_target_pairs={{0,4},{2,6},{4,0},{6,2},{8,12},{10,14},{12,8},{14,10},{16,20},{18,... | collective-permute-start | bytes 884744 | tf_op jit(solution)/shard_map/ppermute | solution.py:69
  107.4 9.9 %collective-permute-start.9 = (f32[2,2,48,384]{3,2,1,0:T(8,128)S(1)}, f32[2,2,48,384]{3,2,1,0:T(8,128)S(1)}, u32[]{:S(2)}, u32[]{:S(2)}) collective-permute-start(f32[2,2,48,384]{3,2,1,0:T(8,128)S(1)} %dynamic-slice_bitcast_fusion.10), channel_id=1, source_target_pairs={{0,8},{2,10},{4,12},{6,14},{8,0},{10,2},{12,4},{14,6},{16,24},{18,... | collective-permute-start | bytes 884744 | tf_op jit(solution)/shard_map/ppermute | solution.py:69
  109.7 13.9 %collective-permute-start.13 = (f32[2,2,48,384]{3,2,1,0:T(8,128)S(1)}, f32[2,2,48,384]{3,2,1,0:T(8,128)S(1)}, u32[]{:S(2)}, u32[]{:S(2)}) collective-permute-start(f32[2,2,48,384]{3,2,1,0:T(8,128)S(1)} %dynamic-slice_bitcast_fusion.9), channel_id=1, source_target_pairs={{0,8},{2,10},{4,12},{6,14},{8,0},{10,2},{12,4},{14,6},{16,24},{18,... | collective-permute-start | bytes 884744 | tf_op jit(solution)/shard_map/ppermute | solution.py:69
  111.5 12.8 %collective-permute-start.21 = (f32[2,2,48,384]{3,2,1,0:T(8,128)S(1)}, f32[2,2,48,384]{3,2,1,0:T(8,128)S(1)}, u32[]{:S(2)}, u32[]{:S(2)}) collective-permute-start(f32[2,2,48,384]{3,2,1,0:T(8,128)S(1)} %dynamic-slice_bitcast_fusion.8), channel_id=1, source_target_pairs={{0,4},{2,6},{4,0},{6,2},{8,12},{10,14},{12,8},{14,10},{16,20},{18,... | collective-permute-start | bytes 884744 | tf_op jit(solution)/shard_map/ppermute | solution.py:69
  112.4 83.9 %collective-permute-start.29 = (f32[2,2,48,768]{3,2,1,0:T(8,128)S(1)}, f32[2,2,48,768]{3,2,1,0:T(8,128)S(1)}, u32[]{:S(2)}, u32[]{:S(2)}) collective-permute-start(f32[2,2,48,768]{3,2,1,0:T(8,128)S(1)} %dynamic-slice_bitcast_fusion.2), channel_id=1, source_target_pairs={{0,8},{2,10},{4,12},{6,14},{8,0},{10,2},{12,4},{14,6},{16,24},{18,... | collective-permute-start | bytes 1769480 | tf_op jit(solution)/shard_map/ppermute | solution.py:69
  113.6 82.8 %collective-permute-start.25 = (f32[2,2,48,768]{3,2,1,0:T(8,128)S(1)}, f32[2,2,48,768]{3,2,1,0:T(8,128)S(1)}, u32[]{:S(2)}, u32[]{:S(2)}) collective-permute-start(f32[2,2,48,768]{3,2,1,0:T(8,128)S(1)} %dynamic-slice_bitcast_fusion.3), channel_id=1, source_target_pairs={{0,4},{2,6},{4,0},{6,2},{8,12},{10,14},{12,8},{14,10},{16,20},{18,... | collective-permute-start | bytes 1769480 | tf_op jit(solution)/shard_map/ppermute | solution.py:69
  117.4 81.6 %collective-permute-start.37 = (f32[2,2,48,768]{3,2,1,0:T(8,128)S(1)}, f32[2,2,48,768]{3,2,1,0:T(8,128)S(1)}, u32[]{:S(2)}, u32[]{:S(2)}) collective-permute-start(f32[2,2,48,768]{3,2,1,0:T(8,128)S(1)} %dynamic-slice_bitcast_fusion), channel_id=1, source_target_pairs={{0,8},{2,10},{4,12},{6,14},{8,0},{10,2},{12,4},{14,6},{16,24},{18,... | collective-permute-start | bytes 1769480 | tf_op jit(solution)/shard_map/ppermute | solution.py:69
  123.7 76.0 %collective-permute-start.33 = (f32[2,2,48,768]{3,2,1,0:T(8,128)S(1)}, f32[2,2,48,768]{3,2,1,0:T(8,128)S(1)}, u32[]{:S(2)}, u32[]{:S(2)}) collective-permute-start(f32[2,2,48,768]{3,2,1,0:T(8,128)S(1)} %dynamic-slice_bitcast_fusion.1), channel_id=1, source_target_pairs={{0,4},{2,6},{4,0},{6,2},{8,12},{10,14},{12,8},{14,10},{16,20},{18,... | collective-permute-start | bytes 1769480 | tf_op jit(solution)/shard_map/ppermute | solution.py:69
  124.3 25.8 %collective-permute-start.6 = (f32[2,48,384]{2,1,0:T(8,128)S(1)}, f32[2,48,384]{2,1,0:T(8,128)S(1)}, u32[]{:S(2)}, u32[]{:S(2)}) collective-permute-start(f32[2,48,384]{2,1,0:T(8,128)S(1)} %dynamic-slice_bitcast_fusion.19), channel_id=1, source_target_pairs={{0,8},{2,10},{4,12},{6,14},{8,0},{10,2},{12,4},{14,6},{16,24},{18,... | collective-permute-start | bytes 442376 | tf_op jit(solution)/shard_map/ppermute | solution.py:69
  150.1 9.4 %collective-permute-start.10 = (f32[2,48,384]{2,1,0:T(8,128)S(1)}, f32[2,48,384]{2,1,0:T(8,128)S(1)}, u32[]{:S(2)}, u32[]{:S(2)}) collective-permute-start(f32[2,48,384]{2,1,0:T(8,128)S(1)} %dynamic-slice_bitcast_fusion.18), channel_id=1, source_target_pairs={{0,16},{2,18},{4,20},{6,22},{8,24},{10,26},{12,28},{14,30},{16,0},... | collective-permute-start | bytes 442376 | tf_op jit(solution)/shard_map/ppermute | solution.py:69
  159.5 9.0 %collective-permute-start.14 = (f32[2,48,384]{2,1,0:T(8,128)S(1)}, f32[2,48,384]{2,1,0:T(8,128)S(1)}, u32[]{:S(2)}, u32[]{:S(2)}) collective-permute-start(f32[2,48,384]{2,1,0:T(8,128)S(1)} %dynamic-slice_bitcast_fusion.17), channel_id=1, source_target_pairs={{0,16},{2,18},{4,20},{6,22},{8,24},{10,26},{12,28},{14,30},{16,0},... | collective-permute-start | bytes 442376 | tf_op jit(solution)/shard_map/ppermute | solution.py:69
  168.6 5.6 %collective-permute-start.22 = (f32[2,48,384]{2,1,0:T(8,128)S(1)}, f32[2,48,384]{2,1,0:T(8,128)S(1)}, u32[]{:S(2)}, u32[]{:S(2)}) collective-permute-start(f32[2,48,384]{2,1,0:T(8,128)S(1)} %dynamic-slice_bitcast_fusion.16), channel_id=1, source_target_pairs={{0,8},{2,10},{4,12},{6,14},{8,0},{10,2},{12,4},{14,6},{16,24},{18,... | collective-permute-start | bytes 442376 | tf_op jit(solution)/shard_map/ppermute | solution.py:69
  174.2 5.3 %collective-permute-start.7 = (f32[48,384]{1,0:T(8,128)S(1)}, f32[48,384]{1,0:T(8,128)S(1)}, u32[]{:S(2)}, u32[]{:S(2)}) collective-permute-start(f32[48,384]{1,0:T(8,128)S(1)} %dynamic-slice_bitcast_fusion.23), channel_id=1, source_target_pairs={{0,16},{2,18},{4,20},{6,22},{8,24},{10,26},{12,28},{14,30},{16,0},... | collective-permute-start | bytes 221192 | tf_op jit(solution)/shard_map/ppermute | solution.py:69
  179.5 4.4 %collective-permute-start.11 = (f32[48,384]{1,0:T(8,128)S(1)}, f32[48,384]{1,0:T(8,128)S(1)}, u32[]{:S(2)}, u32[]{:S(2)}) collective-permute-start(f32[48,384]{1,0:T(8,128)S(1)} %dynamic-slice_bitcast_fusion.22), channel_id=1, source_target_pairs={{0,4},{2,6},{4,0},{6,2},{8,12},{10,14},{12,8},{14,10},{16,20},{18,... | collective-permute-start | bytes 221192 | tf_op jit(solution)/shard_map/ppermute | solution.py:69
  183.8 4.4 %collective-permute-start.15 = (f32[48,384]{1,0:T(8,128)S(1)}, f32[48,384]{1,0:T(8,128)S(1)}, u32[]{:S(2)}, u32[]{:S(2)}) collective-permute-start(f32[48,384]{1,0:T(8,128)S(1)} %dynamic-slice_bitcast_fusion.21), channel_id=1, source_target_pairs={{0,4},{2,6},{4,0},{6,2},{8,12},{10,14},{12,8},{14,10},{16,20},{18,... | collective-permute-start | bytes 221192 | tf_op jit(solution)/shard_map/ppermute | solution.py:69
  188.2 7.5 %collective-permute-start.23 = (f32[48,384]{1,0:T(8,128)S(1)}, f32[48,384]{1,0:T(8,128)S(1)}, u32[]{:S(2)}, u32[]{:S(2)}) collective-permute-start(f32[48,384]{1,0:T(8,128)S(1)} %dynamic-slice_bitcast_fusion.20), channel_id=1, source_target_pairs={{0,16},{2,18},{4,20},{6,22},{8,24},{10,26},{12,28},{14,30},{16,0},... | collective-permute-start | bytes 221192 | tf_op jit(solution)/shard_map/ppermute | solution.py:69
  196.4 18.3 %collective-permute-start.30 = (f32[2,48,768]{2,1,0:T(8,128)S(1)}, f32[2,48,768]{2,1,0:T(8,128)S(1)}, u32[]{:S(2)}, u32[]{:S(2)}) collective-permute-start(f32[2,48,768]{2,1,0:T(8,128)S(1)} %dynamic-slice_bitcast_fusion.6), channel_id=1, source_target_pairs={{0,16},{2,18},{4,20},{6,22},{8,24},{10,26},{12,28},{14,30},{16,0},... | collective-permute-start | bytes 884744 | tf_op jit(solution)/shard_map/ppermute | solution.py:69
  196.6 18.8 %collective-permute-start.26 = (f32[2,48,768]{2,1,0:T(8,128)S(1)}, f32[2,48,768]{2,1,0:T(8,128)S(1)}, u32[]{:S(2)}, u32[]{:S(2)}) collective-permute-start(f32[2,48,768]{2,1,0:T(8,128)S(1)} %dynamic-slice_bitcast_fusion.7), channel_id=1, source_target_pairs={{0,8},{2,10},{4,12},{6,14},{8,0},{10,2},{12,4},{14,6},{16,24},{18,... | collective-permute-start | bytes 884744 | tf_op jit(solution)/shard_map/ppermute | solution.py:69
  199.1 24.9 %collective-permute-start.38 = (f32[2,48,768]{2,1,0:T(8,128)S(1)}, f32[2,48,768]{2,1,0:T(8,128)S(1)}, u32[]{:S(2)}, u32[]{:S(2)}) collective-permute-start(f32[2,48,768]{2,1,0:T(8,128)S(1)} %dynamic-slice_bitcast_fusion.4), channel_id=1, source_target_pairs={{0,16},{2,18},{4,20},{6,22},{8,24},{10,26},{12,28},{14,30},{16,0},... | collective-permute-start | bytes 884744 | tf_op jit(solution)/shard_map/ppermute | solution.py:69
  199.8 24.3 %collective-permute-start.34 = (f32[2,48,768]{2,1,0:T(8,128)S(1)}, f32[2,48,768]{2,1,0:T(8,128)S(1)}, u32[]{:S(2)}, u32[]{:S(2)}) collective-permute-start(f32[2,48,768]{2,1,0:T(8,128)S(1)} %dynamic-slice_bitcast_fusion.5), channel_id=1, source_target_pairs={{0,8},{2,10},{4,12},{6,14},{8,0},{10,2},{12,4},{14,6},{16,24},{18,... | collective-permute-start | bytes 884744 | tf_op jit(solution)/shard_map/ppermute | solution.py:69
  214.7 9.5 %collective-permute-start.31 = (f32[48,768]{1,0:T(8,128)S(1)}, f32[48,768]{1,0:T(8,128)S(1)}, u32[]{:S(2)}, u32[]{:S(2)}) collective-permute-start(f32[48,768]{1,0:T(8,128)S(1)} %dynamic-slice_bitcast_fusion.14), channel_id=1, source_target_pairs={{0,4},{2,6},{4,0},{6,2},{8,12},{10,14},{12,8},{14,10},{16,20},{18,... | collective-permute-start | bytes 442376 | tf_op jit(solution)/shard_map/ppermute | solution.py:69
  215.4 10.9 %collective-permute-start.27 = (f32[48,768]{1,0:T(8,128)S(1)}, f32[48,768]{1,0:T(8,128)S(1)}, u32[]{:S(2)}, u32[]{:S(2)}) collective-permute-start(f32[48,768]{1,0:T(8,128)S(1)} %dynamic-slice_bitcast_fusion.15), channel_id=1, source_target_pairs={{0,16},{2,18},{4,20},{6,22},{8,24},{10,26},{12,28},{14,30},{16,0},... | collective-permute-start | bytes 442376 | tf_op jit(solution)/shard_map/ppermute | solution.py:69
  224.0 5.2 %collective-permute-start.39 = (f32[48,768]{1,0:T(8,128)S(1)}, f32[48,768]{1,0:T(8,128)S(1)}, u32[]{:S(2)}, u32[]{:S(2)}) collective-permute-start(f32[48,768]{1,0:T(8,128)S(1)} %dynamic-slice_bitcast_fusion.12), channel_id=1, source_target_pairs={{0,4},{2,6},{4,0},{6,2},{8,12},{10,14},{12,8},{14,10},{16,20},{18,... | collective-permute-start | bytes 442376 | tf_op jit(solution)/shard_map/ppermute | solution.py:69
  224.2 6.5 %collective-permute-start.35 = (f32[48,768]{1,0:T(8,128)S(1)}, f32[48,768]{1,0:T(8,128)S(1)}, u32[]{:S(2)}, u32[]{:S(2)}) collective-permute-start(f32[48,768]{1,0:T(8,128)S(1)} %dynamic-slice_bitcast_fusion.13), channel_id=1, source_target_pairs={{0,16},{2,18},{4,20},{6,22},{8,24},{10,26},{12,28},{14,30},{16,0},... | collective-permute-start | bytes 442376 | tf_op jit(solution)/shard_map/ppermute | solution.py:69
  (51 other events, 179.6 us)

commit v3 on v1

--- a/solution.py
+++ b/solution.py
@@ -42,16 +42,69 @@
     return part
 
 
-def dp_share(parts):
-    widths = [part.shape[1] for part in parts]
-    share = lax.psum_scatter(
-        jnp.concatenate(parts, axis=1), "dp", scatter_dimension=0, tiled=True
-    )
-    shares, start = [], 0
-    for width in widths:
-        shares.append(share[:, start : start + width])
-        start += width
-    return shares
+def dp_share_open(left, right, rotate):
+    size = lax.axis_size("dp")
+    count = size.bit_length() - 1
+    if size != 1 << count:
+        share = lax.psum_scatter(dot_cols(left, right), "dp", scatter_dimension=0, tiled=True)
+        return (share, [], [])
+    tokens, width = right.shape
+    rows = left.shape[1] // size
+    axes = list(range(count - 1, -1, -1))
+    order = list(range(count))
+    if rotate:
+        order = order[:1] + order[2:] + order[1:2]
+    blocks = left.T.reshape((2,) * count + (rows, tokens))
+    halves = [
+        jnp.dot(half.reshape(-1, tokens), right, preferred_element_type=jnp.float32).reshape(
+            (2,) * (count - 1) + (rows, width)
+        )
+        for half in split_halves(blocks, axes, order[0])
+    ]
+    return exchange(halves, axes, order)
+
+
+def split_halves(part, axes, bit):
+    mine = (lax.axis_index("dp") >> bit) & 1
+    axis = axes.index(bit)
+    return (
+        lax.dynamic_index_in_dim(part, 1 - mine, axis, keepdims=False),
+        lax.dynamic_index_in_dim(part, mine, axis, keepdims=False),
+    )
+
+
+def exchange(halves, axes, order):
+    send, keep = halves
+    bit = order[0]
+    pairs = [(i, i ^ (1 << bit)) for i in range(lax.axis_size("dp"))]
+    part = keep + lax.ppermute(send, "dp", pairs)
+    return (part, [axis for axis in axes if axis != bit], order[1:])
+
+
+def dp_share_step(state):
+    part, axes, order = state
+    if not order:
+        return state
+    return exchange(split_halves(part, axes, order[0]), axes, order)
+
+
+def dp_share_close(state):
+    while state[2]:
+        state = dp_share_step(state)
+    return state[0]
+
+
+def after(values, states):
+    values, parts = lax.optimization_barrier((values, [state[0] for state in states]))
+    return (values, [(part, *state[1:]) for part, state in zip(parts, states)])
+
+
+def open_halves(left, right):
+    middle = right.shape[1] // 2
+    return [
+        dp_share_open(left, right[:, :middle], False),
+        dp_share_open(left, right[:, middle:], True),
+    ]
 
 
 def apply_layer_norm(rows):
@@ -230,42 +283,48 @@
     )
     grad_down_low = grad_res_two.astype(jnp.bfloat16)
     grad_down_bias = jnp.sum(grad_down_low, axis=0, dtype=jnp.float32)
-    grad_down_weight = dot_cols(grad_down_low, act_low)
+    down_states = open_halves(grad_down_low, act_low)
     grad_act = jnp.dot(grad_down_low, down_weight, preferred_element_type=jnp.float32)
     normal_cdf = 0.5 * (1.0 + lax.erf(up_rows * (1.0 / math.sqrt(2.0))))
     normal_density = jnp.exp(-0.5 * up_rows * up_rows) * (1.0 / math.sqrt(2.0 * math.pi))
     grad_up_low = (grad_act * (normal_cdf + up_rows * normal_density)).astype(jnp.bfloat16)
     grad_up_bias = jnp.sum(grad_up_low, axis=0, dtype=jnp.float32)
-    grad_up_weight = dot_cols(hidden_low, grad_up_low)
+    up_states = open_halves(hidden_low, grad_up_low)
     back_sum = tensor_sum(dot_rows(grad_up_low, up_weight))
     hidden_gradient = grad_res_two + back_sum
     grad_res_one, grad_gain_first, grad_shift_first = norm_backward_pass(
         hidden_gradient, centered_rows_first, inverse_deviation_first, attention_norm_gain
     )
-    grad_attn_low = grad_res_one.astype(jnp.bfloat16)
+    grad_attn_low, down_states = after(grad_res_one.astype(jnp.bfloat16), down_states)
+    down_states = [dp_share_step(state) for state in down_states]
     grad_out_bias = jnp.sum(grad_attn_low, axis=0, dtype=jnp.float32)
-    grad_out_weight = dot_cols(grad_attn_low, context)
+    out_state = dp_share_open(grad_attn_low, context, False)
     grad_context = jnp.dot(grad_attn_low, out_weight, preferred_element_type=jnp.float32).astype(
         jnp.bfloat16
     )
-    grad_queries, grad_keys, grad_values = attend_backward(
+    grad_context, up_states = after(grad_context, up_states)
+    up_states = [dp_share_step(state) for state in up_states]
+    attention_gradients = attend_backward(
         queries, key_rows, value_rows, seg_ids, log_mass, grad_context, head_count, head_width
+    )
+    (grad_queries, grad_keys, grad_values), (out_state, *down_states) = after(
+        attention_gradients, [out_state, *down_states]
     )
     grad_query_bias = jnp.sum(grad_queries, axis=0, dtype=jnp.float32)
     grad_value_bias = jnp.sum(grad_values, axis=0, dtype=jnp.float32)
-    grad_query_weight = dot_cols(tokens, grad_queries)
-    grad_key_weight = dot_cols(tokens, grad_keys)
-    grad_value_weight = dot_cols(tokens, grad_values)
+    query_share = dp_share_close(dp_share_open(tokens, grad_queries, False))
+    key_share = dp_share_close(dp_share_open(tokens, grad_keys, True))
+    late_values, up_states = after(grad_values, up_states)
+    value_share = dp_share_close(dp_share_open(tokens, late_values, True))
+    out_share = dp_share_close(out_state)
+    down_share = jnp.concatenate([dp_share_close(state) for state in down_states], axis=1)
+    up_share = jnp.concatenate([dp_share_close(state) for state in up_states], axis=1)
     input_part = (
         dot_rows(grad_queries, query_weight)
         + dot_rows(grad_keys, key_weight)
         + dot_rows(grad_values, value_weight)
     )
     grad_tokens = grad_res_one + tensor_sum(input_part)
-    down_share, up_share = dp_share([grad_down_weight, grad_up_weight])
-    query_share, key_share, value_share, out_share = dp_share(
-        [grad_query_weight, grad_key_weight, grad_value_weight, grad_out_weight]
-    )
     rows = [
         grad_query_bias,
         grad_value_bias,
@@ -277,11 +336,14 @@
         grad_gain_second,
         grad_shift_second,
     ]
-    sums, start = [], 0
-    total = dp_sum(jnp.concatenate(rows))
-    for row in rows:
-        sums.append(total[start : start + row.shape[0]])
-        start += row.shape[0]
+    width = max(row.shape[0] for row in rows)
+    line = lax.broadcasted_iota(jnp.int32, (len(rows), width), 0)
+    stacked = jnp.zeros((len(rows), width), jnp.float32)
+    for index, row in enumerate(rows):
+        padded = jnp.pad(row, (0, width - row.shape[0]))
+        stacked = jnp.where(line == index, padded[None, :], stacked)
+    total = dp_sum(stacked)
+    sums = [total[index, : row.shape[0]] for index, row in enumerate(rows)]
     (
         query_bias_sum,
         value_bias_sum,

time: 278 us -> 206 us (0.74)
  waiting for transfers between devices: 177 us -> 101 us
  starting transfers between devices: 11.5 us -> 36.5 us
  local copies, waits for them, and re-layouts: 29 us -> 13.6 us
  between operations: 14.6 us -> 2.27 us
  matrix products: 25.4 us -> 30 us
    reduce_scatter x1 -> x0, waiting for transfers between devices: 113 us -> none  [dp_share(): lax.psum_scatter(jnp.concatenate(parts, axis=1), 'dp', scatter_dimension=...]
    ppermute x0 -> x32, waiting for transfers between devices: none -> 54.9 us  [exchange(): part = keep + lax.ppermute(send, 'dp', pairs)]
    unnamed x3 -> x0, waiting for transfers between devices: 26.8 us -> none
    ppermute x0 -> x32, starting transfers between devices: none -> 23.8 us  [exchange(): part = keep + lax.ppermute(send, 'dp', pairs)]
    unnamed x89 -> x175, local copies, waits for them, and re-layouts: 18.2 us -> 1.85 us
    ppermute x4, waiting for transfers between devices: 9.53 us -> 24 us  [dp_sum(): part = part + lax.ppermute(part, 'dp', [(i, i ^ step) for i in range(size)])]
    dot_general x6 -> x16, matrix products: 6 us -> 16.5 us  [dp_share_open(): jnp.dot(half.reshape(-1, tokens), right, preferred_element_type=jnp.float32)]
    concatenate x2, other arithmetic: 9.66 us -> 1.47 us  [the longest x1 0.73 us: local(): jnp.concatenate([dp_share_close(state) for state in up_states], axis=1)]
  transfers between devices with their start and end apart: 10 -> 40, of which waited for: 10 -> 21; matrix products, arithmetic and copies ran while one was open for 13% -> 20% of each run, Pallas kernels for 0% -> 0%
where the time goes in v3:
time: 206 us; the launch traced here: 205 us
  waiting for transfers between devices  101 us (49%)
  starting transfers between devices  36.5 us (18%)
  matrix products  30 us (15%)
  other arithmetic  21.3 us (10%)
  local copies, waits for them, and re-layouts  13.6 us (7%)
  between operations  2.27 us (1%)
    ppermute x32, waiting for transfers between devices, exchange(): part = keep + lax.ppermute(send, 'dp', pairs)  54.9 us
    ppermute x4, waiting for transfers between devices, dp_sum(): part = part + lax.ppermute(part, 'dp', [(i, i ^ step) for i in range(size)])  24 us
    ppermute x32, starting transfers between devices, exchange(): part = keep + lax.ppermute(send, 'dp', pairs)  23.8 us
    ppermute x4, waiting for transfers between devices, tensor_sum(): return part + lax.ppermute(part, 'tensor', [(0, 1), (1, 0)])  22.4 us
    dot_general x16, matrix products, dp_share_open(): jnp.dot(half.reshape(-1, tokens), right, preferred_element_type=jnp.float32)  16.5 us
    ppermute x4, starting transfers between devices, tensor_sum(): return part + lax.ppermute(part, 'tensor', [(0, 1), (1, 0)])  7.85 us
    add x24, other arithmetic, exchange(): part = keep + lax.ppermute(send, 'dp', pairs)  5.39 us
    ppermute x4, starting transfers between devices, dp_sum(): part = part + lax.ppermute(part, 'dp', [(i, i ^ step) for i in range(size)])  4.85 us
  transfers between devices with their start and end apart: 40, of which 21 were waited for; matrix products, arithmetic and copies ran while one was open for 20% of the time, Pallas kernels for 0%

profile of v3, /device:TPU:0, one launch (start us, length us, event | category | flops | bytes accessed | tf_op | source)
XLA Modules:
  0.0 205.0 jit_solution(16992893923151023167)
XLA Ops:
  0.7 0.9 broadcast_compare_fusion
  1.6 1.4 fusion.2
  4.2 1.4 fusion.1
  7.5 3.0 %collective-permute-start = (f32[128,768]{1,0:T(8,128)S(1)}, f32[128,768]{1,0:T(8,128)}, u32[]{:S(2)}, u32[]{:S(2)}) collective-permute-start(f32[128,768]{1,0:T(8,128)S(1)} %fusion.101), channel_id=1, source_target_pairs={{0,1},{1,0},{2,3},{3,2},{4,5},{5,4},{6,7},{7,6},{8,9},{9,8},{10,11... | collective-permute-start | bytes 1179656 | tf_op jit(solution)/shard_map/ppermute | solution.py:31
  13.6 6.1 %collective-permute-done = f32[128,768]{1,0:T(8,128)} collective-permute-done((f32[128,768]{1,0:T(8,128)S(1)}, f32[128,768]{1,0:T(8,128)}, u32[]{:S(2)}, u32[]{:S(2)}) %collective-permute-start) | collective-permute-done | bytes 393248 | tf_op jit(solution)/shard_map/ppermute | solution.py:31
  19.7 1.3 fusion.100
  21.3 2.1 %fusion.7 = (bf16[128,1536]{1,0:T(8,128)(2,1)S(1)}, f32[128,1536]{1,0:T(8,128)S(1)}) fusion(f32[1536]{0:T(1024)S(1)} %copy-done.86, bf16[768,1536]{1,0:T(8,128)(2,1)S(1)} %copy-done, f32[128,768]{1,0:T(8,128)S(1)} %get-tuple-element.128, f32[768]{0:T(1024)S(1)} %copy-done.80, f32[768]{0:T(1024)S(1)} %copy-done.50, f32[128]{0:T(128)S(1)} %add_rsqrt_fusion.1, ...), kind=kOutput, calls=%fused_computation.30 | convolution fusion | flops 315457536 | bytes 3945472 | tf_op jit(solution)/shard_map/dot_general | solution.py:272
  24.3 1.8 collective-permute-start.1
  26.8 7.9 %collective-permute-done.1 = f32[128,768]{1,0:T(8,128)S(1)} collective-permute-done((f32[128,768]{1,0:T(8,128)S(1)}, f32[128,768]{1,0:T(8,128)S(1)}, u32[]{:S(2)}, u32[]{:S(2)}) %collective-permute-start.1) | collective-permute-done | bytes 393248 | tf_op jit(solution)/shard_map/ppermute | solution.py:31
  34.7 0.9 fusion.99
  36.6 1.5 convert_reduce_fusion.2
  38.1 1.3 convert_reduce_fusion
  39.4 1.6 fusion.103
  41.1 1.4 collective-permute-start.2
  42.5 1.1 copy.68
  43.7 2.5 %fusion.33 = f32[2,2,2,48,768]{4,3,2,1,0:T(8,128)} fusion(bf16[128,1536]{1,0:T(8,128)(2,1)} %copy-done.10, bf16[2,2,2,2,48,128]{5,4,3,2,1,0:T(8,128)(2,1)S(1)} %bitcast.257, s32[]{:T(128)S(6)} %select_n.140), kind=kOutput, calls=%fused_computation.122 | convolution fusion | flops 75497472 | bytes 1474564 | tf_op jit(solution)/shard_map/dot_general | solution.py:59
  46.1 1.3 fusion.32
  49.8 0.9 collective-permute-done.2
  50.8 2.6 %multiply_reduce_fusion = (f32[768]{0:T(1024)}, f32[128]{0:T(128)}, f32[128]{0:T(128)}, f32[768]{0:T(1024)}, f32[128,768]{1,0:T(8,128)}, /*index=5*/bf16[768,128]{0,1:T(8,128)(2,1)}) fusion(f32[128,768]{1,0:T(8,128)S(1)} %get-tuple-element.128, f32[128]{0:T(128)S(1)} %copy-done.77, f32[128]{0:T(128)S(1)} %copy-done.65, f32[768]{0:T(1024)S(1)} %copy-done.51, ...), kind=kLoop, calls=%fused_computation.60 | loop fusion | flops 1177856 | bytes 2173952 | tf_op jit(solution)/shard_map/reduce_sum | solution.py:126
  53.4 1.1 copy.67
  54.6 1.3 fusion.31
  56.0 1.3 fusion.30
  59.1 0.9 fusion.98
  60.0 2.6 %convolution_add_fusion.1 = f32[2,2,2,48,768]{4,3,2,1,0:T(8,128)} fusion(f32[2,2,2,48,768]{4,3,2,1,0:T(8,128)} %collective-permute-done.6, bf16[128,1536]{1,0:T(8,128)(2,1)S(1)} %copy-done.12, bf16[2,2,2,2,48,128]{5,4,3,2,1,0:T(8,128)(2,1)S(1)} %bitcast.259, s32[]{:T(128)S(6)} %select_n.139), kind=kOutput, calls=%fused_computation.3 | convolution fusion | flops 75792384 | bytes 2654212 | tf_op jit(solution)/shard_map/dot_general | solution.py:59
  62.6 2.7 %convolution_add_fusion.2 = f32[2,2,2,48,768]{4,3,2,1,0:T(8,128)} fusion(f32[2,2,2,48,768]{4,3,2,1,0:T(8,128)} %collective-permute-done.5, bf16[128,1536]{1,0:T(8,128)(2,1)S(1)} %copy-done.12, bf16[2,2,2,2,48,128]{5,4,3,2,1,0:T(8,128)(2,1)S(1)} %bitcast.260, s32[]{:T(128)S(6)} %select_n.139), kind=kOutput, calls=%fused_computation.4 | convolution fusion | flops 75792384 | bytes 2654212 | tf_op jit(solution)/shard_map/dot_general | solution.py:59
  65.3 1.4 convolution_add_fusion.3
  66.7 1.3 convolution_add_fusion.4
  68.9 1.6 multiply_reduce_fusion.2
  71.4 1.2 collective-permute-start.9
  72.6 0.9 dynamic-slice_bitcast_fusion.3
  73.4 1.5 collective-permute-start.8
  75.5 1.3 dynamic-slice_bitcast_fusion
  77.4 1.0 collective-permute-start.19
  79.0 8.8 %collective-permute-done.9 = f32[2,2,48,768]{3,2,1,0:T(8,128)} collective-permute-done((f32[2,2,48,768]{3,2,1,0:T(8,128)}, f32[2,2,48,768]{3,2,1,0:T(8,128)}, u32[]{:S(2)}, u32[]{:S(2)}) %collective-permute-start.9) | collective-permute-done | bytes 589856 | tf_op jit(solution)/shard_map/ppermute | solution.py:80
  87.9 1.1 bitcast_add_fusion.2
  90.0 1.1 bitcast_add_fusion.3
  92.7 6.9 %collective-permute-done.20 = f32[2,2,48,768]{3,2,1,0:T(8,128)S(1)} collective-permute-done((f32[2,2,48,768]{3,2,1,0:T(8,128)S(1)}, f32[2,2,48,768]{3,2,1,0:T(8,128)S(1)}, u32[]{:S(2)}, u32[]{:S(2)}) %collective-permute-start.20) | collective-permute-done | bytes 589856 | tf_op jit(solution)/shard_map/ppermute | solution.py:80
  99.8 1.5 collective-permute-done.19
  101.5 0.9 collective-permute-start.32
  102.4 2.2 %collective-permute-start.34 = (f32[2,48,768]{2,1,0:T(8,128)S(1)}, f32[2,48,768]{2,1,0:T(8,128)S(1)}, u32[]{:S(2)}, u32[]{:S(2)}) collective-permute-start(f32[2,48,768]{2,1,0:T(8,128)S(1)} %dynamic-slice_bitcast_fusion.6), channel_id=1, source_target_pairs={{0,16},{2,18},{4,20},{6,22},{8,24},{10,26},{12,28},{14,30},{16,0},... | collective-permute-start | bytes 884744 | tf_op jit(solution)/shard_map/ppermute | solution.py:80
  105.7 1.7 collective-permute-start.36
  107.5 1.6 collective-permute-start.26
  109.4 3.0 %collective-permute-done.26 = f32[9,1536]{1,0:T(8,128)S(1)} collective-permute-done((f32[9,1536]{1,0:T(8,128)S(1)}, f32[9,1536]{1,0:T(8,128)S(1)}, u32[]{:S(2)}, u32[]{:S(2)}) %collective-permute-start.26) | collective-permute-done | bytes 55328 | tf_op jit(solution)/shard_map/ppermute | solution.py:40
  113.3 17.1 %collective-permute-done.27 = f32[9,1536]{1,0:T(8,128)S(1)} collective-permute-done((f32[9,1536]{1,0:T(8,128)S(1)}, f32[9,1536]{1,0:T(8,128)S(1)}, u32[]{:S(2)}, u32[]{:S(2)}) %collective-permute-start.27) | collective-permute-done | bytes 55328 | tf_op jit(solution)/shard_map/ppermute | solution.py:40
  130.5 2.7 %collective-permute-start.28 = (f32[9,1536]{1,0:T(8,128)S(1)}, f32[9,1536]{1,0:T(8,128)S(1)}, u32[]{:S(2)}, u32[]{:S(2)}) collective-permute-start(f32[9,1536]{1,0:T(8,128)S(1)} %add.405), channel_id=1, source_target_pairs={{0,16},{2,18},{4,20},{6,22},{8,24},{10,26},{12,28},{14,30},{16,0},... | collective-permute-start | bytes 165896 | tf_op jit(solution)/shard_map/ppermute | solution.py:40
  133.2 3.9 %collective-permute-done.28 = f32[9,1536]{1,0:T(8,128)S(1)} collective-permute-done((f32[9,1536]{1,0:T(8,128)S(1)}, f32[9,1536]{1,0:T(8,128)S(1)}, u32[]{:S(2)}, u32[]{:S(2)}) %collective-permute-start.28) | collective-permute-done | bytes 55328 | tf_op jit(solution)/shard_map/ppermute | solution.py:40
  137.1 1.4 collective-permute-start.29
  141.3 1.6 collective-permute-start.10
  143.8 1.6 collective-permute-start.37
  145.5 7.4 %collective-permute-done.10 = f32[128,768]{1,0:T(8,128)S(1)} collective-permute-done((f32[128,768]{1,0:T(8,128)S(1)}, f32[128,768]{1,0:T(8,128)S(1)}, u32[]{:S(2)}, u32[]{:S(2)}) %collective-permute-start.10) | collective-permute-done | bytes 393248 | tf_op jit(solution)/shard_map/ppermute | solution.py:31
  154.3 1.8 collective-permute-start.33
  156.2 2.2 %collective-permute-done.39 = f32[48,768]{1,0:T(8,128)S(1)} collective-permute-done((f32[48,768]{1,0:T(8,128)S(1)}, f32[48,768]{1,0:T(8,128)S(1)}, u32[]{:S(2)}, u32[]{:S(2)}) %collective-permute-start.39) | collective-permute-done | bytes 147488 | tf_op jit(solution)/shard_map/ppermute | solution.py:80
  159.1 6.9 %collective-permute-done.30 = f32[2,48,384]{2,1,0:T(8,128)S(1)} collective-permute-done((f32[2,48,384]{2,1,0:T(8,128)S(1)}, f32[2,48,384]{2,1,0:T(8,128)S(1)}, u32[]{:S(2)}, u32[]{:S(2)}) %collective-permute-start.30) | collective-permute-done | bytes 147488 | tf_op jit(solution)/shard_map/ppermute | solution.py:80
  166.7 4.9 %collective-permute-done.35 = f32[48,768]{1,0:T(8,128)S(1)} collective-permute-done((f32[48,768]{1,0:T(8,128)S(1)}, f32[48,768]{1,0:T(8,128)S(1)}, u32[]{:S(2)}, u32[]{:S(2)}) %collective-permute-start.35) | collective-permute-done | bytes 147488 | tf_op jit(solution)/shard_map/ppermute | solution.py:80
  173.7 2.1 %collective-permute-start.16 = (f32[2,2,48,384]{3,2,1,0:T(8,128)S(1)}, f32[2,2,48,384]{3,2,1,0:T(8,128)S(1)}, u32[]{:S(2)}, u32[]{:S(2)}) collective-permute-start(f32[2,2,48,384]{3,2,1,0:T(8,128)S(1)} %dynamic-slice_bitcast_fusion.10), channel_id=1, source_target_pairs={{0,8},{2,10},{4,12},{6,14},{8,0},{10,2},{12,4},{14,6},{16,24},{18,... | collective-permute-start | bytes 884744 | tf_op jit(solution)/shard_map/ppermute | solution.py:80
  176.1 1.3 collective-permute-start.12
  177.4 6.7 %collective-permute-done.22 = f32[2,2,48,384]{3,2,1,0:T(8,128)S(1)} collective-permute-done((f32[2,2,48,384]{3,2,1,0:T(8,128)S(1)}, f32[2,2,48,384]{3,2,1,0:T(8,128)S(1)}, u32[]{:S(2)}, u32[]{:S(2)}) %collective-permute-start.22) | collective-permute-done | bytes 294944 | tf_op jit(solution)/shard_map/ppermute | solution.py:80
  184.2 5.0 %collective-permute-done.16 = f32[2,2,48,384]{3,2,1,0:T(8,128)S(1)} collective-permute-done((f32[2,2,48,384]{3,2,1,0:T(8,128)S(1)}, f32[2,2,48,384]{3,2,1,0:T(8,128)S(1)}, u32[]{:S(2)}, u32[]{:S(2)}) %collective-permute-start.16) | collective-permute-done | bytes 294944 | tf_op jit(solution)/shard_map/ppermute | solution.py:80
  189.8 3.5 %collective-permute-done.23 = f32[2,48,384]{2,1,0:T(8,128)S(1)} collective-permute-done((f32[2,48,384]{2,1,0:T(8,128)S(1)}, f32[2,48,384]{2,1,0:T(8,128)S(1)}, u32[]{:S(2)}, u32[]{:S(2)}) %collective-permute-start.23) | collective-permute-done | bytes 147488 | tf_op jit(solution)/shard_map/ppermute | solution.py:80
  193.4 1.0 collective-permute-start.24
  194.4 2.9 %collective-permute-done.17 = f32[2,48,384]{2,1,0:T(8,128)S(1)} collective-permute-done((f32[2,48,384]{2,1,0:T(8,128)S(1)}, f32[2,48,384]{2,1,0:T(8,128)S(1)}, u32[]{:S(2)}, u32[]{:S(2)}) %collective-permute-start.17) | collective-permute-done | bytes 147488 | tf_op jit(solution)/shard_map/ppermute | solution.py:80
  197.4 1.6 collective-permute-start.18
  199.7 2.1 %collective-permute-done.18 = f32[48,384]{1,0:T(8,128)S(1)} collective-permute-done((f32[48,384]{1,0:T(8,128)S(1)}, f32[48,384]{1,0:T(8,128)S(1)}, u32[]{:S(2)}, u32[]{:S(2)}) %collective-permute-start.18) | collective-permute-done | bytes 73760 | tf_op jit(solution)/shard_map/ppermute | solution.py:80
  202.4 2.0 collective-permute-done.14
  (327 shorter events, 33.0 us)
Async XLA Ops:
  0.7 20.6 %copy-start = (bf16[768,1536]{1,0:T(8,128)(2,1)S(1)}, bf16[768,1536]{1,0:T(8,128)(2,1)}, u32[]{:S(2)}) copy-start(bf16[768,1536]{1,0:T(8,128)(2,1)} %param.29) | copy-start | bytes 7077892
  7.5 6.1 %copy-start.27 = (f32[128,768]{1,0:T(8,128)}, f32[128,768]{1,0:T(8,128)S(1)}, u32[]{:S(2)}) copy-start(f32[128,768]{1,0:T(8,128)S(1)} %fusion.101) | copy-start | bytes 1179652
  7.5 12.3 %collective-permute-start = (f32[128,768]{1,0:T(8,128)S(1)}, f32[128,768]{1,0:T(8,128)}, u32[]{:S(2)}, u32[]{:S(2)}) collective-permute-start(f32[128,768]{1,0:T(8,128)S(1)} %fusion.101), channel_id=1, source_target_pairs={{0,1},{1,0},{2,3},{3,2},{4,5},{5,4},{6,7},{7,6},{8,9},{9,8},{10,11... | collective-permute-start | bytes 1179656 | tf_op jit(solution)/shard_map/ppermute | solution.py:31
  11.2 10.0 %copy-start.50 = (f32[768]{0:T(1024)S(1)}, f32[768]{0:T(1024)}, u32[]{:S(2)}) copy-start(f32[768]{0:T(1024)} %param.27) | copy-start | bytes 9220
  11.3 10.0 %copy-start.80 = (f32[768]{0:T(1024)S(1)}, f32[768]{0:T(1024)}, u32[]{:S(2)}) copy-start(f32[768]{0:T(1024)} %param.28) | copy-start | bytes 9220
  11.3 10.0 %copy-start.86 = (f32[1536]{0:T(1024)S(1)}, f32[1536]{0:T(1024)}, u32[]{:S(2)}) copy-start(f32[1536]{0:T(1024)} %param.30) | copy-start | bytes 18436
  21.0 13.7 %copy-start.64 = (f32[128]{0:T(128)}, f32[128]{0:T(128)S(1)}, u32[]{:S(2)}) copy-start(f32[128]{0:T(128)S(1)} %broadcast_multiply_fusion.5) | copy-start | bytes 1540
  21.3 13.4 %copy-start.76 = (f32[128]{0:T(128)}, f32[128]{0:T(128)S(1)}, u32[]{:S(2)}) copy-start(f32[128]{0:T(128)S(1)} %add_rsqrt_fusion.1) | copy-start | bytes 1540
  23.4 11.3 %copy-start.79 = (f32[768]{0:T(1024)S(1)}, f32[768]{0:T(1024)}, u32[]{:S(2)}) copy-start(f32[768]{0:T(1024)} %param.32) | copy-start | bytes 9220
  24.3 11.5 %copy-start.39 = (bf16[128,768]{1,0:T(8,128)(2,1)S(1)}, bf16[128,768]{1,0:T(8,128)(2,1)}, u32[]{:S(2)}) copy-start(bf16[128,768]{1,0:T(8,128)(2,1)} %param.35) | copy-start | bytes 589828
  24.3 11.5 %copy-start.55 = (f32[768]{0:T(1024)S(1)}, f32[768]{0:T(1024)}, u32[]{:S(2)}) copy-start(f32[768]{0:T(1024)} %param.33) | copy-start | bytes 9220
  24.3 10.4 %collective-permute-start.1 = (f32[128,768]{1,0:T(8,128)S(1)}, f32[128,768]{1,0:T(8,128)S(1)}, u32[]{:S(2)}, u32[]{:S(2)}) collective-permute-start(f32[128,768]{1,0:T(8,128)S(1)} %fusion.102), channel_id=1, source_target_pairs={{0,1},{1,0},{2,3},{3,2},{4,5},{5,4},{6,7},{7,6},{8,9},{9,8},{10,11... | collective-permute-start | bytes 1179656 | tf_op jit(solution)/shard_map/ppermute | solution.py:31
  26.8 9.9 %copy-start.81 = (f32[768]{0:T(1024)S(1)}, f32[768]{0:T(1024)}, u32[]{:S(2)}) copy-start(f32[768]{0:T(1024)} %param.34) | copy-start | bytes 9220
  41.1 9.7 %collective-permute-start.2 = (f32[128,768]{1,0:T(8,128)}, f32[128,768]{1,0:T(8,128)}, u32[]{:S(2)}, u32[]{:S(2)}) collective-permute-start(f32[128,768]{1,0:T(8,128)} %fusion.103), channel_id=1, source_target_pairs={{0,1},{1,0},{2,3},{3,2},{4,5},{5,4},{6,7},{7,6},{8,9},{9,8},{10,11... | collective-permute-start | bytes 1179656 | tf_op jit(solution)/shard_map/ppermute | solution.py:31
  43.6 5.0 %copy-start.60 = (f32[768]{0:T(1024)S(1)}, f32[768]{0:T(1024)}, u32[]{:S(2)}) copy-start(f32[768]{0:T(1024)} %get-tuple-element.111) | copy-start | bytes 9220
  43.6 5.6 %copy-start.59 = (f32[768]{0:T(1024)S(1)}, f32[768]{0:T(1024)}, u32[]{:S(2)}) copy-start(f32[768]{0:T(1024)} %get-tuple-element.106) | copy-start | bytes 9220
  43.6 7.1 %copy-start.25 = (f32[128,768]{1,0:T(8,128)S(1)}, f32[128,768]{1,0:T(8,128)}, u32[]{:S(2)}) copy-start(f32[128,768]{1,0:T(8,128)} %copy-done.24) | copy-start | bytes 1179652
  43.6 7.1 %copy-start.51 = (f32[768]{0:T(1024)S(1)}, f32[768]{0:T(1024)}, u32[]{:S(2)}) copy-start(f32[768]{0:T(1024)} %param.27) | copy-start | bytes 9220
  43.7 7.1 %copy-start.65 = (f32[128]{0:T(128)S(1)}, f32[128]{0:T(128)}, u32[]{:S(2)}) copy-start(f32[128]{0:T(128)} %copy-done.64) | copy-start | bytes 1540
  43.7 7.1 %copy-start.77 = (f32[128]{0:T(128)S(1)}, f32[128]{0:T(128)}, u32[]{:S(2)}) copy-start(f32[128]{0:T(128)} %copy-done.76) | copy-start | bytes 1540
  46.1 13.8 %collective-permute-start.6 = (f32[2,2,2,48,768]{4,3,2,1,0:T(8,128)}, f32[2,2,2,48,768]{4,3,2,1,0:T(8,128)}, u32[]{:S(2)}, u32[]{:S(2)}) collective-permute-start(f32[2,2,2,48,768]{4,3,2,1,0:T(8,128)} %fusion.33), channel_id=1, source_target_pairs={{0,2},{2,0},{4,6},{6,4},{8,10},{10,8},{12,14},{14,12},{16,18},{18,... | collective-permute-start | bytes 3538952 | tf_op jit(solution)/shard_map/ppermute | solution.py:80
  47.5 15.1 %collective-permute-start.5 = (f32[2,2,2,48,768]{4,3,2,1,0:T(8,128)}, f32[2,2,2,48,768]{4,3,2,1,0:T(8,128)}, u32[]{:S(2)}, u32[]{:S(2)}) collective-permute-start(f32[2,2,2,48,768]{4,3,2,1,0:T(8,128)} %fusion.32), channel_id=1, source_target_pairs={{0,2},{2,0},{4,6},{6,4},{8,10},{10,8},{12,14},{14,12},{16,18},{18,... | collective-permute-start | bytes 3538952 | tf_op jit(solution)/shard_map/ppermute | solution.py:80
  55.9 9.4 %collective-permute-start.4 = (f32[2,2,2,48,768]{4,3,2,1,0:T(8,128)S(1)}, f32[2,2,2,48,768]{4,3,2,1,0:T(8,128)S(1)}, u32[]{:S(2)}, u32[]{:S(2)}) collective-permute-start(f32[2,2,2,48,768]{4,3,2,1,0:T(8,128)S(1)} %fusion.31), channel_id=1, source_target_pairs={{0,2},{2,0},{4,6},{6,4},{8,10},{10,8},{12,14},{14,12},{16,18},{18,... | collective-permute-start | bytes 3538952 | tf_op jit(solution)/shard_map/ppermute | solution.py:80
  57.3 9.4 %collective-permute-start.3 = (f32[2,2,2,48,768]{4,3,2,1,0:T(8,128)S(1)}, f32[2,2,2,48,768]{4,3,2,1,0:T(8,128)S(1)}, u32[]{:S(2)}, u32[]{:S(2)}) collective-permute-start(f32[2,2,2,48,768]{4,3,2,1,0:T(8,128)S(1)} %fusion.30), channel_id=1, source_target_pairs={{0,2},{2,0},{4,6},{6,4},{8,10},{10,8},{12,14},{14,12},{16,18},{18,... | collective-permute-start | bytes 3538952 | tf_op jit(solution)/shard_map/ppermute | solution.py:80
  71.4 16.5 %collective-permute-start.9 = (f32[2,2,48,768]{3,2,1,0:T(8,128)}, f32[2,2,48,768]{3,2,1,0:T(8,128)}, u32[]{:S(2)}, u32[]{:S(2)}) collective-permute-start(f32[2,2,48,768]{3,2,1,0:T(8,128)} %dynamic-slice_bitcast_fusion.2), channel_id=1, source_target_pairs={{0,8},{2,10},{4,12},{6,14},{8,0},{10,2},{12,4},{14,6},{16,24},{18,... | collective-permute-start | bytes 1769480 | tf_op jit(solution)/shard_map/ppermute | solution.py:80
  73.4 16.5 %collective-permute-start.8 = (f32[2,2,48,768]{3,2,1,0:T(8,128)}, f32[2,2,48,768]{3,2,1,0:T(8,128)}, u32[]{:S(2)}, u32[]{:S(2)}) collective-permute-start(f32[2,2,48,768]{3,2,1,0:T(8,128)} %dynamic-slice_bitcast_fusion.3), channel_id=1, source_target_pairs={{0,4},{2,6},{4,0},{6,2},{8,12},{10,14},{12,8},{14,10},{16,20},{18,... | collective-permute-start | bytes 1769480 | tf_op jit(solution)/shard_map/ppermute | solution.py:80
  75.4 13.6 %collective-permute-start.7 = (f32[2,2,2,48,384]{4,3,2,1,0:T(8,128)S(1)}, f32[2,2,2,48,384]{4,3,2,1,0:T(8,128)S(1)}, u32[]{:S(2)}, u32[]{:S(2)}) collective-permute-start(f32[2,2,2,48,384]{4,3,2,1,0:T(8,128)S(1)} %fusion.49), channel_id=1, source_target_pairs={{0,2},{2,0},{4,6},{6,4},{8,10},{10,8},{12,14},{14,12},{16,18},{18,... | collective-permute-start | bytes 1769480 | tf_op jit(solution)/shard_map/ppermute | solution.py:80
  76.8 22.8 %collective-permute-start.20 = (f32[2,2,48,768]{3,2,1,0:T(8,128)S(1)}, f32[2,2,48,768]{3,2,1,0:T(8,128)S(1)}, u32[]{:S(2)}, u32[]{:S(2)}) collective-permute-start(f32[2,2,48,768]{3,2,1,0:T(8,128)S(1)} %dynamic-slice_bitcast_fusion), channel_id=1, source_target_pairs={{0,8},{2,10},{4,12},{6,14},{8,0},{10,2},{12,4},{14,6},{16,24},{18,... | collective-permute-start | bytes 1769480 | tf_op jit(solution)/shard_map/ppermute | solution.py:80
  77.4 10.5 %copy-start.7 = (f32[2,2,2,48,768]{4,3,2,1,0:T(8,128)S(1)}, f32[2,2,2,48,768]{4,3,2,1,0:T(8,128)}, u32[]{:S(2)}) copy-start(f32[2,2,2,48,768]{4,3,2,1,0:T(8,128)} %convolution_add_fusion.3) | copy-start | bytes 3538948
  77.4 24.0 %collective-permute-start.19 = (f32[2,2,48,768]{3,2,1,0:T(8,128)S(1)}, f32[2,2,48,768]{3,2,1,0:T(8,128)S(1)}, u32[]{:S(2)}, u32[]{:S(2)}) collective-permute-start(f32[2,2,48,768]{3,2,1,0:T(8,128)S(1)} %dynamic-slice_bitcast_fusion.1), channel_id=1, source_target_pairs={{0,4},{2,6},{4,0},{6,2},{8,12},{10,14},{12,8},{14,10},{16,20},{18,... | collective-permute-start | bytes 1769480 | tf_op jit(solution)/shard_map/ppermute | solution.py:80
  78.8 10.2 %copy-start.32 = (bf16[6,64,128]{2,1,0:T(8,128)(2,1)S(1)}, bf16[6,64,128]{2,1,0:T(8,128)(2,1)}, u32[]{:S(2)}) copy-start(bf16[6,64,128]{2,1,0:T(8,128)(2,1)} %copy-done.30) | copy-start | bytes 294916
  78.8 10.2 %copy-start.38 = (bf16[768,128]{1,0:T(8,128)(2,1)S(1)}, bf16[768,128]{1,0:T(8,128)(2,1)}, u32[]{:S(2)}) copy-start(bf16[768,128]{1,0:T(8,128)(2,1)} %copy-done.37) | copy-start | bytes 589828
  79.0 10.9 %copy-start.5 = (f32[2,2,2,48,768]{4,3,2,1,0:T(8,128)S(1)}, f32[2,2,2,48,768]{4,3,2,1,0:T(8,128)}, u32[]{:S(2)}) copy-start(f32[2,2,2,48,768]{4,3,2,1,0:T(8,128)} %convolution_add_fusion.4) | copy-start | bytes 3538948
  91.5 8.1 %copy-start.3 = (f32[2,2,2,48,768]{4,3,2,1,0:T(8,128)S(1)}, f32[2,2,2,48,768]{4,3,2,1,0:T(8,128)}, u32[]{:S(2)}) copy-start(f32[2,2,2,48,768]{4,3,2,1,0:T(8,128)} %convolution_add_fusion.1) | copy-start | bytes 3538948
  99.8 5.2 %copy-start.18 = (bf16[768,384]{1,0:T(8,128)(2,1)S(1)}, bf16[768,384]{1,0:T(8,128)(2,1)}, u32[]{:S(2)}) copy-start(bf16[768,384]{1,0:T(8,128)(2,1)} %param.20) | copy-start | bytes 1769476
  101.5 39.7 %collective-permute-start.32 = (f32[2,48,768]{2,1,0:T(8,128)S(1)}, f32[2,48,768]{2,1,0:T(8,128)S(1)}, u32[]{:S(2)}, u32[]{:S(2)}) collective-permute-start(f32[2,48,768]{2,1,0:T(8,128)S(1)} %dynamic-slice_bitcast_fusion.7), channel_id=1, source_target_pairs={{0,8},{2,10},{4,12},{6,14},{8,0},{10,2},{12,4},{14,6},{16,24},{18,... | collective-permute-start | bytes 884744 | tf_op jit(solution)/shard_map/ppermute | solution.py:80
  102.4 38.9 %collective-permute-start.34 = (f32[2,48,768]{2,1,0:T(8,128)S(1)}, f32[2,48,768]{2,1,0:T(8,128)S(1)}, u32[]{:S(2)}, u32[]{:S(2)}) collective-permute-start(f32[2,48,768]{2,1,0:T(8,128)S(1)} %dynamic-slice_bitcast_fusion.6), channel_id=1, source_target_pairs={{0,16},{2,18},{4,20},{6,22},{8,24},{10,26},{12,28},{14,30},{16,0},... | collective-permute-start | bytes 884744 | tf_op jit(solution)/shard_map/ppermute | solution.py:80
  104.9 2.5 %collective-permute-start.25 = (f32[9,1536]{1,0:T(8,128)S(1)}, f32[9,1536]{1,0:T(8,128)S(1)}, u32[]{:S(2)}, u32[]{:S(2)}) collective-permute-start(f32[9,1536]{1,0:T(8,128)S(1)} %select_select_fusion), channel_id=1, source_target_pairs={{0,2},{2,0},{4,6},{6,4},{8,10},{10,8},{12,14},{14,12},{16,18},{18,... | collective-permute-start | bytes 165896 | tf_op jit(solution)/shard_map/ppermute | solution.py:40
  105.7 34.7 %collective-permute-start.36 = (f32[2,48,768]{2,1,0:T(8,128)S(1)}, f32[2,48,768]{2,1,0:T(8,128)S(1)}, u32[]{:S(2)}, u32[]{:S(2)}) collective-permute-start(f32[2,48,768]{2,1,0:T(8,128)S(1)} %dynamic-slice_bitcast_fusion.5), channel_id=1, source_target_pairs={{0,8},{2,10},{4,12},{6,14},{8,0},{10,2},{12,4},{14,6},{16,24},{18,... | collective-permute-start | bytes 884744 | tf_op jit(solution)/shard_map/ppermute | solution.py:80
  107.5 5.0 %collective-permute-start.26 = (f32[9,1536]{1,0:T(8,128)S(1)}, f32[9,1536]{1,0:T(8,128)S(1)}, u32[]{:S(2)}, u32[]{:S(2)}) collective-permute-start(f32[9,1536]{1,0:T(8,128)S(1)} %fusion.95), channel_id=1, source_target_pairs={{0,4},{2,6},{4,0},{6,2},{8,12},{10,14},{12,8},{14,10},{16,20},{18,... | collective-permute-start | bytes 165896 | tf_op jit(solution)/shard_map/ppermute | solution.py:40
  109.1 31.4 %collective-permute-start.38 = (f32[2,48,768]{2,1,0:T(8,128)S(1)}, f32[2,48,768]{2,1,0:T(8,128)S(1)}, u32[]{:S(2)}, u32[]{:S(2)}) collective-permute-start(f32[2,48,768]{2,1,0:T(8,128)S(1)} %dynamic-slice_bitcast_fusion.4), channel_id=1, source_target_pairs={{0,16},{2,18},{4,20},{6,22},{8,24},{10,26},{12,28},{14,30},{16,0},... | collective-permute-start | bytes 884744 | tf_op jit(solution)/shard_map/ppermute | solution.py:80
  112.6 17.9 %collective-permute-start.27 = (f32[9,1536]{1,0:T(8,128)S(1)}, f32[9,1536]{1,0:T(8,128)S(1)}, u32[]{:S(2)}, u32[]{:S(2)}) collective-permute-start(f32[9,1536]{1,0:T(8,128)S(1)} %fusion.139), channel_id=1, source_target_pairs={{0,8},{2,10},{4,12},{6,14},{8,0},{10,2},{12,4},{14,6},{16,24},{18,... | collective-permute-start | bytes 165896 | tf_op jit(solution)/shard_map/ppermute | solution.py:40
  130.5 6.6 %collective-permute-start.28 = (f32[9,1536]{1,0:T(8,128)S(1)}, f32[9,1536]{1,0:T(8,128)S(1)}, u32[]{:S(2)}, u32[]{:S(2)}) collective-permute-start(f32[9,1536]{1,0:T(8,128)S(1)} %add.405), channel_id=1, source_target_pairs={{0,16},{2,18},{4,20},{6,22},{8,24},{10,26},{12,28},{14,30},{16,0},... | collective-permute-start | bytes 165896 | tf_op jit(solution)/shard_map/ppermute | solution.py:40
  137.1 6.7 %collective-permute-start.29 = (f32[2,2,48,384]{3,2,1,0:T(8,128)S(1)}, f32[2,2,48,384]{3,2,1,0:T(8,128)S(1)}, u32[]{:S(2)}, u32[]{:S(2)}) collective-permute-start(f32[2,2,48,384]{3,2,1,0:T(8,128)S(1)} %dynamic-slice_bitcast_fusion.8), channel_id=1, source_target_pairs={{0,4},{2,6},{4,0},{6,2},{8,12},{10,14},{12,8},{14,10},{16,20},{18,... | collective-permute-start | bytes 884744 | tf_op jit(solution)/shard_map/ppermute | solution.py:80
  140.4 32.6 %collective-permute-start.21 = (f32[2,2,2,48,384]{4,3,2,1,0:T(8,128)S(1)}, f32[2,2,2,48,384]{4,3,2,1,0:T(8,128)S(1)}, u32[]{:S(2)}, u32[]{:S(2)}) collective-permute-start(f32[2,2,2,48,384]{4,3,2,1,0:T(8,128)S(1)} %fusion.34), channel_id=1, source_target_pairs={{0,2},{2,0},{4,6},{6,4},{8,10},{10,8},{12,14},{14,12},{16,18},{18,... | collective-permute-start | bytes 1769480 | tf_op jit(solution)/shard_map/ppermute | solution.py:80
  140.5 32.9 %collective-permute-start.15 = (f32[2,2,2,48,384]{4,3,2,1,0:T(8,128)S(1)}, f32[2,2,2,48,384]{4,3,2,1,0:T(8,128)S(1)}, u32[]{:S(2)}, u32[]{:S(2)}) collective-permute-start(f32[2,2,2,48,384]{4,3,2,1,0:T(8,128)S(1)} %fusion.37), channel_id=1, source_target_pairs={{0,2},{2,0},{4,6},{6,4},{8,10},{10,8},{12,14},{14,12},{16,18},{18,... | collective-permute-start | bytes 1769480 | tf_op jit(solution)/shard_map/ppermute | solution.py:80
  141.2 34.6 %collective-permute-start.11 = (f32[2,2,2,48,384]{4,3,2,1,0:T(8,128)S(1)}, f32[2,2,2,48,384]{4,3,2,1,0:T(8,128)S(1)}, u32[]{:S(2)}, u32[]{:S(2)}) collective-permute-start(f32[2,2,2,48,384]{4,3,2,1,0:T(8,128)S(1)} %fusion.42), channel_id=1, source_target_pairs={{0,2},{2,0},{4,6},{6,4},{8,10},{10,8},{12,14},{14,12},{16,18},{18,... | collective-permute-start | bytes 1769480 | tf_op jit(solution)/shard_map/ppermute | solution.py:80
  141.3 12.2 %copy-start.28 = (f32[128,768]{1,0:T(8,128)S(1)}, f32[128,768]{1,0:T(8,128)}, u32[]{:S(2)}) copy-start(f32[128,768]{1,0:T(8,128)} %get-tuple-element.123) | copy-start | bytes 1179652
  141.3 11.6 %collective-permute-start.10 = (f32[128,768]{1,0:T(8,128)S(1)}, f32[128,768]{1,0:T(8,128)S(1)}, u32[]{:S(2)}, u32[]{:S(2)}) collective-permute-start(f32[128,768]{1,0:T(8,128)S(1)} %convolution_add_fusion.9), channel_id=1, source_target_pairs={{0,1},{1,0},{2,3},{3,2},{4,5},{5,4},{6,7},{7,6},{8,9},{9,8},{10,11... | collective-permute-start | bytes 1179656 | tf_op jit(solution)/shard_map/ppermute | solution.py:31
  143.8 10.5 %collective-permute-start.37 = (f32[48,768]{1,0:T(8,128)S(1)}, f32[48,768]{1,0:T(8,128)S(1)}, u32[]{:S(2)}, u32[]{:S(2)}) collective-permute-start(f32[48,768]{1,0:T(8,128)S(1)} %dynamic-slice_bitcast_fusion.13), channel_id=1, source_target_pairs={{0,16},{2,18},{4,20},{6,22},{8,24},{10,26},{12,28},{14,30},{16,0},... | collective-permute-start | bytes 442376 | tf_op jit(solution)/shard_map/ppermute | solution.py:80
  152.9 5.5 %collective-permute-start.39 = (f32[48,768]{1,0:T(8,128)S(1)}, f32[48,768]{1,0:T(8,128)S(1)}, u32[]{:S(2)}, u32[]{:S(2)}) collective-permute-start(f32[48,768]{1,0:T(8,128)S(1)} %dynamic-slice_bitcast_fusion.12), channel_id=1, source_target_pairs={{0,4},{2,6},{4,0},{6,2},{8,12},{10,14},{12,8},{14,10},{16,20},{18,... | collective-permute-start | bytes 442376 | tf_op jit(solution)/shard_map/ppermute | solution.py:80
  154.3 12.3 %collective-permute-start.33 = (f32[48,768]{1,0:T(8,128)S(1)}, f32[48,768]{1,0:T(8,128)S(1)}, u32[]{:S(2)}, u32[]{:S(2)}) collective-permute-start(f32[48,768]{1,0:T(8,128)S(1)} %dynamic-slice_bitcast_fusion.15), channel_id=1, source_target_pairs={{0,16},{2,18},{4,20},{6,22},{8,24},{10,26},{12,28},{14,30},{16,0},... | collective-permute-start | bytes 442376 | tf_op jit(solution)/shard_map/ppermute | solution.py:80
  158.4 7.6 %collective-permute-start.30 = (f32[2,48,384]{2,1,0:T(8,128)S(1)}, f32[2,48,384]{2,1,0:T(8,128)S(1)}, u32[]{:S(2)}, u32[]{:S(2)}) collective-permute-start(f32[2,48,384]{2,1,0:T(8,128)S(1)} %dynamic-slice_bitcast_fusion.16), channel_id=1, source_target_pairs={{0,8},{2,10},{4,12},{6,14},{8,0},{10,2},{12,4},{14,6},{16,24},{18,... | collective-permute-start | bytes 442376 | tf_op jit(solution)/shard_map/ppermute | solution.py:80
  166.0 5.6 %collective-permute-start.35 = (f32[48,768]{1,0:T(8,128)S(1)}, f32[48,768]{1,0:T(8,128)S(1)}, u32[]{:S(2)}, u32[]{:S(2)}) collective-permute-start(f32[48,768]{1,0:T(8,128)S(1)} %dynamic-slice_bitcast_fusion.14), channel_id=1, source_target_pairs={{0,4},{2,6},{4,0},{6,2},{8,12},{10,14},{12,8},{14,10},{16,20},{18,... | collective-permute-start | bytes 442376 | tf_op jit(solution)/shard_map/ppermute | solution.py:80
  166.6 5.7 %collective-permute-start.31 = (f32[48,384]{1,0:T(8,128)S(1)}, f32[48,384]{1,0:T(8,128)S(1)}, u32[]{:S(2)}, u32[]{:S(2)}) collective-permute-start(f32[48,384]{1,0:T(8,128)S(1)} %dynamic-slice_bitcast_fusion.20), channel_id=1, source_target_pairs={{0,16},{2,18},{4,20},{6,22},{8,24},{10,26},{12,28},{14,30},{16,0},... | collective-permute-start | bytes 221192 | tf_op jit(solution)/shard_map/ppermute | solution.py:80
  173.3 10.8 %collective-permute-start.22 = (f32[2,2,48,384]{3,2,1,0:T(8,128)S(1)}, f32[2,2,48,384]{3,2,1,0:T(8,128)S(1)}, u32[]{:S(2)}, u32[]{:S(2)}) collective-permute-start(f32[2,2,48,384]{3,2,1,0:T(8,128)S(1)} %dynamic-slice_bitcast_fusion.9), channel_id=1, source_target_pairs={{0,8},{2,10},{4,12},{6,14},{8,0},{10,2},{12,4},{14,6},{16,24},{18,... | collective-permute-start | bytes 884744 | tf_op jit(solution)/shard_map/ppermute | solution.py:80
  173.7 15.5 %collective-permute-start.16 = (f32[2,2,48,384]{3,2,1,0:T(8,128)S(1)}, f32[2,2,48,384]{3,2,1,0:T(8,128)S(1)}, u32[]{:S(2)}, u32[]{:S(2)}) collective-permute-start(f32[2,2,48,384]{3,2,1,0:T(8,128)S(1)} %dynamic-slice_bitcast_fusion.10), channel_id=1, source_target_pairs={{0,8},{2,10},{4,12},{6,14},{8,0},{10,2},{12,4},{14,6},{16,24},{18,... | collective-permute-start | bytes 884744 | tf_op jit(solution)/shard_map/ppermute | solution.py:80
  176.1 13.3 %collective-permute-start.12 = (f32[2,2,48,384]{3,2,1,0:T(8,128)S(1)}, f32[2,2,48,384]{3,2,1,0:T(8,128)S(1)}, u32[]{:S(2)}, u32[]{:S(2)}) collective-permute-start(f32[2,2,48,384]{3,2,1,0:T(8,128)S(1)} %dynamic-slice_bitcast_fusion.11), channel_id=1, source_target_pairs={{0,4},{2,6},{4,0},{6,2},{8,12},{10,14},{12,8},{14,10},{16,20},{18,... | collective-permute-start | bytes 884744 | tf_op jit(solution)/shard_map/ppermute | solution.py:80
  184.2 9.2 %collective-permute-start.23 = (f32[2,48,384]{2,1,0:T(8,128)S(1)}, f32[2,48,384]{2,1,0:T(8,128)S(1)}, u32[]{:S(2)}, u32[]{:S(2)}) collective-permute-start(f32[2,48,384]{2,1,0:T(8,128)S(1)} %dynamic-slice_bitcast_fusion.17), channel_id=1, source_target_pairs={{0,16},{2,18},{4,20},{6,22},{8,24},{10,26},{12,28},{14,30},{16,0},... | collective-permute-start | bytes 442376 | tf_op jit(solution)/shard_map/ppermute | solution.py:80
  189.3 8.0 %collective-permute-start.17 = (f32[2,48,384]{2,1,0:T(8,128)S(1)}, f32[2,48,384]{2,1,0:T(8,128)S(1)}, u32[]{:S(2)}, u32[]{:S(2)}) collective-permute-start(f32[2,48,384]{2,1,0:T(8,128)S(1)} %dynamic-slice_bitcast_fusion.18), channel_id=1, source_target_pairs={{0,16},{2,18},{4,20},{6,22},{8,24},{10,26},{12,28},{14,30},{16,0},... | collective-permute-start | bytes 442376 | tf_op jit(solution)/shard_map/ppermute | solution.py:80
  189.5 9.4 %collective-permute-start.13 = (f32[2,48,384]{2,1,0:T(8,128)S(1)}, f32[2,48,384]{2,1,0:T(8,128)S(1)}, u32[]{:S(2)}, u32[]{:S(2)}) collective-permute-start(f32[2,48,384]{2,1,0:T(8,128)S(1)} %dynamic-slice_bitcast_fusion.19), channel_id=1, source_target_pairs={{0,8},{2,10},{4,12},{6,14},{8,0},{10,2},{12,4},{14,6},{16,24},{18,... | collective-permute-start | bytes 442376 | tf_op jit(solution)/shard_map/ppermute | solution.py:80
  193.4 5.7 %collective-permute-start.24 = (f32[48,384]{1,0:T(8,128)S(1)}, f32[48,384]{1,0:T(8,128)S(1)}, u32[]{:S(2)}, u32[]{:S(2)}) collective-permute-start(f32[48,384]{1,0:T(8,128)S(1)} %dynamic-slice_bitcast_fusion.21), channel_id=1, source_target_pairs={{0,4},{2,6},{4,0},{6,2},{8,12},{10,14},{12,8},{14,10},{16,20},{18,... | collective-permute-start | bytes 221192 | tf_op jit(solution)/shard_map/ppermute | solution.py:80
  197.4 4.4 %collective-permute-start.18 = (f32[48,384]{1,0:T(8,128)S(1)}, f32[48,384]{1,0:T(8,128)S(1)}, u32[]{:S(2)}, u32[]{:S(2)}) collective-permute-start(f32[48,384]{1,0:T(8,128)S(1)} %dynamic-slice_bitcast_fusion.22), channel_id=1, source_target_pairs={{0,4},{2,6},{4,0},{6,2},{8,12},{10,14},{12,8},{14,10},{16,20},{18,... | collective-permute-start | bytes 221192 | tf_op jit(solution)/shard_map/ppermute | solution.py:80
  199.0 5.4 %collective-permute-start.14 = (f32[48,384]{1,0:T(8,128)S(1)}, f32[48,384]{1,0:T(8,128)S(1)}, u32[]{:S(2)}, u32[]{:S(2)}) collective-permute-start(f32[48,384]{1,0:T(8,128)S(1)} %dynamic-slice_bitcast_fusion.23), channel_id=1, source_target_pairs={{0,16},{2,18},{4,20},{6,22},{8,24},{10,26},{12,28},{14,30},{16,0},... | collective-permute-start | bytes 221192 | tf_op jit(solution)/shard_map/ppermute | solution.py:80
  (63 other events, 202.2 us)

commit v4 on v3

--- a/solution.py
+++ b/solution.py
@@ -312,13 +312,9 @@
     )
     grad_query_bias = jnp.sum(grad_queries, axis=0, dtype=jnp.float32)
     grad_value_bias = jnp.sum(grad_values, axis=0, dtype=jnp.float32)
-    query_share = dp_share_close(dp_share_open(tokens, grad_queries, False))
-    key_share = dp_share_close(dp_share_open(tokens, grad_keys, True))
-    late_values, up_states = after(grad_values, up_states)
-    value_share = dp_share_close(dp_share_open(tokens, late_values, True))
-    out_share = dp_share_close(out_state)
-    down_share = jnp.concatenate([dp_share_close(state) for state in down_states], axis=1)
-    up_share = jnp.concatenate([dp_share_close(state) for state in up_states], axis=1)
+    query_state = dp_share_open(tokens, grad_queries, False)
+    key_state = dp_share_open(tokens, grad_keys, True)
+    value_state = dp_share_open(tokens, grad_values, True)
     input_part = (
         dot_rows(grad_queries, query_weight)
         + dot_rows(grad_keys, key_weight)
@@ -342,6 +338,15 @@
     for index, row in enumerate(rows):
         padded = jnp.pad(row, (0, width - row.shape[0]))
         stacked = jnp.where(line == index, padded[None, :], stacked)
+    stacked, (query_state, key_state, value_state, *up_states) = after(
+        stacked, [query_state, key_state, value_state, *up_states]
+    )
+    query_share = dp_share_close(query_state)
+    key_share = dp_share_close(key_state)
+    value_share = dp_share_close(value_state)
+    out_share = dp_share_close(out_state)
+    down_share = jnp.concatenate([dp_share_close(state) for state in down_states], axis=1)
+    up_share = jnp.concatenate([dp_share_close(state) for state in up_states], axis=1)
     total = dp_sum(stacked)
     sums = [total[index, : row.shape[0]] for index, row in enumerate(rows)]
     (

time: 206 us -> 199 us (0.966)
  waiting for transfers between devices: 101 us -> 88.4 us
  starting transfers between devices: 36.5 us -> 42.9 us
    ppermute x32, starting transfers between devices: 23.8 us -> 31.6 us  [exchange(): part = keep + lax.ppermute(send, 'dp', pairs)]
    ppermute x4, waiting for transfers between devices: 22.4 us -> 16.7 us  [tensor_sum(): return part + lax.ppermute(part, 'tensor', [(0, 1), (1, 0)])]
    ppermute x4, waiting for transfers between devices: 24 us -> 20.2 us  [dp_sum(): part = part + lax.ppermute(part, 'dp', [(i, i ^ step) for i in range(size)])]
    ppermute x32, waiting for transfers between devices: 54.9 us -> 51.5 us  [exchange(): part = keep + lax.ppermute(send, 'dp', pairs)]
  transfers between devices with their start and end apart: 40 -> 40, of which waited for: 21 -> 21; matrix products, arithmetic and copies ran while one was open for 20% -> 21% of each run, Pallas kernels for 0% -> 0%
where the time goes in v4:
time: 199 us; the launch traced here: 198 us
  waiting for transfers between devices  88.4 us (44%)
  starting transfers between devices  42.9 us (22%)
  matrix products  29.9 us (15%)
  other arithmetic  21.1 us (11%)
  local copies, waits for them, and re-layouts  13.7 us (7%)
  between operations  2.24 us (1%)
    ppermute x32, waiting for transfers between devices, exchange(): part = keep + lax.ppermute(send, 'dp', pairs)  51.5 us
    ppermute x32, starting transfers between devices, exchange(): part = keep + lax.ppermute(send, 'dp', pairs)  31.6 us
    ppermute x4, waiting for transfers between devices, dp_sum(): part = part + lax.ppermute(part, 'dp', [(i, i ^ step) for i in range(size)])  20.2 us
    ppermute x4, waiting for transfers between devices, tensor_sum(): return part + lax.ppermute(part, 'tensor', [(0, 1), (1, 0)])  16.7 us
    dot_general x16, matrix products, dp_share_open(): jnp.dot(half.reshape(-1, tokens), right, preferred_element_type=jnp.float32)  16.7 us
    ppermute x4, starting transfers between devices, tensor_sum(): return part + lax.ppermute(part, 'tensor', [(0, 1), (1, 0)])  7.85 us
    add x24, other arithmetic, exchange(): part = keep + lax.ppermute(send, 'dp', pairs)  5.38 us
  transfers between devices with their start and end apart: 40, of which 21 were waited for; matrix products, arithmetic and copies ran while one was open for 21% of the time, Pallas kernels for 0%

profile of v4, /device:TPU:0, one launch (start us, length us, event | category | flops | bytes accessed | tf_op | source)
XLA Modules:
  0.0 198.4 jit_solution(7380329724460938691)
XLA Ops:
  0.7 0.9 broadcast_compare_fusion
  1.6 1.4 fusion.2
  4.2 1.4 fusion.1
  7.5 3.0 %collective-permute-start = (f32[128,768]{1,0:T(8,128)S(1)}, f32[128,768]{1,0:T(8,128)}, u32[]{:S(2)}, u32[]{:S(2)}) collective-permute-start(f32[128,768]{1,0:T(8,128)S(1)} %fusion.100), channel_id=1, source_target_pairs={{0,1},{1,0},{2,3},{3,2},{4,5},{5,4},{6,7},{7,6},{8,9},{9,8},{10,11... | collective-permute-start | bytes 1179656 | tf_op jit(solution)/shard_map/ppermute | solution.py:31
  13.6 6.2 %collective-permute-done = f32[128,768]{1,0:T(8,128)} collective-permute-done((f32[128,768]{1,0:T(8,128)S(1)}, f32[128,768]{1,0:T(8,128)}, u32[]{:S(2)}, u32[]{:S(2)}) %collective-permute-start) | collective-permute-done | bytes 393248 | tf_op jit(solution)/shard_map/ppermute | solution.py:31
  19.7 1.3 fusion.99
  21.3 2.1 %fusion.7 = (bf16[128,1536]{1,0:T(8,128)(2,1)S(1)}, f32[128,1536]{1,0:T(8,128)S(1)}) fusion(f32[1536]{0:T(1024)S(1)} %copy-done.86, bf16[768,1536]{1,0:T(8,128)(2,1)S(1)} %copy-done, f32[128,768]{1,0:T(8,128)S(1)} %get-tuple-element.134, f32[768]{0:T(1024)S(1)} %copy-done.71, f32[768]{0:T(1024)S(1)} %copy-done.44, f32[128]{0:T(128)S(1)} %add_rsqrt_fusion.1, ...), kind=kOutput, calls=%fused_computation.30 | convolution fusion | flops 315457536 | bytes 3945472 | tf_op jit(solution)/shard_map/dot_general | solution.py:272
  24.3 1.8 collective-permute-start.1
  26.8 7.9 %collective-permute-done.1 = f32[128,768]{1,0:T(8,128)S(1)} collective-permute-done((f32[128,768]{1,0:T(8,128)S(1)}, f32[128,768]{1,0:T(8,128)S(1)}, u32[]{:S(2)}, u32[]{:S(2)}) %collective-permute-start.1) | collective-permute-done | bytes 393248 | tf_op jit(solution)/shard_map/ppermute | solution.py:31
  34.7 0.9 fusion.98
  36.6 1.5 convert_reduce_fusion.2
  38.1 1.3 convert_reduce_fusion
  39.4 1.6 fusion.102
  41.1 1.4 collective-permute-start.2
  42.5 1.1 copy.68
  43.7 2.5 %fusion.33 = f32[2,2,2,48,768]{4,3,2,1,0:T(8,128)} fusion(bf16[128,1536]{1,0:T(8,128)(2,1)} %copy-done.10, bf16[2,2,2,2,48,128]{5,4,3,2,1,0:T(8,128)(2,1)S(1)} %bitcast.257, s32[]{:T(128)S(6)} %select_n.140), kind=kOutput, calls=%fused_computation.122 | convolution fusion | flops 75497472 | bytes 1474564 | tf_op jit(solution)/shard_map/dot_general | solution.py:59
  46.1 1.3 fusion.32
  49.8 0.9 collective-permute-done.2
  50.8 2.6 %multiply_reduce_fusion = (f32[768]{0:T(1024)}, f32[128]{0:T(128)}, f32[128]{0:T(128)}, f32[768]{0:T(1024)}, f32[128,768]{1,0:T(8,128)}, /*index=5*/bf16[768,128]{0,1:T(8,128)(2,1)}) fusion(f32[128,768]{1,0:T(8,128)S(1)} %get-tuple-element.134, f32[128]{0:T(128)S(1)} %copy-done.68, f32[128]{0:T(128)S(1)} %copy-done.64, f32[768]{0:T(1024)S(1)} %copy-done.45, ...), kind=kLoop, calls=%fused_computation.60 | loop fusion | flops 1177856 | bytes 2173952 | tf_op jit(solution)/shard_map/reduce_sum | solution.py:126
  53.4 1.1 copy.67
  54.6 1.3 fusion.31
  56.0 1.3 fusion.30
  59.1 0.9 fusion.97
  60.0 2.6 %convolution_add_fusion.1 = f32[2,2,2,48,768]{4,3,2,1,0:T(8,128)} fusion(f32[2,2,2,48,768]{4,3,2,1,0:T(8,128)} %collective-permute-done.6, bf16[128,1536]{1,0:T(8,128)(2,1)S(1)} %copy-done.12, bf16[2,2,2,2,48,128]{5,4,3,2,1,0:T(8,128)(2,1)S(1)} %bitcast.259, s32[]{:T(128)S(6)} %select_n.139), kind=kOutput, calls=%fused_computation.3 | convolution fusion | flops 75792384 | bytes 2654212 | tf_op jit(solution)/shard_map/dot_general | solution.py:59
  62.6 2.7 %convolution_add_fusion.2 = f32[2,2,2,48,768]{4,3,2,1,0:T(8,128)} fusion(f32[2,2,2,48,768]{4,3,2,1,0:T(8,128)} %collective-permute-done.5, bf16[128,1536]{1,0:T(8,128)(2,1)S(1)} %copy-done.12, bf16[2,2,2,2,48,128]{5,4,3,2,1,0:T(8,128)(2,1)S(1)} %bitcast.260, s32[]{:T(128)S(6)} %select_n.139), kind=kOutput, calls=%fused_computation.4 | convolution fusion | flops 75792384 | bytes 2654212 | tf_op jit(solution)/shard_map/dot_general | solution.py:59
  65.3 1.4 convolution_add_fusion.3
  66.7 1.3 convolution_add_fusion.4
  68.9 1.6 multiply_reduce_fusion.2
  71.4 1.2 collective-permute-start.9
  73.4 1.5 collective-permute-start.8
  75.5 1.3 dynamic-slice_bitcast_fusion
  77.4 1.0 collective-permute-start.14
  79.0 8.8 %collective-permute-done.9 = f32[2,2,48,768]{3,2,1,0:T(8,128)} collective-permute-done((f32[2,2,48,768]{3,2,1,0:T(8,128)}, f32[2,2,48,768]{3,2,1,0:T(8,128)}, u32[]{:S(2)}, u32[]{:S(2)}) %collective-permute-start.9) | collective-permute-done | bytes 589856 | tf_op jit(solution)/shard_map/ppermute | solution.py:80
  87.9 1.1 bitcast_add_fusion.2
  90.0 1.1 bitcast_add_fusion.3
  91.1 0.9 collective-permute-start.36
  92.1 2.4 %collective-permute-start.38 = (f32[2,48,768]{2,1,0:T(8,128)S(1)}, f32[2,48,768]{2,1,0:T(8,128)S(1)}, u32[]{:S(2)}, u32[]{:S(2)}) collective-permute-start(f32[2,48,768]{2,1,0:T(8,128)S(1)} %dynamic-slice_bitcast_fusion.4), channel_id=1, source_target_pairs={{0,16},{2,18},{4,20},{6,22},{8,24},{10,26},{12,28},{14,30},{16,0},... | collective-permute-start | bytes 884744 | tf_op jit(solution)/shard_map/ppermute | solution.py:80
  96.4 10.3 %collective-permute-done.15 = f32[2,2,48,768]{3,2,1,0:T(8,128)S(1)} collective-permute-done((f32[2,2,48,768]{3,2,1,0:T(8,128)S(1)}, f32[2,2,48,768]{3,2,1,0:T(8,128)S(1)}, u32[]{:S(2)}, u32[]{:S(2)}) %collective-permute-start.15) | collective-permute-done | bytes 589856 | tf_op jit(solution)/shard_map/ppermute | solution.py:80
  108.7 3.5 %collective-permute-done.36 = f32[2,48,768]{2,1,0:T(8,128)S(1)} collective-permute-done((f32[2,48,768]{2,1,0:T(8,128)S(1)}, f32[2,48,768]{2,1,0:T(8,128)S(1)}, u32[]{:S(2)}, u32[]{:S(2)}) %collective-permute-start.36) | collective-permute-done | bytes 294944 | tf_op jit(solution)/shard_map/ppermute | solution.py:80
  112.2 1.1 collective-permute-start.29
  113.4 1.6 collective-permute-start.10
  115.0 5.4 %collective-permute-done.29 = f32[2,2,48,384]{3,2,1,0:T(8,128)S(1)} collective-permute-done((f32[2,2,48,384]{3,2,1,0:T(8,128)S(1)}, f32[2,2,48,384]{3,2,1,0:T(8,128)S(1)}, u32[]{:S(2)}, u32[]{:S(2)}) %collective-permute-start.29) | collective-permute-done | bytes 294944 | tf_op jit(solution)/shard_map/ppermute | solution.py:80
  120.4 1.3 collective-permute-start.37
  121.7 1.7 collective-permute-done.10
  123.4 1.2 collective-permute-start.30
  125.5 4.4 %collective-permute-done.30 = f32[2,48,384]{2,1,0:T(8,128)S(1)} collective-permute-done((f32[2,48,384]{2,1,0:T(8,128)S(1)}, f32[2,48,384]{2,1,0:T(8,128)S(1)}, u32[]{:S(2)}, u32[]{:S(2)}) %collective-permute-start.30) | collective-permute-done | bytes 147488 | tf_op jit(solution)/shard_map/ppermute | solution.py:80
  130.7 1.4 collective-permute-start.31
  132.0 3.0 %collective-permute-done.39 = f32[48,768]{1,0:T(8,128)S(1)} collective-permute-done((f32[48,768]{1,0:T(8,128)S(1)}, f32[48,768]{1,0:T(8,128)S(1)}, u32[]{:S(2)}, u32[]{:S(2)}) %collective-permute-start.39) | collective-permute-done | bytes 147488 | tf_op jit(solution)/shard_map/ppermute | solution.py:80
  135.8 1.0 collective-permute-done.31
  138.5 2.9 %collective-permute-start.34 = (f32[2,48,768]{2,1,0:T(8,128)S(1)}, f32[2,48,768]{2,1,0:T(8,128)S(1)}, u32[]{:S(2)}, u32[]{:S(2)}) collective-permute-start(f32[2,48,768]{2,1,0:T(8,128)S(1)} %dynamic-slice_bitcast_fusion.6), channel_id=1, source_target_pairs={{0,16},{2,18},{4,20},{6,22},{8,24},{10,26},{12,28},{14,30},{16,0},... | collective-permute-start | bytes 884744 | tf_op jit(solution)/shard_map/ppermute | solution.py:80
  141.4 1.1 collective-permute-start.26
  143.2 3.3 %collective-permute-done.26 = f32[9,1536]{1,0:T(8,128)S(1)} collective-permute-done((f32[9,1536]{1,0:T(8,128)S(1)}, f32[9,1536]{1,0:T(8,128)S(1)}, u32[]{:S(2)}, u32[]{:S(2)}) %collective-permute-start.26) | collective-permute-done | bytes 55328 | tf_op jit(solution)/shard_map/ppermute | solution.py:40
  146.7 1.9 collective-permute-start.19
  148.6 12.8 %collective-permute-done.27 = f32[9,1536]{1,0:T(8,128)S(1)} collective-permute-done((f32[9,1536]{1,0:T(8,128)S(1)}, f32[9,1536]{1,0:T(8,128)S(1)}, u32[]{:S(2)}, u32[]{:S(2)}) %collective-permute-start.27) | collective-permute-done | bytes 55328 | tf_op jit(solution)/shard_map/ppermute | solution.py:40
  161.4 2.1 %collective-permute-start.28 = (f32[9,1536]{1,0:T(8,128)S(1)}, f32[9,1536]{1,0:T(8,128)S(1)}, u32[]{:S(2)}, u32[]{:S(2)}) collective-permute-start(f32[9,1536]{1,0:T(8,128)S(1)} %add.405), channel_id=1, source_target_pairs={{0,16},{2,18},{4,20},{6,22},{8,24},{10,26},{12,28},{14,30},{16,0},... | collective-permute-start | bytes 165896 | tf_op jit(solution)/shard_map/ppermute | solution.py:40
  163.5 4.2 %collective-permute-done.28 = f32[9,1536]{1,0:T(8,128)S(1)} collective-permute-done((f32[9,1536]{1,0:T(8,128)S(1)}, f32[9,1536]{1,0:T(8,128)S(1)}, u32[]{:S(2)}, u32[]{:S(2)}) %collective-permute-start.28) | collective-permute-done | bytes 55328 | tf_op jit(solution)/shard_map/ppermute | solution.py:40
  167.7 3.0 %collective-permute-start.16 = (f32[2,2,48,384]{3,2,1,0:T(8,128)S(1)}, f32[2,2,48,384]{3,2,1,0:T(8,128)S(1)}, u32[]{:S(2)}, u32[]{:S(2)}) collective-permute-start(f32[2,2,48,384]{3,2,1,0:T(8,128)S(1)} %dynamic-slice_bitcast_fusion.11), channel_id=1, source_target_pairs={{0,4},{2,6},{4,0},{6,2},{8,12},{10,14},{12,8},{14,10},{16,20},{18,... | collective-permute-start | bytes 884744 | tf_op jit(solution)/shard_map/ppermute | solution.py:80
  173.6 2.4 %collective-permute-start.23 = (f32[2,48,384]{2,1,0:T(8,128)S(1)}, f32[2,48,384]{2,1,0:T(8,128)S(1)}, u32[]{:S(2)}, u32[]{:S(2)}) collective-permute-start(f32[2,48,384]{2,1,0:T(8,128)S(1)} %dynamic-slice_bitcast_fusion.17), channel_id=1, source_target_pairs={{0,16},{2,18},{4,20},{6,22},{8,24},{10,26},{12,28},{14,30},{16,0},... | collective-permute-start | bytes 442376 | tf_op jit(solution)/shard_map/ppermute | solution.py:80
  177.1 2.3 %collective-permute-start.17 = (f32[2,48,384]{2,1,0:T(8,128)S(1)}, f32[2,48,384]{2,1,0:T(8,128)S(1)}, u32[]{:S(2)}, u32[]{:S(2)}) collective-permute-start(f32[2,48,384]{2,1,0:T(8,128)S(1)} %dynamic-slice_bitcast_fusion.19), channel_id=1, source_target_pairs={{0,8},{2,10},{4,12},{6,14},{8,0},{10,2},{12,4},{14,6},{16,24},{18,... | collective-permute-start | bytes 442376 | tf_op jit(solution)/shard_map/ppermute | solution.py:80
  179.4 10.1 %collective-permute-done.23 = f32[2,48,384]{2,1,0:T(8,128)S(1)} collective-permute-done((f32[2,48,384]{2,1,0:T(8,128)S(1)}, f32[2,48,384]{2,1,0:T(8,128)S(1)}, u32[]{:S(2)}, u32[]{:S(2)}) %collective-permute-start.23) | collective-permute-done | bytes 147488 | tf_op jit(solution)/shard_map/ppermute | solution.py:80
  190.3 0.9 collective-permute-done.20
  191.2 1.1 collective-permute-start.21
  194.8 0.9 collective-permute-done.21
  196.3 1.5 collective-permute-done.18
  (327 shorter events, 35.3 us)
Async XLA Ops:
  0.7 20.6 %copy-start = (bf16[768,1536]{1,0:T(8,128)(2,1)S(1)}, bf16[768,1536]{1,0:T(8,128)(2,1)}, u32[]{:S(2)}) copy-start(bf16[768,1536]{1,0:T(8,128)(2,1)} %param.29) | copy-start | bytes 7077892
  7.5 12.3 %collective-permute-start = (f32[128,768]{1,0:T(8,128)S(1)}, f32[128,768]{1,0:T(8,128)}, u32[]{:S(2)}, u32[]{:S(2)}) collective-permute-start(f32[128,768]{1,0:T(8,128)S(1)} %fusion.100), channel_id=1, source_target_pairs={{0,1},{1,0},{2,3},{3,2},{4,5},{5,4},{6,7},{7,6},{8,9},{9,8},{10,11... | collective-permute-start | bytes 1179656 | tf_op jit(solution)/shard_map/ppermute | solution.py:31
  21.0 13.7 %copy-start.63 = (f32[128]{0:T(128)}, f32[128]{0:T(128)S(1)}, u32[]{:S(2)}) copy-start(f32[128]{0:T(128)S(1)} %broadcast_multiply_fusion.5) | copy-start | bytes 1540
  21.3 13.4 %copy-start.67 = (f32[128]{0:T(128)}, f32[128]{0:T(128)S(1)}, u32[]{:S(2)}) copy-start(f32[128]{0:T(128)S(1)} %add_rsqrt_fusion.1) | copy-start | bytes 1540
  23.4 11.3 %copy-start.70 = (f32[768]{0:T(1024)S(1)}, f32[768]{0:T(1024)}, u32[]{:S(2)}) copy-start(f32[768]{0:T(1024)} %param.32) | copy-start | bytes 9220
  24.3 11.5 %copy-start.39 = (bf16[128,768]{1,0:T(8,128)(2,1)S(1)}, bf16[128,768]{1,0:T(8,128)(2,1)}, u32[]{:S(2)}) copy-start(bf16[128,768]{1,0:T(8,128)(2,1)} %param.35) | copy-start | bytes 589828
  24.3 11.5 %copy-start.54 = (f32[768]{0:T(1024)S(1)}, f32[768]{0:T(1024)}, u32[]{:S(2)}) copy-start(f32[768]{0:T(1024)} %param.33) | copy-start | bytes 9220
  24.3 10.4 %collective-permute-start.1 = (f32[128,768]{1,0:T(8,128)S(1)}, f32[128,768]{1,0:T(8,128)S(1)}, u32[]{:S(2)}, u32[]{:S(2)}) collective-permute-start(f32[128,768]{1,0:T(8,128)S(1)} %fusion.101), channel_id=1, source_target_pairs={{0,1},{1,0},{2,3},{3,2},{4,5},{5,4},{6,7},{7,6},{8,9},{9,8},{10,11... | collective-permute-start | bytes 1179656 | tf_op jit(solution)/shard_map/ppermute | solution.py:31
  41.1 9.7 %collective-permute-start.2 = (f32[128,768]{1,0:T(8,128)}, f32[128,768]{1,0:T(8,128)}, u32[]{:S(2)}, u32[]{:S(2)}) collective-permute-start(f32[128,768]{1,0:T(8,128)} %fusion.102), channel_id=1, source_target_pairs={{0,1},{1,0},{2,3},{3,2},{4,5},{5,4},{6,7},{7,6},{8,9},{9,8},{10,11... | collective-permute-start | bytes 1179656 | tf_op jit(solution)/shard_map/ppermute | solution.py:31
  46.1 13.8 %collective-permute-start.6 = (f32[2,2,2,48,768]{4,3,2,1,0:T(8,128)}, f32[2,2,2,48,768]{4,3,2,1,0:T(8,128)}, u32[]{:S(2)}, u32[]{:S(2)}) collective-permute-start(f32[2,2,2,48,768]{4,3,2,1,0:T(8,128)} %fusion.33), channel_id=1, source_target_pairs={{0,2},{2,0},{4,6},{6,4},{8,10},{10,8},{12,14},{14,12},{16,18},{18,... | collective-permute-start | bytes 3538952 | tf_op jit(solution)/shard_map/ppermute | solution.py:80
  47.5 15.1 %collective-permute-start.5 = (f32[2,2,2,48,768]{4,3,2,1,0:T(8,128)}, f32[2,2,2,48,768]{4,3,2,1,0:T(8,128)}, u32[]{:S(2)}, u32[]{:S(2)}) collective-permute-start(f32[2,2,2,48,768]{4,3,2,1,0:T(8,128)} %fusion.32), channel_id=1, source_target_pairs={{0,2},{2,0},{4,6},{6,4},{8,10},{10,8},{12,14},{14,12},{16,18},{18,... | collective-permute-start | bytes 3538952 | tf_op jit(solution)/shard_map/ppermute | solution.py:80
  55.9 9.4 %collective-permute-start.4 = (f32[2,2,2,48,768]{4,3,2,1,0:T(8,128)S(1)}, f32[2,2,2,48,768]{4,3,2,1,0:T(8,128)S(1)}, u32[]{:S(2)}, u32[]{:S(2)}) collective-permute-start(f32[2,2,2,48,768]{4,3,2,1,0:T(8,128)S(1)} %fusion.31), channel_id=1, source_target_pairs={{0,2},{2,0},{4,6},{6,4},{8,10},{10,8},{12,14},{14,12},{16,18},{18,... | collective-permute-start | bytes 3538952 | tf_op jit(solution)/shard_map/ppermute | solution.py:80
  57.3 9.4 %collective-permute-start.3 = (f32[2,2,2,48,768]{4,3,2,1,0:T(8,128)S(1)}, f32[2,2,2,48,768]{4,3,2,1,0:T(8,128)S(1)}, u32[]{:S(2)}, u32[]{:S(2)}) collective-permute-start(f32[2,2,2,48,768]{4,3,2,1,0:T(8,128)S(1)} %fusion.30), channel_id=1, source_target_pairs={{0,2},{2,0},{4,6},{6,4},{8,10},{10,8},{12,14},{14,12},{16,18},{18,... | collective-permute-start | bytes 3538952 | tf_op jit(solution)/shard_map/ppermute | solution.py:80
  71.4 16.5 %collective-permute-start.9 = (f32[2,2,48,768]{3,2,1,0:T(8,128)}, f32[2,2,48,768]{3,2,1,0:T(8,128)}, u32[]{:S(2)}, u32[]{:S(2)}) collective-permute-start(f32[2,2,48,768]{3,2,1,0:T(8,128)} %dynamic-slice_bitcast_fusion.2), channel_id=1, source_target_pairs={{0,8},{2,10},{4,12},{6,14},{8,0},{10,2},{12,4},{14,6},{16,24},{18,... | collective-permute-start | bytes 1769480 | tf_op jit(solution)/shard_map/ppermute | solution.py:80
  73.4 16.5 %collective-permute-start.8 = (f32[2,2,48,768]{3,2,1,0:T(8,128)}, f32[2,2,48,768]{3,2,1,0:T(8,128)}, u32[]{:S(2)}, u32[]{:S(2)}) collective-permute-start(f32[2,2,48,768]{3,2,1,0:T(8,128)} %dynamic-slice_bitcast_fusion.3), channel_id=1, source_target_pairs={{0,4},{2,6},{4,0},{6,2},{8,12},{10,14},{12,8},{14,10},{16,20},{18,... | collective-permute-start | bytes 1769480 | tf_op jit(solution)/shard_map/ppermute | solution.py:80
  75.4 13.6 %collective-permute-start.7 = (f32[2,2,2,48,384]{4,3,2,1,0:T(8,128)S(1)}, f32[2,2,2,48,384]{4,3,2,1,0:T(8,128)S(1)}, u32[]{:S(2)}, u32[]{:S(2)}) collective-permute-start(f32[2,2,2,48,384]{4,3,2,1,0:T(8,128)S(1)} %fusion.49), channel_id=1, source_target_pairs={{0,2},{2,0},{4,6},{6,4},{8,10},{10,8},{12,14},{14,12},{16,18},{18,... | collective-permute-start | bytes 1769480 | tf_op jit(solution)/shard_map/ppermute | solution.py:80
  76.8 30.0 %collective-permute-start.15 = (f32[2,2,48,768]{3,2,1,0:T(8,128)S(1)}, f32[2,2,48,768]{3,2,1,0:T(8,128)S(1)}, u32[]{:S(2)}, u32[]{:S(2)}) collective-permute-start(f32[2,2,48,768]{3,2,1,0:T(8,128)S(1)} %dynamic-slice_bitcast_fusion), channel_id=1, source_target_pairs={{0,8},{2,10},{4,12},{6,14},{8,0},{10,2},{12,4},{14,6},{16,24},{18,... | collective-permute-start | bytes 1769480 | tf_op jit(solution)/shard_map/ppermute | solution.py:80
  77.4 30.0 %collective-permute-start.14 = (f32[2,2,48,768]{3,2,1,0:T(8,128)S(1)}, f32[2,2,48,768]{3,2,1,0:T(8,128)S(1)}, u32[]{:S(2)}, u32[]{:S(2)}) collective-permute-start(f32[2,2,48,768]{3,2,1,0:T(8,128)S(1)} %dynamic-slice_bitcast_fusion.1), channel_id=1, source_target_pairs={{0,4},{2,6},{4,0},{6,2},{8,12},{10,14},{12,8},{14,10},{16,20},{18,... | collective-permute-start | bytes 1769480 | tf_op jit(solution)/shard_map/ppermute | solution.py:80
  79.0 10.9 %copy-start.5 = (f32[2,2,2,48,768]{4,3,2,1,0:T(8,128)S(1)}, f32[2,2,2,48,768]{4,3,2,1,0:T(8,128)}, u32[]{:S(2)}) copy-start(f32[2,2,2,48,768]{4,3,2,1,0:T(8,128)} %convolution_add_fusion.4) | copy-start | bytes 3538948
  91.1 21.1 %collective-permute-start.36 = (f32[2,48,768]{2,1,0:T(8,128)S(1)}, f32[2,48,768]{2,1,0:T(8,128)S(1)}, u32[]{:S(2)}, u32[]{:S(2)}) collective-permute-start(f32[2,48,768]{2,1,0:T(8,128)S(1)} %dynamic-slice_bitcast_fusion.5), channel_id=1, source_target_pairs={{0,8},{2,10},{4,12},{6,14},{8,0},{10,2},{12,4},{14,6},{16,24},{18,... | collective-permute-start | bytes 884744 | tf_op jit(solution)/shard_map/ppermute | solution.py:80
  92.1 21.3 %collective-permute-start.38 = (f32[2,48,768]{2,1,0:T(8,128)S(1)}, f32[2,48,768]{2,1,0:T(8,128)S(1)}, u32[]{:S(2)}, u32[]{:S(2)}) collective-permute-start(f32[2,48,768]{2,1,0:T(8,128)S(1)} %dynamic-slice_bitcast_fusion.4), channel_id=1, source_target_pairs={{0,16},{2,18},{4,20},{6,22},{8,24},{10,26},{12,28},{14,30},{16,0},... | collective-permute-start | bytes 884744 | tf_op jit(solution)/shard_map/ppermute | solution.py:80
  94.8 42.6 %collective-permute-start.13 = (f32[2,2,2,48,384]{4,3,2,1,0:T(8,128)S(1)}, f32[2,2,2,48,384]{4,3,2,1,0:T(8,128)S(1)}, u32[]{:S(2)}, u32[]{:S(2)}) collective-permute-start(f32[2,2,2,48,384]{4,3,2,1,0:T(8,128)S(1)} %fusion.34), channel_id=1, source_target_pairs={{0,2},{2,0},{4,6},{6,4},{8,10},{10,8},{12,14},{14,12},{16,18},{18,... | collective-permute-start | bytes 1769480 | tf_op jit(solution)/shard_map/ppermute | solution.py:80
  95.5 11.3 %copy-start.3 = (f32[2,2,2,48,768]{4,3,2,1,0:T(8,128)S(1)}, f32[2,2,2,48,768]{4,3,2,1,0:T(8,128)}, u32[]{:S(2)}) copy-start(f32[2,2,2,48,768]{4,3,2,1,0:T(8,128)} %convolution_add_fusion.1) | copy-start | bytes 3538948
  96.2 10.9 %copy-start.49 = (f32[1536]{0:T(1024)S(1)}, f32[1536]{0:T(1024)}, u32[]{:S(2)}) copy-start(f32[1536]{0:T(1024)} %pad.28) | copy-start | bytes 18436
  96.2 10.9 %copy-start.50 = (f32[1536]{0:T(1024)S(1)}, f32[1536]{0:T(1024)}, u32[]{:S(2)}) copy-start(f32[1536]{0:T(1024)} %pad.26) | copy-start | bytes 18436
  96.2 10.9 %copy-start.51 = (f32[1536]{0:T(1024)S(1)}, f32[1536]{0:T(1024)}, u32[]{:S(2)}) copy-start(f32[1536]{0:T(1024)} %pad.27) | copy-start | bytes 18436
  96.3 10.8 %copy-start.52 = (f32[1536]{0:T(1024)S(1)}, f32[1536]{0:T(1024)}, u32[]{:S(2)}) copy-start(f32[1536]{0:T(1024)} %pad.29) | copy-start | bytes 18436
  96.3 10.8 %copy-start.53 = (f32[1536]{0:T(1024)S(1)}, f32[1536]{0:T(1024)}, u32[]{:S(2)}) copy-start(f32[1536]{0:T(1024)} %pad.30) | copy-start | bytes 18436
  96.3 10.8 %copy-start.66 = (f32[1536]{0:T(1024)S(1)}, f32[1536]{0:T(1024)}, u32[]{:S(2)}) copy-start(f32[1536]{0:T(1024)} %get-tuple-element.144) | copy-start | bytes 18436
  96.3 10.8 %copy-start.75 = (pred[9]{0:T(512)(128)(4,1)S(1)}, pred[9]{0:T(512)(128)(4,1)}, u32[]{:S(2)}) copy-start(pred[9]{0:T(512)(128)(4,1)} %get-tuple-element.148) | copy-start | bytes 31
  96.3 10.8 %copy-start.76 = (pred[9]{0:T(512)(128)(4,1)S(1)}, pred[9]{0:T(512)(128)(4,1)}, u32[]{:S(2)}) copy-start(pred[9]{0:T(512)(128)(4,1)} %get-tuple-element.149) | copy-start | bytes 31
  96.3 10.8 %copy-start.77 = (pred[9]{0:T(512)(128)(4,1)S(1)}, pred[9]{0:T(512)(128)(4,1)}, u32[]{:S(2)}) copy-start(pred[9]{0:T(512)(128)(4,1)} %iota_compare_fusion.8) | copy-start | bytes 31
  96.3 10.8 %copy-start.78 = (pred[9]{0:T(512)(128)(4,1)S(1)}, pred[9]{0:T(512)(128)(4,1)}, u32[]{:S(2)}) copy-start(pred[9]{0:T(512)(128)(4,1)} %get-tuple-element.150) | copy-start | bytes 31
  96.3 10.8 %copy-start.79 = (pred[9]{0:T(512)(128)(4,1)S(1)}, pred[9]{0:T(512)(128)(4,1)}, u32[]{:S(2)}) copy-start(pred[9]{0:T(512)(128)(4,1)} %get-tuple-element.151) | copy-start | bytes 31
  96.3 10.8 %copy-start.80 = (pred[9]{0:T(512)(128)(4,1)S(1)}, pred[9]{0:T(512)(128)(4,1)}, u32[]{:S(2)}) copy-start(pred[9]{0:T(512)(128)(4,1)} %get-tuple-element.152) | copy-start | bytes 31
  96.4 10.8 %copy-start.81 = (pred[9]{0:T(512)(128)(4,1)S(1)}, pred[9]{0:T(512)(128)(4,1)}, u32[]{:S(2)}) copy-start(pred[9]{0:T(512)(128)(4,1)} %get-tuple-element.153) | copy-start | bytes 31
  96.4 10.8 %copy-start.82 = (pred[9]{0:T(512)(128)(4,1)S(1)}, pred[9]{0:T(512)(128)(4,1)}, u32[]{:S(2)}) copy-start(pred[9]{0:T(512)(128)(4,1)} %get-tuple-element.154) | copy-start | bytes 31
  96.4 10.8 %copy-start.83 = (pred[9]{0:T(512)(128)(4,1)S(1)}, pred[9]{0:T(512)(128)(4,1)}, u32[]{:S(2)}) copy-start(pred[9]{0:T(512)(128)(4,1)} %get-tuple-element.155) | copy-start | bytes 31
  106.7 31.0 %collective-permute-start.12 = (f32[2,2,2,48,384]{4,3,2,1,0:T(8,128)S(1)}, f32[2,2,2,48,384]{4,3,2,1,0:T(8,128)S(1)}, u32[]{:S(2)}, u32[]{:S(2)}) collective-permute-start(f32[2,2,2,48,384]{4,3,2,1,0:T(8,128)S(1)} %fusion.37), channel_id=1, source_target_pairs={{0,2},{2,0},{4,6},{6,4},{8,10},{10,8},{12,14},{14,12},{16,18},{18,... | collective-permute-start | bytes 1769480 | tf_op jit(solution)/shard_map/ppermute | solution.py:80
  107.4 30.6 %collective-permute-start.11 = (f32[2,2,2,48,384]{4,3,2,1,0:T(8,128)S(1)}, f32[2,2,2,48,384]{4,3,2,1,0:T(8,128)S(1)}, u32[]{:S(2)}, u32[]{:S(2)}) collective-permute-start(f32[2,2,2,48,384]{4,3,2,1,0:T(8,128)S(1)} %fusion.42), channel_id=1, source_target_pairs={{0,2},{2,0},{4,6},{6,4},{8,10},{10,8},{12,14},{14,12},{16,18},{18,... | collective-permute-start | bytes 1769480 | tf_op jit(solution)/shard_map/ppermute | solution.py:80
  112.2 8.2 %collective-permute-start.29 = (f32[2,2,48,384]{3,2,1,0:T(8,128)S(1)}, f32[2,2,48,384]{3,2,1,0:T(8,128)S(1)}, u32[]{:S(2)}, u32[]{:S(2)}) collective-permute-start(f32[2,2,48,384]{3,2,1,0:T(8,128)S(1)} %dynamic-slice_bitcast_fusion.8), channel_id=1, source_target_pairs={{0,4},{2,6},{4,0},{6,2},{8,12},{10,14},{12,8},{14,10},{16,20},{18,... | collective-permute-start | bytes 884744 | tf_op jit(solution)/shard_map/ppermute | solution.py:80
  113.3 11.3 %copy-start.28 = (f32[128,768]{1,0:T(8,128)S(1)}, f32[128,768]{1,0:T(8,128)}, u32[]{:S(2)}) copy-start(f32[128,768]{1,0:T(8,128)} %get-tuple-element.129) | copy-start | bytes 1179652
  113.4 10.1 %collective-permute-start.10 = (f32[128,768]{1,0:T(8,128)S(1)}, f32[128,768]{1,0:T(8,128)S(1)}, u32[]{:S(2)}, u32[]{:S(2)}) collective-permute-start(f32[128,768]{1,0:T(8,128)S(1)} %convolution_add_fusion.9), channel_id=1, source_target_pairs={{0,1},{1,0},{2,3},{3,2},{4,5},{5,4},{6,7},{7,6},{8,9},{9,8},{10,11... | collective-permute-start | bytes 1179656 | tf_op jit(solution)/shard_map/ppermute | solution.py:31
  120.4 10.3 %collective-permute-start.37 = (f32[48,768]{1,0:T(8,128)S(1)}, f32[48,768]{1,0:T(8,128)S(1)}, u32[]{:S(2)}, u32[]{:S(2)}) collective-permute-start(f32[48,768]{1,0:T(8,128)S(1)} %dynamic-slice_bitcast_fusion.13), channel_id=1, source_target_pairs={{0,16},{2,18},{4,20},{6,22},{8,24},{10,26},{12,28},{14,30},{16,0},... | collective-permute-start | bytes 442376 | tf_op jit(solution)/shard_map/ppermute | solution.py:80
  123.4 6.5 %collective-permute-start.30 = (f32[2,48,384]{2,1,0:T(8,128)S(1)}, f32[2,48,384]{2,1,0:T(8,128)S(1)}, u32[]{:S(2)}, u32[]{:S(2)}) collective-permute-start(f32[2,48,384]{2,1,0:T(8,128)S(1)} %dynamic-slice_bitcast_fusion.16), channel_id=1, source_target_pairs={{0,8},{2,10},{4,12},{6,14},{8,0},{10,2},{12,4},{14,6},{16,24},{18,... | collective-permute-start | bytes 442376 | tf_op jit(solution)/shard_map/ppermute | solution.py:80
  129.9 5.1 %collective-permute-start.39 = (f32[48,768]{1,0:T(8,128)S(1)}, f32[48,768]{1,0:T(8,128)S(1)}, u32[]{:S(2)}, u32[]{:S(2)}) collective-permute-start(f32[48,768]{1,0:T(8,128)S(1)} %dynamic-slice_bitcast_fusion.12), channel_id=1, source_target_pairs={{0,4},{2,6},{4,0},{6,2},{8,12},{10,14},{12,8},{14,10},{16,20},{18,... | collective-permute-start | bytes 442376 | tf_op jit(solution)/shard_map/ppermute | solution.py:80
  130.7 6.1 %collective-permute-start.31 = (f32[48,384]{1,0:T(8,128)S(1)}, f32[48,384]{1,0:T(8,128)S(1)}, u32[]{:S(2)}, u32[]{:S(2)}) collective-permute-start(f32[48,384]{1,0:T(8,128)S(1)} %dynamic-slice_bitcast_fusion.20), channel_id=1, source_target_pairs={{0,16},{2,18},{4,20},{6,22},{8,24},{10,26},{12,28},{14,30},{16,0},... | collective-permute-start | bytes 221192 | tf_op jit(solution)/shard_map/ppermute | solution.py:80
  138.3 34.4 %collective-permute-start.32 = (f32[2,48,768]{2,1,0:T(8,128)S(1)}, f32[2,48,768]{2,1,0:T(8,128)S(1)}, u32[]{:S(2)}, u32[]{:S(2)}) collective-permute-start(f32[2,48,768]{2,1,0:T(8,128)S(1)} %dynamic-slice_bitcast_fusion.7), channel_id=1, source_target_pairs={{0,8},{2,10},{4,12},{6,14},{8,0},{10,2},{12,4},{14,6},{16,24},{18,... | collective-permute-start | bytes 884744 | tf_op jit(solution)/shard_map/ppermute | solution.py:80
  138.5 2.9 %collective-permute-start.25 = (f32[9,1536]{1,0:T(8,128)S(1)}, f32[9,1536]{1,0:T(8,128)S(1)}, u32[]{:S(2)}, u32[]{:S(2)}) collective-permute-start(f32[9,1536]{1,0:T(8,128)S(1)} %select_select_fusion), channel_id=1, source_target_pairs={{0,2},{2,0},{4,6},{6,4},{8,10},{10,8},{12,14},{14,12},{16,18},{18,... | collective-permute-start | bytes 165896 | tf_op jit(solution)/shard_map/ppermute | solution.py:40
  138.5 34.2 %collective-permute-start.34 = (f32[2,48,768]{2,1,0:T(8,128)S(1)}, f32[2,48,768]{2,1,0:T(8,128)S(1)}, u32[]{:S(2)}, u32[]{:S(2)}) collective-permute-start(f32[2,48,768]{2,1,0:T(8,128)S(1)} %dynamic-slice_bitcast_fusion.6), channel_id=1, source_target_pairs={{0,16},{2,18},{4,20},{6,22},{8,24},{10,26},{12,28},{14,30},{16,0},... | collective-permute-start | bytes 884744 | tf_op jit(solution)/shard_map/ppermute | solution.py:80
  141.4 5.0 %collective-permute-start.26 = (f32[9,1536]{1,0:T(8,128)S(1)}, f32[9,1536]{1,0:T(8,128)S(1)}, u32[]{:S(2)}, u32[]{:S(2)}) collective-permute-start(f32[9,1536]{1,0:T(8,128)S(1)} %add.403), channel_id=1, source_target_pairs={{0,4},{2,6},{4,0},{6,2},{8,12},{10,14},{12,8},{14,10},{16,20},{18,... | collective-permute-start | bytes 165896 | tf_op jit(solution)/shard_map/ppermute | solution.py:40
  142.5 31.0 %collective-permute-start.22 = (f32[2,2,48,384]{3,2,1,0:T(8,128)S(1)}, f32[2,2,48,384]{3,2,1,0:T(8,128)S(1)}, u32[]{:S(2)}, u32[]{:S(2)}) collective-permute-start(f32[2,2,48,384]{3,2,1,0:T(8,128)S(1)} %dynamic-slice_bitcast_fusion.9), channel_id=1, source_target_pairs={{0,8},{2,10},{4,12},{6,14},{8,0},{10,2},{12,4},{14,6},{16,24},{18,... | collective-permute-start | bytes 884744 | tf_op jit(solution)/shard_map/ppermute | solution.py:80
  146.4 14.9 %collective-permute-start.27 = (f32[9,1536]{1,0:T(8,128)S(1)}, f32[9,1536]{1,0:T(8,128)S(1)}, u32[]{:S(2)}, u32[]{:S(2)}) collective-permute-start(f32[9,1536]{1,0:T(8,128)S(1)} %add.404), channel_id=1, source_target_pairs={{0,8},{2,10},{4,12},{6,14},{8,0},{10,2},{12,4},{14,6},{16,24},{18,... | collective-permute-start | bytes 165896 | tf_op jit(solution)/shard_map/ppermute | solution.py:40
  146.7 29.3 %collective-permute-start.19 = (f32[2,2,48,384]{3,2,1,0:T(8,128)S(1)}, f32[2,2,48,384]{3,2,1,0:T(8,128)S(1)}, u32[]{:S(2)}, u32[]{:S(2)}) collective-permute-start(f32[2,2,48,384]{3,2,1,0:T(8,128)S(1)} %dynamic-slice_bitcast_fusion.10), channel_id=1, source_target_pairs={{0,8},{2,10},{4,12},{6,14},{8,0},{10,2},{12,4},{14,6},{16,24},{18,... | collective-permute-start | bytes 884744 | tf_op jit(solution)/shard_map/ppermute | solution.py:80
  161.4 6.3 %collective-permute-start.28 = (f32[9,1536]{1,0:T(8,128)S(1)}, f32[9,1536]{1,0:T(8,128)S(1)}, u32[]{:S(2)}, u32[]{:S(2)}) collective-permute-start(f32[9,1536]{1,0:T(8,128)S(1)} %add.405), channel_id=1, source_target_pairs={{0,16},{2,18},{4,20},{6,22},{8,24},{10,26},{12,28},{14,30},{16,0},... | collective-permute-start | bytes 165896 | tf_op jit(solution)/shard_map/ppermute | solution.py:40
  167.7 9.3 %collective-permute-start.16 = (f32[2,2,48,384]{3,2,1,0:T(8,128)S(1)}, f32[2,2,48,384]{3,2,1,0:T(8,128)S(1)}, u32[]{:S(2)}, u32[]{:S(2)}) collective-permute-start(f32[2,2,48,384]{3,2,1,0:T(8,128)S(1)} %dynamic-slice_bitcast_fusion.11), channel_id=1, source_target_pairs={{0,4},{2,6},{4,0},{6,2},{8,12},{10,14},{12,8},{14,10},{16,20},{18,... | collective-permute-start | bytes 884744 | tf_op jit(solution)/shard_map/ppermute | solution.py:80
  172.7 19.8 %collective-permute-start.33 = (f32[48,768]{1,0:T(8,128)S(1)}, f32[48,768]{1,0:T(8,128)S(1)}, u32[]{:S(2)}, u32[]{:S(2)}) collective-permute-start(f32[48,768]{1,0:T(8,128)S(1)} %dynamic-slice_bitcast_fusion.15), channel_id=1, source_target_pairs={{0,16},{2,18},{4,20},{6,22},{8,24},{10,26},{12,28},{14,30},{16,0},... | collective-permute-start | bytes 442376 | tf_op jit(solution)/shard_map/ppermute | solution.py:80
  172.9 19.7 %collective-permute-start.35 = (f32[48,768]{1,0:T(8,128)S(1)}, f32[48,768]{1,0:T(8,128)S(1)}, u32[]{:S(2)}, u32[]{:S(2)}) collective-permute-start(f32[48,768]{1,0:T(8,128)S(1)} %dynamic-slice_bitcast_fusion.14), channel_id=1, source_target_pairs={{0,4},{2,6},{4,0},{6,2},{8,12},{10,14},{12,8},{14,10},{16,20},{18,... | collective-permute-start | bytes 442376 | tf_op jit(solution)/shard_map/ppermute | solution.py:80
  173.6 15.9 %collective-permute-start.23 = (f32[2,48,384]{2,1,0:T(8,128)S(1)}, f32[2,48,384]{2,1,0:T(8,128)S(1)}, u32[]{:S(2)}, u32[]{:S(2)}) collective-permute-start(f32[2,48,384]{2,1,0:T(8,128)S(1)} %dynamic-slice_bitcast_fusion.17), channel_id=1, source_target_pairs={{0,16},{2,18},{4,20},{6,22},{8,24},{10,26},{12,28},{14,30},{16,0},... | collective-permute-start | bytes 442376 | tf_op jit(solution)/shard_map/ppermute | solution.py:80
  176.1 15.1 %collective-permute-start.20 = (f32[2,48,384]{2,1,0:T(8,128)S(1)}, f32[2,48,384]{2,1,0:T(8,128)S(1)}, u32[]{:S(2)}, u32[]{:S(2)}) collective-permute-start(f32[2,48,384]{2,1,0:T(8,128)S(1)} %dynamic-slice_bitcast_fusion.18), channel_id=1, source_target_pairs={{0,16},{2,18},{4,20},{6,22},{8,24},{10,26},{12,28},{14,30},{16,0},... | collective-permute-start | bytes 442376 | tf_op jit(solution)/shard_map/ppermute | solution.py:80
  177.1 15.3 %collective-permute-start.17 = (f32[2,48,384]{2,1,0:T(8,128)S(1)}, f32[2,48,384]{2,1,0:T(8,128)S(1)}, u32[]{:S(2)}, u32[]{:S(2)}) collective-permute-start(f32[2,48,384]{2,1,0:T(8,128)S(1)} %dynamic-slice_bitcast_fusion.19), channel_id=1, source_target_pairs={{0,8},{2,10},{4,12},{6,14},{8,0},{10,2},{12,4},{14,6},{16,24},{18,... | collective-permute-start | bytes 442376 | tf_op jit(solution)/shard_map/ppermute | solution.py:80
  189.5 4.6 %collective-permute-start.24 = (f32[48,384]{1,0:T(8,128)S(1)}, f32[48,384]{1,0:T(8,128)S(1)}, u32[]{:S(2)}, u32[]{:S(2)}) collective-permute-start(f32[48,384]{1,0:T(8,128)S(1)} %dynamic-slice_bitcast_fusion.21), channel_id=1, source_target_pairs={{0,4},{2,6},{4,0},{6,2},{8,12},{10,14},{12,8},{14,10},{16,20},{18,... | collective-permute-start | bytes 221192 | tf_op jit(solution)/shard_map/ppermute | solution.py:80
  191.2 4.4 %collective-permute-start.21 = (f32[48,384]{1,0:T(8,128)S(1)}, f32[48,384]{1,0:T(8,128)S(1)}, u32[]{:S(2)}, u32[]{:S(2)}) collective-permute-start(f32[48,384]{1,0:T(8,128)S(1)} %dynamic-slice_bitcast_fusion.22), channel_id=1, source_target_pairs={{0,4},{2,6},{4,0},{6,2},{8,12},{10,14},{12,8},{14,10},{16,20},{18,... | collective-permute-start | bytes 221192 | tf_op jit(solution)/shard_map/ppermute | solution.py:80
  192.4 5.3 %collective-permute-start.18 = (f32[48,384]{1,0:T(8,128)S(1)}, f32[48,384]{1,0:T(8,128)S(1)}, u32[]{:S(2)}, u32[]{:S(2)}) collective-permute-start(f32[48,384]{1,0:T(8,128)S(1)} %dynamic-slice_bitcast_fusion.23), channel_id=1, source_target_pairs={{0,16},{2,18},{4,20},{6,22},{8,24},{10,26},{12,28},{14,30},{16,0},... | collective-permute-start | bytes 221192 | tf_op jit(solution)/shard_map/ppermute | solution.py:80
  (63 other events, 244.8 us)
